TPU v7x, 128 devices: a whole 4x4x4 slice. The times are simulated.
128 devices in a mesh: seg: 64 (over x, y, z), sub: 2 (over core).
Axes of the slice: x: 4, y: 4, z: 4, core: 2. Of those that a mesh axis runs over, the one named last changes fastest.
Arguments:
- start_field: float32 [3, 884736], P(None, ('seg', 'sub')), may hold values from -6 to 6
- element_loads: float32 [192, 32768], P(None, ('seg', 'sub')), may hold values from -6 to 6
- element_coefs: float32 [2, 32768], P(None, ('seg', 'sub')), may hold values from 0.2 to 5
- element_nodes: int32 [64, 32768], P(None, ('seg', 'sub')), may hold values from 0 to 7295, as said below
- move_list: int32 [3, 32768], P(None, ('seg', 'sub')), may hold values from 0 to 255, as said below
- face_nodes: int32 [2, 24576], P(None, ('seg', 'sub')), may hold values from 0 to 6911, as said below
- stiffness: float32 [2, 192, 192], replicated, as said below
Outputs:
- smoothed: float32 [3, 884736], P(None, ('seg', 'sub'))
- moved_loads: float32 [192, 32768], P(None, ('seg', 'sub'))
- moved_coefs: float32 [2, 32768], P(None, ('seg', 'sub'))
Inputs may be any that keep to these rules, and one draw needn't show every extreme that they name: `move_list`: column e describes the record in slot e of its device before migration: row 0 its destination device p, row 1 its slot there, row 2 its place in the list that its device sends to p. A record that stays keeps its slot and has place 0. Every slot after migration receives exactly one record. A record leaves only for the device just before or after its own, with at most 16 records from one device to each and places below 16, or for a device two or more positions away, with at most 1 records from one device to one such device and places below 1; places are distinct for one source and destination. Both bounds are reached. `element_nodes`: column e lists the nodes of the element in slot e after migration in its device's numbering: values below 6912 are the device's own nodes, 6912 + s is entry s of face_nodes row 1 of the device before, 7104 + s entry s of face_nodes row 0 of the device after. The nodes of one element are distinct, every own node belongs to some element, the first device refers to no device before it and the last to none after it. `face_nodes`: for each device, row 0 lists own nodes that the device before refers to and row 1 those that the device after refers to; the 384 entries of one device are distinct. `stiffness`: both blocks are symmetric with positive diagonals and strictly diagonally dominant rows.
All inputs are finite; a program needn't handle non-finite values.
Results may differ from a plain program's by a relative error of at most 0.0001.
Values sent between devices are 32-bit elements; how exact they have to be, the bound alone decides.
No kernel may reach another device: no remote copies, remote signals or barrier semaphores. Data moves between devices by JAX's collectives and lax.ppermute only.
A program may use at most 128 MiB of HBM per device.

v0:
```python
import jax
import jax.numpy as jnp
from jax import lax
from jax.sharding import PartitionSpec as P

NEAR_CAP = 16
DEGREE = 4
SWEEPS = 2


center = 1.125
half_width = 0.875


def shifted(x, axis, by):
    length = lax.axis_size(axis)
    pairs = [(i, i + by) for i in range(length) if 0 <= i + by < length]
    return lax.ppermute(x, axis, pairs)


def local(
    start_field, element_loads, element_coefs, element_nodes, move_list, face_nodes, stiffness
):
    dof_count = element_loads.shape[0]
    slot_count = element_loads.shape[1]
    per_element = element_nodes.shape[0]
    components = dof_count // per_element
    owned_count = start_field.shape[1]
    face_count = face_nodes.shape[1]
    myself = lax.axis_index(("seg", "sub"))
    target_device = move_list[0]
    target_slot = move_list[1]
    list_place = move_list[2]
    staying = target_device == myself
    records = (
        jnp.where(staying[None, :], element_loads, 0.0),
        jnp.where(staying[None, :], element_coefs, 0.0),
    )
    devices = lax.axis_size(("seg", "sub"))
    columns = devices * NEAR_CAP
    where_to = jnp.where(~staying, target_device * NEAR_CAP + list_place, columns)
    packed_loads = (
        jnp.zeros((dof_count, columns), jnp.float32).at[:, where_to].set(element_loads, mode="drop")
    )
    packed_coefs = (
        jnp.zeros((2, columns), jnp.float32).at[:, where_to].set(element_coefs, mode="drop")
    )
    packed_slots = (
        jnp.zeros((1, columns), jnp.int32)
        .at[:, where_to]
        .set((target_slot + 1)[None, :], mode="drop")
    )
    received = (
        lax.all_to_all(packed_loads, ("seg", "sub"), split_axis=1, concat_axis=1, tiled=True),
        lax.all_to_all(packed_coefs, ("seg", "sub"), split_axis=1, concat_axis=1, tiled=True),
        lax.all_to_all(packed_slots, ("seg", "sub"), split_axis=1, concat_axis=1, tiled=True),
    )
    got_slots = received[2][0]
    where_to = jnp.where(got_slots > 0, got_slots - 1, slot_count)
    records = (
        records[0].at[:, where_to].set(received[0], mode="drop"),
        records[1].at[:, where_to].set(received[1], mode="drop"),
    )
    moved_loads, moved_coefs = records
    flat_nodes = element_nodes.reshape(-1)
    back_list = face_nodes[0]
    ahead_list = face_nodes[1]
    blocks = stiffness.reshape(2 * dof_count, dof_count)

    def extend_field(field):
        from_before = shifted(field[:, ahead_list], ("seg", "sub"), 1)
        from_after = shifted(field[:, back_list], ("seg", "sub"), -1)
        return jnp.concatenate([field, from_before, from_after], axis=1)

    def assemble(values):
        channels = values.shape[0] // per_element
        partial_sums = (
            jnp.zeros((channels, owned_count + 2 * face_count), jnp.float32)
            .at[:, flat_nodes]
            .add(values.reshape(channels, -1))
        )
        to_before = partial_sums[:, owned_count : owned_count + face_count]
        to_after = partial_sums[:, owned_count + face_count :]
        from_after = shifted(to_before, ("seg", "sub"), -1)
        from_before = shifted(to_after, ("seg", "sub"), 1)
        return (
            partial_sums[:, :owned_count]
            .at[:, ahead_list]
            .add(from_after)
            .at[:, back_list]
            .add(from_before)
        )

    def operate(field):
        gathered = extend_field(field)[:, flat_nodes].reshape(dof_count, slot_count)
        products = jnp.dot(
            blocks, gathered, precision=lax.Precision.HIGHEST, preferred_element_type=jnp.float32
        )
        return assemble(
            products[:dof_count] * moved_coefs[0] + products[dof_count:] * moved_coefs[1]
        )

    diagonals = jnp.diagonal(stiffness, axis1=1, axis2=2)
    element_diag = diagonals[0][:, None] * moved_coefs[0] + diagonals[1][:, None] * moved_coefs[1]
    totals = assemble(jnp.concatenate([moved_loads, element_diag], axis=0))
    right_side = totals[:components]
    diagonal = totals[components:]
    field = start_field
    scaled_center = center / half_width
    for sweep_index in range(SWEEPS):
        residual = right_side - operate(field)
        update = residual / (center * diagonal)
        ratio = 1.0 / scaled_center
        for degree_step in range(DEGREE):
            field = field + update
            if degree_step + 1 < DEGREE:
                residual = residual - operate(update)
                ratio_next = 1.0 / (2.0 * scaled_center - ratio)
                update = (
                    ratio_next * ratio * update
                    + 2.0 * ratio_next / half_width * residual / diagonal
                )
                ratio = ratio_next
    return (field, moved_loads, moved_coefs)


def solution(mesh):
    return jax.shard_map(
        local,
        mesh=mesh,
        in_specs=(
            P(None, ("seg", "sub")),
            P(None, ("seg", "sub")),
            P(None, ("seg", "sub")),
            P(None, ("seg", "sub")),
            P(None, ("seg", "sub")),
            P(None, ("seg", "sub")),
            P(),
        ),
        out_specs=(P(None, ("seg", "sub")), P(None, ("seg", "sub")), P(None, ("seg", "sub"))),
        check_vma=False,
    )
```

profile of v0, /device:TPU:6, one launch (start us, length us, event | category | flops | bytes accessed | tf_op | source)
XLA Modules:
  0.0 1875.8 jit_solution(17156017127629865213)
XLA Ops:
  12.0 8.1 collective-permute-start.3
  32.3 9.6 copy.257
  47.1 9.8 all-to-all-start.2
  75.9 56.5 %gather_fusion.3 = f32[16384,3]{1,0:T(8,128)} fusion(f32[3,7296]{0,1:T(8,128)} %pad_maximum_fusion, s32[16384]{0:T(1024)S(1)} %broadcast_clamp_fusion), kind=kCustom, calls=%fused_computation.3 | custom fusion | bytes 458752 | tf_op jit(solution)/shard_map/gather | solution.py:95
  157.3 89.7 %scatter_custom_fusion.8 = f32[3,7296]{0,1:T(8,128)} fusion(s32[16384]{0:T(1024)} %bitcast.180, f32[16384,3]{1,0:T(8,128)} %copy.271, f32[]{:T(128)} %constant.19.clone.1), kind=kCustom, calls=%fused_computation.72 | custom fusion | flops 49152 | bytes 88064 | tf_op jit(solution)/shard_map/scatter-add | solution.py:80
  247.0 9.2 scatter_fusion
  261.9 89.7 %scatter_custom_fusion.5 = f32[6,7296]{0,1:T(8,128)} fusion(s32[16384]{0:T(1024)} %bitcast.181, f32[16384,6]{1,0:T(8,128)} %copy.264, f32[]{:T(128)} %constant.19.clone.1), kind=kCustom, calls=%fused_computation.74 | custom fusion | flops 98304 | bytes 175616 | tf_op jit(solution)/shard_map/scatter-add | solution.py:80
  352.5 7.6 collective-permute-start
  363.0 7.9 collective-permute-start.4
  424.6 7.9 collective-permute-start.7
  434.5 7.2 collective-permute-done.6
  444.5 56.5 %gather_fusion.6 = f32[16384,3]{1,0:T(8,128)} fusion(f32[3,7296]{0,1:T(8,128)} %copy.278, s32[16384]{0:T(1024)S(1)} %broadcast_clamp_fusion), kind=kCustom, calls=%fused_computation.6 | custom fusion | bytes 458752 | tf_op jit(solution)/shard_map/gather | solution.py:95
  513.2 89.7 %scatter_custom_fusion.11 = f32[3,7296]{0,1:T(8,128)} fusion(s32[16384]{0:T(1024)} %bitcast.182, f32[16384,3]{1,0:T(8,128)} %copy.281, f32[]{:T(128)} %constant.19.clone.1), kind=kCustom, calls=%fused_computation.70 | custom fusion | flops 49152 | bytes 88064 | tf_op jit(solution)/shard_map/scatter-add | solution.py:80
  633.2 7.4 collective-permute-start.11
  642.6 7.2 collective-permute-done.10
  652.6 56.5 %gather_fusion.9 = f32[16384,3]{1,0:T(8,128)} fusion(f32[3,7296]{0,1:T(8,128)} %copy.287, s32[16384]{0:T(1024)S(1)} %broadcast_clamp_fusion), kind=kCustom, calls=%fused_computation.9 | custom fusion | bytes 458752 | tf_op jit(solution)/shard_map/gather | solution.py:95
  721.3 89.7 %scatter_custom_fusion.14 = f32[3,7296]{0,1:T(8,128)} fusion(s32[16384]{0:T(1024)} %bitcast.183, f32[16384,3]{1,0:T(8,128)} %copy.290, f32[]{:T(128)} %constant.19.clone.1), kind=kCustom, calls=%fused_computation.68 | custom fusion | flops 49152 | bytes 88064 | tf_op jit(solution)/shard_map/scatter-add | solution.py:80
  841.2 7.4 collective-permute-start.15
  860.6 56.5 %gather_fusion.12 = f32[16384,3]{1,0:T(8,128)} fusion(f32[3,7296]{0,1:T(8,128)} %copy.296, s32[16384]{0:T(1024)S(1)} %broadcast_clamp_fusion), kind=kCustom, calls=%fused_computation.12 | custom fusion | bytes 458752 | tf_op jit(solution)/shard_map/gather | solution.py:95
  929.2 89.7 %scatter_custom_fusion.17 = f32[3,7296]{0,1:T(8,128)} fusion(s32[16384]{0:T(1024)} %bitcast.184, f32[16384,3]{1,0:T(8,128)} %copy.299, f32[]{:T(128)} %constant.19.clone.1), kind=kCustom, calls=%fused_computation.66 | custom fusion | flops 49152 | bytes 88064 | tf_op jit(solution)/shard_map/scatter-add | solution.py:80
  1049.2 7.4 collective-permute-start.19
  1068.6 56.5 %gather_fusion.15 = f32[16384,3]{1,0:T(8,128)} fusion(f32[3,7296]{0,1:T(8,128)} %copy.305, s32[16384]{0:T(1024)S(1)} %broadcast_clamp_fusion), kind=kCustom, calls=%fused_computation.15 | custom fusion | bytes 458752 | tf_op jit(solution)/shard_map/gather | solution.py:95
  1137.3 89.7 %scatter_custom_fusion.20 = f32[3,7296]{0,1:T(8,128)} fusion(s32[16384]{0:T(1024)} %bitcast.185, f32[16384,3]{1,0:T(8,128)} %copy.308, f32[]{:T(128)} %constant.19.clone.1), kind=kCustom, calls=%fused_computation.64 | custom fusion | flops 49152 | bytes 88064 | tf_op jit(solution)/shard_map/scatter-add | solution.py:80
  1257.1 7.4 collective-permute-start.23
  1276.5 56.5 %gather_fusion.18 = f32[16384,3]{1,0:T(8,128)} fusion(f32[3,7296]{0,1:T(8,128)} %copy.314, s32[16384]{0:T(1024)S(1)} %broadcast_clamp_fusion), kind=kCustom, calls=%fused_computation.18 | custom fusion | bytes 458752 | tf_op jit(solution)/shard_map/gather | solution.py:95
  1345.2 89.7 %scatter_custom_fusion.23 = f32[3,7296]{0,1:T(8,128)} fusion(s32[16384]{0:T(1024)} %bitcast.186, f32[16384,3]{1,0:T(8,128)} %copy.317, f32[]{:T(128)} %constant.19.clone.1), kind=kCustom, calls=%fused_computation.62 | custom fusion | flops 49152 | bytes 88064 | tf_op jit(solution)/shard_map/scatter-add | solution.py:80
  1465.0 7.4 collective-permute-start.27
  1484.4 56.5 %gather_fusion.21 = f32[16384,3]{1,0:T(8,128)} fusion(f32[3,7296]{0,1:T(8,128)} %copy.323, s32[16384]{0:T(1024)S(1)} %broadcast_clamp_fusion), kind=kCustom, calls=%fused_computation.21 | custom fusion | bytes 458752 | tf_op jit(solution)/shard_map/gather | solution.py:95
  1553.1 89.7 %scatter_custom_fusion.26 = f32[3,7296]{0,1:T(8,128)} fusion(s32[16384]{0:T(1024)} %bitcast.187, f32[16384,3]{1,0:T(8,128)} %copy.326, f32[]{:T(128)} %constant.19.clone.1), kind=kCustom, calls=%fused_computation.60 | custom fusion | flops 49152 | bytes 88064 | tf_op jit(solution)/shard_map/scatter-add | solution.py:80
  1673.0 7.4 collective-permute-start.31
  1692.4 56.5 %gather_fusion.24 = f32[16384,3]{1,0:T(8,128)} fusion(f32[3,7296]{0,1:T(8,128)} %copy.332, s32[16384]{0:T(1024)S(1)} %broadcast_clamp_fusion), kind=kCustom, calls=%fused_computation.24 | custom fusion | bytes 458752 | tf_op jit(solution)/shard_map/gather | solution.py:95
  1761.0 89.7 %scatter_custom_fusion.29 = f32[3,7296]{0,1:T(8,128)} fusion(s32[16384]{0:T(1024)} %bitcast.188, f32[16384,3]{1,0:T(8,128)} %copy.335, f32[]{:T(128)} %constant.19.clone.1), kind=kCustom, calls=%fused_computation.58 | custom fusion | flops 49152 | bytes 88064 | tf_op jit(solution)/shard_map/scatter-add | solution.py:80
  (282 shorter events, 496.0 us)
Async XLA Ops:
  7.4 64.4 %collective-permute-start.2 = (f32[3,192]{0,1:T(8,128)S(1)}, f32[3,192]{0,1:T(8,128)S(1)}, u32[]{:S(2)}, u32[]{:S(2)}) collective-permute-start(f32[3,192]{0,1:T(8,128)S(1)} %bitcast.233), channel_id=1, source_target_pairs={{0,1},{1,2},{2,3},{3,4},{4,5},{5,6},{6,7},{7,8},{8,9},{9,10},{10,1... | collective-permute-start | bytes 6920 | tf_op jit(solution)/shard_map/ppermute | solution.py:18
  12.0 59.8 %collective-permute-start.3 = (f32[3,192]{0,1:T(8,128)S(1)}, f32[3,192]{0,1:T(8,128)S(1)}, u32[]{:S(2)}, u32[]{:S(2)}) collective-permute-start(f32[3,192]{0,1:T(8,128)S(1)} %bitcast.234), channel_id=1, source_target_pairs={{1,0},{2,1},{3,2},{4,3},{5,4},{6,5},{7,6},{8,7},{9,8},{10,9},{11,1... | collective-permute-start | bytes 6920 | tf_op jit(solution)/shard_map/ppermute | solution.py:18
  22.3 24.2 %all-to-all-start = ((s32[1,128,16]{2,0,1:T(1,128)}), s32[1,128,16]{2,0,1:T(1,128)S(1)}, u32[]{:S(2)}, u32[]{:S(2)}) async-start(s32[1,128,16]{2,0,1:T(1,128)} %bitcast.4), calls=%async_computation | async-start | bytes 131072 | tf_op jit(solution)/shard_map/all_to_all | solution.py:56
  47.1 18.4 all-to-all-start.2
  66.1 180.8 %all-to-all-start.1 = ((f32[192,128,16]{0,2,1:T(8,128)}), f32[192,128,16]{0,2,1:T(8,128)S(1)}, u32[]{:S(2)}, u32[]{:S(2)}) async-start(f32[192,128,16]{0,2,1:T(8,128)} %bitcast.7), calls=%async_computation.1 | async-start | bytes 4194304 | tf_op jit(solution)/shard_map/all_to_all | solution.py:54
  352.5 41.5 %collective-permute-start = (f32[6,192]{0,1:T(8,128)S(1)}, f32[6,192]{0,1:T(8,128)S(1)}, u32[]{:S(2)}, u32[]{:S(2)}) collective-permute-start(f32[6,192]{0,1:T(8,128)S(1)} %get-tuple-element.54), channel_id=1, source_target_pairs={{1,0},{2,1},{3,2},{4,3},{5,4},{6,5},{7,6},{8,7},{9,8},{10,9},{11,1... | collective-permute-start | bytes 13832 | tf_op jit(solution)/shard_map/ppermute | solution.py:18
  360.2 39.1 %collective-permute-start.1 = (f32[6,192]{0,1:T(8,128)S(1)}, f32[6,192]{0,1:T(8,128)S(1)}, u32[]{:S(2)}, u32[]{:S(2)}) collective-permute-start(f32[6,192]{0,1:T(8,128)S(1)} %get-tuple-element.53), channel_id=1, source_target_pairs={{0,1},{1,2},{2,3},{3,4},{4,5},{5,6},{6,7},{7,8},{8,9},{9,10},{10,1... | collective-permute-start | bytes 13832 | tf_op jit(solution)/shard_map/ppermute | solution.py:18
  363.0 13.8 collective-permute-start.4
  370.9 11.1 collective-permute-start.5
  424.6 9.9 collective-permute-start.7
  432.6 9.1 collective-permute-start.6
  603.8 8.3 collective-permute-start.8
  605.7 11.6 collective-permute-start.9
  633.2 9.4 collective-permute-start.11
  640.7 9.1 collective-permute-start.10
  813.8 11.6 collective-permute-start.13
  841.2 9.8 collective-permute-start.15
  848.6 9.1 collective-permute-start.14
  1021.8 11.6 collective-permute-start.17
  1049.2 9.6 collective-permute-start.19
  1056.7 9.1 collective-permute-start.18
  1229.8 11.6 collective-permute-start.21
  1257.1 9.6 collective-permute-start.23
  1264.6 9.1 collective-permute-start.22
  1437.7 11.6 collective-permute-start.25
  1465.0 9.6 collective-permute-start.27
  1472.5 9.1 collective-permute-start.26
  1645.6 11.6 collective-permute-start.29
  1673.0 9.7 collective-permute-start.31
  1680.4 9.1 collective-permute-start.30
  1851.7 9.8 collective-permute-start.32
  1853.6 13.1 collective-permute-start.33
  (15 other events, 194.9 us)
where the time goes:
time: 1890 us; the launch traced here: 1880 us
  other arithmetic  912 us (48%)
  local copies, waits for them, and re-layouts  751 us (40%)
  starting transfers between devices  148 us (8%)
  waiting for transfers between devices  53.9 us (3%)
    scatter-add x9, other arithmetic, assemble(): partial_sums = jnp.zeros((channels, owned_count + 2 * face_count), jnp.fl...  807 us
    gather x16, local copies, waits for them, and re-layouts, operate(): gathered = extend_field(field)[:, flat_nodes].reshape(dof_count, slot_count)  495 us
    ppermute x34, starting transfers between devices, shifted(): return lax.ppermute(x, axis, pairs)  127 us
    scatter-add x18, other arithmetic, assemble(): return partial_sums[:, :owned_count].at[:, ahead_list].add(from_after).at...  94.3 us
    ppermute x34, waiting for transfers between devices, shifted(): return lax.ppermute(x, axis, pairs)  49.2 us
    reshape x18, local copies, waits for them, and re-layouts, assemble(): values.reshape(channels, -1)  46.9 us
  transfers between devices with their start and end apart: 37, of which 8 were waited for; matrix products, arithmetic and copies ran while one was open for 16% of the time, Pallas kernels for 0%

commit v1 on v0

v1 whole, which is shorter than its diff:
```python
import functools

import jax
import jax.numpy as jnp
from jax import lax
from jax.experimental import pallas as pl
from jax.experimental.pallas import tpu as pltpu
from jax.sharding import PartitionSpec as P

NEAR_CAP = 16
DEGREE = 4
SWEEPS = 2
DEVICES = 128
ELEM = 256
DOFS = 192
PER = 64
OWN = 6912
FACE = 192
BACK_ROW = 27
AHEAD_ROW = 28
OWN_CHUNKS = OWN // 128
CHUNKS = 58
NODE_BLOCK = 8

center = 1.125
half_width = 0.875

AXES = ("seg", "sub")
F32 = jnp.float32
BF16 = jnp.bfloat16


def fill_table(table, rows, chunks):
    for c in range(3):
        for k in range(chunks):
            table[c * CHUNKS + k] = jnp.broadcast_to(rows(c, k), (8, 128))


def lane_gather(table, index, chunks):
    lane = index & 127
    chunk = index >> 7
    found = [jnp.zeros((8, 128), F32)] * 3
    for k in range(chunks):
        here = chunk == k
        for c in range(3):
            picked = jnp.take_along_axis(table[c * CHUNKS + k], lane, axis=1)
            found[c] = jnp.where(here, picked, found[c])
    return found


def gather_elements(table, nodes_ref, out_ref):
    def block(b, carry):
        row = pl.multiple_of(b * 8, 8)
        for half in range(2):
            lanes = slice(half * 128, half * 128 + 128)
            found = lane_gather(table, nodes_ref[pl.ds(row, 8), lanes], CHUNKS)
            for c in range(3):
                out_ref[pl.ds(c * PER + row, 8), lanes] = found[c]
        return carry

    lax.fori_loop(0, PER // 8, block, 0)


def split(x):
    high = x.astype(BF16).astype(F32)
    return high, x - high


def one_hot_sum(node_rows, value_rows):
    low = node_rows & 255
    high = node_rows >> 8
    row_of = lax.broadcasted_iota(jnp.int32, (32, 256), 0)
    lane_of = lax.broadcasted_iota(jnp.int32, (256, 256), 0)
    parts = [part for rows in value_rows for part in split(rows)]
    left, right = [], []
    for k in range(node_rows.shape[0]):
        here = high[k : k + 1, :] == row_of
        left.append(
            jnp.concatenate(
                [jnp.where(here, part[k : k + 1, :], 0.0) for part in parts], axis=0
            ).astype(BF16)
        )
        right.append(jnp.where(low[k : k + 1, :] == lane_of, 1.0, 0.0).astype(BF16))
    left = jnp.concatenate(left, axis=1)
    right = jnp.concatenate(right, axis=1)
    return lax.dot_general(left, right, (((1,), (1,)), ((), ())), preferred_element_type=F32)


def scatter_elements(nodes_ref, value_refs, sums_ref):
    sums_ref[...] = jnp.zeros_like(sums_ref)

    def block(b, carry):
        row = pl.multiple_of(b * NODE_BLOCK, NODE_BLOCK)
        values = [
            ref[pl.ds(c * PER + row, NODE_BLOCK), :] for ref in value_refs for c in range(3)
        ]
        sums_ref[...] += one_hot_sum(nodes_ref[pl.ds(row, NODE_BLOCK), :], values)
        return carry

    lax.fori_loop(0, PER // NODE_BLOCK, block, 0)


def add_parts(sums, first, channels):
    return jnp.concatenate(
        [
            sums[64 * (first + c) : 64 * (first + c) + 32]
            + sums[64 * (first + c) + 32 : 64 * (first + c) + 64]
            for c in range(channels)
        ],
        axis=0,
    )


def face_messages(table, state, places, to_before, to_after, row):
    found = lane_gather(table, places, OWN_CHUNKS)
    for c in range(3):
        got = found[c]
        turned = pltpu.roll(got, 64, 1)
        to_before[row + c : row + c + 1, :] = jnp.concatenate([got[0:1], got[1:2]], axis=1)
        to_after[row + c : row + c + 1, :] = jnp.concatenate([got[2:3], turned[1:2]], axis=1)
        if state is not None:
            back = 32 * c + BACK_ROW
            ahead = 32 * c + AHEAD_ROW
            to_before[row + 3 + c : row + 4 + c, :] = state[back : back + 1, :]
            to_after[row + 3 + c : row + 4 + c, :] = state[ahead : ahead + 1, :]


def state_rows(ref):
    return lambda c, k: ref[32 * c + k // 2 : 32 * c + k // 2 + 1, (k % 2) * 128 : (k % 2) * 128 + 128]


def completed(partial, before, after, lists, row):
    nodes = lists[0:2, :]
    values = [
        jnp.concatenate(
            [before[row + 3 + c : row + 4 + c, :], after[row + 3 + c : row + 4 + c, :]], axis=0
        )
        for c in range(3)
    ]
    shared = add_parts(one_hot_sum(nodes, values), 0, 3)
    line = lax.broadcasted_iota(jnp.int32, (32, 256), 0)
    ghost = jnp.concatenate(
        [
            jnp.where(
                line == BACK_ROW,
                before[row + c : row + c + 1, :],
                jnp.where(line == AHEAD_ROW, after[row + c : row + c + 1, :], 0.0),
            )
            for c in range(3)
        ],
        axis=0,
    )
    return partial + shared + ghost


def pack_kernel(
    loads_ref,
    coefs_ref,
    move_ref,
    face_ref,
    field_ref,
    far_ref,
    to_before,
    to_after,
    lists_ref,
    places_ref,
    table,
):
    me = lax.axis_index(AXES)
    away = move_ref[0:1, :] - me
    place = move_ref[2:3, :]
    code = jnp.where(
        away == 1,
        DEVICES + place,
        jnp.where(away == -1, DEVICES + NEAR_CAP + place, jnp.where(away == 0, -1, move_ref[0:1, :])),
    )
    rows = DEVICES + 2 * NEAR_CAP
    chosen = jnp.where(code == lax.broadcasted_iota(jnp.int32, (rows, ELEM), 0), 1.0, 0.0)
    slot = (move_ref[1:2, :] + 1).astype(F32)
    records = jnp.concatenate(
        [loads_ref[...], coefs_ref[...], slot, jnp.zeros((61, ELEM), F32)], axis=0
    )
    packed = lax.dot_general(
        chosen,
        records,
        (((1,), (1,)), ((), ())),
        precision=lax.Precision.HIGHEST,
        preferred_element_type=F32,
    )
    far_ref[...] = packed[:DEVICES]
    to_after[0:NEAR_CAP, :] = packed[DEVICES : DEVICES + NEAR_CAP]
    to_before[0:NEAR_CAP, :] = packed[DEVICES + NEAR_CAP :]
    to_after[NEAR_CAP:, :] = jnp.zeros((8, 256), F32)
    to_before[NEAR_CAP:, :] = jnp.zeros((8, 256), F32)
    lists_ref[...] = jnp.full((8, 256), -1, jnp.int32)
    lists_ref[0:2, 0:FACE] = face_ref[...]
    places_ref[...] = jnp.zeros((8, 128), jnp.int32)
    places_ref[0:1, :] = face_ref[0:1, 0:128]
    places_ref[1:2, 0:64] = face_ref[0:1, 128:192]
    places_ref[1:2, 64:128] = face_ref[1:2, 128:192]
    places_ref[2:3, :] = face_ref[1:2, 0:128]
    fill_table(table, lambda c, k: field_ref[c : c + 1, 128 * k : 128 * k + 128], OWN_CHUNKS)
    face_messages(table, None, places_ref[...], to_before, to_after, NEAR_CAP)


def first_kernel(
    field_ref,
    before,
    after,
    nodes_ref,
    stiff_ref,
    state_ref,
    index_ref,
    high_ref,
    low_ref,
    products_ref,
    table,
    gathered,
):
    state_ref[...] = jnp.zeros_like(state_ref)
    for c in range(3):
        for h in range(BACK_ROW):
            state_ref[32 * c + h : 32 * c + h + 1, :] = field_ref[c : c + 1, 256 * h : 256 * h + 256]
        row = NEAR_CAP + c
        state_ref[32 * c + BACK_ROW : 32 * c + BACK_ROW + 1, :] = before[row : row + 1, :]
        state_ref[32 * c + AHEAD_ROW : 32 * c + AHEAD_ROW + 1, :] = after[row : row + 1, :]
    nodes = nodes_ref[...]
    index_ref[...] = jnp.where(nodes >= OWN + FACE, nodes + 64, nodes)
    fill_table(table, state_rows(state_ref), CHUNKS)
    gather_elements(table, index_ref, gathered)
    x_high, x_low = split(gathered[...])
    x_high = x_high.astype(BF16)
    x_low = x_low.astype(BF16)
    for i in range(2):
        block_high, block_low = split(stiff_ref[i])
        block_high = block_high.astype(BF16)
        block_low = block_low.astype(BF16)
        high_ref[i] = block_high
        low_ref[i] = block_low
        products_ref[i] = (
            jnp.dot(block_high, x_low, preferred_element_type=F32)
            + jnp.dot(block_low, x_high, preferred_element_type=F32)
            + jnp.dot(block_high, x_high, preferred_element_type=F32)
        )


def place_kernel(
    loads_ref,
    coefs_ref,
    move_ref,
    far_ref,
    before,
    after,
    stiff_ref,
    products_ref,
    nodes_ref,
    places_ref,
    moved_loads,
    moved_coefs,
    partial_ref,
    diagonal_ref,
    to_before,
    to_after,
    sums,
    first_values,
    diag_values,
    table,
):
    me = lax.axis_index(AXES)
    received = jnp.concatenate([far_ref[...], before[0:NEAR_CAP, :], after[0:NEAR_CAP, :]], axis=0)
    rows = DEVICES + 2 * NEAR_CAP
    slot = received[:, DOFS + 2 : DOFS + 3].astype(jnp.int32)
    chosen = jnp.where(slot == lax.broadcasted_iota(jnp.int32, (rows, ELEM), 1) + 1, 1.0, 0.0)
    arrived = lax.dot_general(
        received,
        chosen,
        (((0,), (0,)), ((), ())),
        precision=lax.Precision.HIGHEST,
        preferred_element_type=F32,
    )
    stays = move_ref[0:1, :] == me
    loads = jnp.where(stays, loads_ref[...], 0.0) + arrived[:DOFS]
    coefs = jnp.where(stays, coefs_ref[...], 0.0) + arrived[DOFS : DOFS + 2]
    moved_loads[...] = loads
    moved_coefs[...] = coefs
    first_values[...] = loads - (products_ref[0] * coefs[0:1, :] + products_ref[1] * coefs[1:2, :])
    eye = lax.broadcasted_iota(jnp.int32, (DOFS, DOFS), 0) == lax.broadcasted_iota(
        jnp.int32, (DOFS, DOFS), 1
    )
    first_diag = jnp.sum(jnp.where(eye, stiff_ref[0], 0.0), axis=1, keepdims=True)
    second_diag = jnp.sum(jnp.where(eye, stiff_ref[1], 0.0), axis=1, keepdims=True)
    diag_values[...] = first_diag * coefs[0:1, :] + second_diag * coefs[1:2, :]
    scatter_elements(nodes_ref, [first_values, diag_values], sums)
    total = sums[...]
    partial_ref[...] = add_parts(total, 0, 3)
    diagonal_ref[...] = add_parts(total, 3, 3)
    to_before[12:16, :] = jnp.zeros((4, 256), F32)
    to_after[12:16, :] = jnp.zeros((4, 256), F32)
    for i, ref in enumerate((partial_ref, diagonal_ref)):
        fill_table(table, state_rows(ref), OWN_CHUNKS)
        face_messages(table, ref, places_ref[...], to_before, to_after, 6 * i)


def apply_operator(
    update_ref, nodes_ref, coefs_ref, high_ref, low_ref, places_ref, partial_ref, to_before, to_after,
    table, gathered, sums,
):
    fill_table(table, state_rows(update_ref), CHUNKS)
    gather_elements(table, nodes_ref, gathered)
    x = gathered[...]
    total = jnp.zeros((DOFS, ELEM), F32)
    for i in range(2):
        x_high, x_low = split(x * coefs_ref[i : i + 1, :])
        x_high = x_high.astype(BF16)
        x_low = x_low.astype(BF16)
        total += (
            jnp.dot(high_ref[i], x_low, preferred_element_type=F32)
            + jnp.dot(low_ref[i], x_high, preferred_element_type=F32)
            + jnp.dot(high_ref[i], x_high, preferred_element_type=F32)
        )
    gathered[...] = total
    scatter_elements(nodes_ref, [gathered], sums)
    partial_ref[...] = add_parts(sums[...], 0, 3)
    to_before[6:8, :] = jnp.zeros((2, 256), F32)
    to_after[6:8, :] = jnp.zeros((2, 256), F32)
    fill_table(table, state_rows(partial_ref), OWN_CHUNKS)
    face_messages(table, partial_ref, places_ref[...], to_before, to_after, 0)


def start_kernel(
    step,
    partial_ref,
    diagonal_ref,
    before,
    after,
    lists_ref,
    field_ref,
    nodes_ref,
    coefs_ref,
    high_ref,
    low_ref,
    places_ref,
    residual_out,
    inverse_out,
    update_out,
    field_out,
    partial_out,
    to_before,
    to_after,
    table,
    gathered,
    sums,
):
    residual = completed(partial_ref[...], before, after, lists_ref, 0)
    diagonal = completed(diagonal_ref[...], before, after, lists_ref, 6)
    inverse = jnp.where(diagonal == 0.0, 0.0, 1.0 / diagonal)
    update = step[1] * (residual * inverse)
    residual_out[...] = residual
    inverse_out[...] = inverse
    update_out[...] = update
    field_out[...] = field_ref[...] + update
    apply_operator(
        update_out, nodes_ref, coefs_ref, high_ref, low_ref, places_ref, partial_out, to_before,
        to_after, table, gathered, sums,
    )


def step_kernel(
    step,
    partial_ref,
    before,
    after,
    lists_ref,
    residual_ref,
    inverse_ref,
    update_ref,
    field_ref,
    nodes_ref,
    coefs_ref,
    high_ref,
    low_ref,
    places_ref,
    residual_out,
    update_out,
    field_out,
    partial_out,
    to_before,
    to_after,
    table,
    gathered,
    sums,
):
    residual = residual_ref[...] - completed(partial_ref[...], before, after, lists_ref, 0)
    update = step[1] * (residual * inverse_ref[...])
    if step[0]:
        update = step[0] * update_ref[...] + update
    residual_out[...] = residual
    update_out[...] = update
    field_out[...] = field_ref[...] + update
    apply_operator(
        update_out, nodes_ref, coefs_ref, high_ref, low_ref, places_ref, partial_out, to_before,
        to_after, table, gathered, sums,
    )


def last_kernel(
    step, partial_ref, before, after, lists_ref, residual_ref, inverse_ref, update_ref, field_ref, out_ref
):
    residual = residual_ref[...] - completed(partial_ref[...], before, after, lists_ref, 0)
    update = step[1] * (residual * inverse_ref[...])
    if step[0]:
        update = step[0] * update_ref[...] + update
    field = field_ref[...] + update
    for c in range(3):
        for h in range(BACK_ROW):
            out_ref[c : c + 1, 256 * h : 256 * h + 256] = field[32 * c + h : 32 * c + h + 1, :]


def shaped(*shape, dtype=F32):
    return jax.ShapeDtypeStruct(shape, dtype)


def steps():
    scaled_center = center / half_width
    found = []
    for _ in range(SWEEPS):
        found.append((0.0, 1.0 / center))
        ratio = 1.0 / scaled_center
        for _ in range(DEGREE - 1):
            ratio_next = 1.0 / (2.0 * scaled_center - ratio)
            found.append((ratio_next * ratio, 2.0 * ratio_next / half_width))
            ratio = ratio_next
    return found


def exchange(to_before, to_after):
    devices = DEVICES
    from_before = lax.ppermute(to_after, AXES, [(i, i + 1) for i in range(devices - 1)])
    from_after = lax.ppermute(to_before, AXES, [(i + 1, i) for i in range(devices - 1)])
    return from_before, from_after


TABLE = pltpu.VMEM((3 * CHUNKS, 8, 128), F32)
ELEMENT_ROWS = pltpu.VMEM((DOFS, ELEM), F32)
STATE = shaped(96, 256)


def local(
    start_field, element_loads, element_coefs, element_nodes, move_list, face_nodes, stiffness
):
    far, to_before, to_after, lists, places = pl.pallas_call(
        pack_kernel,
        out_shape=(
            shaped(DEVICES, 256),
            shaped(24, 256),
            shaped(24, 256),
            shaped(8, 256, dtype=jnp.int32),
            shaped(8, 128, dtype=jnp.int32),
        ),
        scratch_shapes=[TABLE],
        name="pack",
    )(element_loads, element_coefs, move_list, face_nodes, start_field)
    before, after = exchange(to_before, to_after)
    far = lax.all_to_all(far, AXES, split_axis=0, concat_axis=0, tiled=True)
    field, nodes, high, low, products = pl.pallas_call(
        first_kernel,
        out_shape=(
            STATE,
            shaped(PER, ELEM, dtype=jnp.int32),
            shaped(2, DOFS, DOFS, dtype=BF16),
            shaped(2, DOFS, DOFS, dtype=BF16),
            shaped(2, DOFS, ELEM),
        ),
        scratch_shapes=[TABLE, ELEMENT_ROWS],
        name="first",
    )(start_field, before, after, element_nodes, stiffness)
    moved_loads, moved_coefs, partial, diagonal, to_before, to_after = pl.pallas_call(
        place_kernel,
        out_shape=(
            shaped(DOFS, ELEM),
            shaped(2, ELEM),
            STATE,
            STATE,
            shaped(16, 256),
            shaped(16, 256),
        ),
        scratch_shapes=[pltpu.VMEM((384, 256), F32), ELEMENT_ROWS, ELEMENT_ROWS, TABLE],
        name="place",
    )(
        element_loads, element_coefs, move_list, far, before, after, stiffness, products, nodes,
        places,
    )
    before, after = exchange(to_before, to_after)
    plan = steps()
    scratch = [TABLE, ELEMENT_ROWS, pltpu.VMEM((192, 256), F32)]
    message = shaped(8, 256)
    residual, inverse, update, field, partial, to_before, to_after = pl.pallas_call(
        functools.partial(start_kernel, plan[0]),
        out_shape=(STATE, STATE, STATE, STATE, STATE, message, message),
        scratch_shapes=scratch,
        name="start",
    )(partial, diagonal, before, after, lists, field, nodes, moved_coefs, high, low, places)
    for step in plan[1:-1]:
        before, after = exchange(to_before, to_after)
        residual, update, field, partial, to_before, to_after = pl.pallas_call(
            functools.partial(step_kernel, step),
            out_shape=(STATE, STATE, STATE, STATE, message, message),
            scratch_shapes=scratch,
            name="step",
        )(
            partial, before, after, lists, residual, inverse, update, field, nodes, moved_coefs,
            high, low, places,
        )
    before, after = exchange(to_before, to_after)
    field = pl.pallas_call(
        functools.partial(last_kernel, plan[-1]), out_shape=shaped(3, OWN), name="last"
    )(partial, before, after, lists, residual, inverse, update, field)
    return field, moved_loads, moved_coefs


def solution(mesh):
    split_columns = P(None, AXES)
    return jax.shard_map(
        local,
        mesh=mesh,
        in_specs=(split_columns,) * 6 + (P(),),
        out_specs=(split_columns,) * 3,
        check_vma=False,
    )
```

time: 1890 us -> 214 us (0.11)
  other arithmetic: 912 us -> 0 us
  local copies, waits for them, and re-layouts: 751 us -> 7.71 us
  Pallas kernels: 0 us -> 92.2 us
  starting transfers between devices: 148 us -> 98.6 us
  waiting for transfers between devices: 53.9 us -> 13.7 us
    scatter-add x27 -> x0, other arithmetic: 901 us -> none  [the longest x9 807 us: assemble(): partial_sums = jnp.zeros((channels, owned_count + 2 * face_count), jnp.fl...]
    gather x47 -> x0, local copies, waits for them, and re-layouts: 544 us -> none  [the longest x16 495 us: operate(): gathered = extend_field(field)[:, flat_nodes].reshape(dof_count, slot_count)]
    pallas_call x0 -> x11, Pallas kernels: none -> 92.2 us  [the longest x6 63.6 us: local(): pl.pallas_call(functools.partial(step_kernel, step), out_shape=(STATE, ST...]
    slice x21 -> x0, local copies, waits for them, and re-layouts: 52.6 us -> none  [the longest x9 35.9 us: assemble(): partial_sums[:, :owned_count].at[:, ahead_list].add(from_after)]
    reshape x26 -> x0, local copies, waits for them, and re-layouts: 48.1 us -> none  [the longest x18 46.9 us: assemble(): values.reshape(channels, -1)]
    ppermute x34 -> x18, starting transfers between devices: 127 us -> 88.1 us  [the longest x9 70.8 us: exchange(): lax.ppermute(to_before, AXES, [(i + 1, i) for i in range(devices - 1)])]
    ppermute x34 -> x18, waiting for transfers between devices: 49.2 us -> 13.7 us  [the longest x9 13.7 us: exchange(): lax.ppermute(to_before, AXES, [(i + 1, i) for i in range(devices - 1)])]
    scatter x5 -> x0, local copies, waits for them, and re-layouts: 21.3 us -> none  [the longest x1 9.16 us: local(): records[0].at[:, where_to].set(received[0], mode='drop')]
  transfers between devices with their start and end apart: 37 -> 19, of which waited for: 8 -> 9; matrix products, arithmetic and copies ran while one was open for 16% -> 0% of each run, Pallas kernels for 0% -> 3%
where the time goes in v1:
time: 214 us; the launch traced here: 213 us
  starting transfers between devices  98.6 us (46%)
  Pallas kernels  92.2 us (43%)
  waiting for transfers between devices  13.7 us (6%)
  local copies, waits for them, and re-layouts  7.71 us (4%)
    ppermute x9, starting transfers between devices, exchange(): lax.ppermute(to_before, AXES, [(i + 1, i) for i in range(devices - 1)])  70.8 us
    pallas_call x6, Pallas kernels, local(): pl.pallas_call(functools.partial(step_kernel, step), out_shape=(STATE, ST...  63.6 us
    ppermute x9, starting transfers between devices, exchange(): lax.ppermute(to_after, AXES, [(i, i + 1) for i in range(devices - 1)])  17.3 us
    ppermute x9, waiting for transfers between devices, exchange(): lax.ppermute(to_before, AXES, [(i + 1, i) for i in range(devices - 1)])  13.7 us
    pallas_call x1, Pallas kernels, local(): pl.pallas_call(functools.partial(start_kernel, plan[0]), out_shape=(STATE...  10.7 us
    all_to_all x1, starting transfers between devices, local(): far = lax.all_to_all(far, AXES, split_axis=0, concat_axis=0, tiled=True)  10.5 us
    pallas_call x1, Pallas kernels, local(): pl.pallas_call(place_kernel, out_shape=(shaped(DOFS, ELEM), shaped(2, ELE...  7.9 us
    unnamed x41, local copies, waits for them, and re-layouts  6.02 us
  transfers between devices with their start and end apart: 19, of which 9 were waited for; matrix products, arithmetic and copies ran while one was open for 0% of the time, Pallas kernels for 3%

profile of v1, /device:TPU:6, one launch (start us, length us, event | category | flops | bytes accessed | tf_op | source)
XLA Modules:
  0.0 213.2 jit_solution(16868630260267024247)
XLA Ops:
  0.6 2.1 pack.1
  2.7 1.7 copy.10
  4.4 10.5 %all-to-all-start = ((f32[128,1,256]{2,1,0:T(1,128)}), f32[128,1,256]{2,1,0:T(1,128)S(1)}, u32[]{:S(2)}, u32[]{:S(2)}) async-start(f32[128,1,256]{2,1,0:T(1,128)} %copy.10), calls=%async_computation | async-start | bytes 262144 | tf_op jit(solution)/shard_map/all_to_all | solution.py:464
  14.9 2.0 collective-permute-start
  16.9 7.8 %collective-permute-start.1 = (f32[24,256]{1,0:T(8,128)S(1)}, f32[24,256]{1,0:T(8,128)S(1)}, u32[]{:S(2)}, u32[]{:S(2)}) collective-permute-start(f32[24,256]{1,0:T(8,128)S(1)} %copy-done.18), channel_id=1, source_target_pairs={{1,0},{2,1},{3,2},{4,3},{5,4},{6,5},{7,6},{8,7},{9,8},{10,9},{11,1... | collective-permute-start | bytes 73736 | tf_op jit(solution)/shard_map/ppermute | solution.py:439
  26.8 5.8 %first.1 = (f32[96,256]{1,0:T(8,128)}, s32[64,256]{1,0:T(8,128)}, bf16[2,192,192]{2,1,0:T(8,128)(2,1)}, bf16[2,192,192]{2,1,0:T(8,128)(2,1)}, f32[2,192,256]{2,1,0:T(8,128)}) custom-call(f32[3,6912]{1,0:T(4,128)} %field_ref.3, f32[24,256]{1,0:T(8,128)} %copy-done, f32[24,256]{1,0:T(8,128)} %copy-done.1, s32[64,256]{1,0:T(8,128)} %nodes_ref.1, ...), custom_call_target="tpu_custom_call" | custom-call | tf_op jit(solution)/shard_map/first/pallas_call | solution.py:465
  33.3 7.9 %place.1 = (f32[192,256]{1,0:T(8,128)}, f32[2,256]{1,0:T(2,128)}, f32[96,256]{1,0:T(8,128)}, f32[96,256]{1,0:T(8,128)}, f32[16,256]{1,0:T(8,128)}, /*index=5*/f32[16,256]{1,0:T(8,128)}) custom-call(f32[192,256]{1,0:T(8,128)} %loads_ref.3, f32[2,256]{1,0:T(2,128)} %coefs_ref.3, s32[3,256]{1,0:T(4,128)} %move_ref.3, f32[128,256]{1,0:T(8,128)} %bitcast.4, ...), custom_call_target="tpu_custom_call" | custom-call | tf_op jit(solution)/shard_map/place/pallas_call | solution.py:477
  41.2 1.9 collective-permute-start.2
  43.1 7.9 %collective-permute-start.3 = (f32[16,256]{1,0:T(8,128)}, f32[16,256]{1,0:T(8,128)S(1)}, u32[]{:S(2)}, u32[]{:S(2)}) collective-permute-start(f32[16,256]{1,0:T(8,128)} %get-tuple-element.71), channel_id=1, source_target_pairs={{1,0},{2,1},{3,2},{4,3},{5,4},{6,5},{7,6},{8,7},{9,8},{10,9},{11,1... | collective-permute-start | bytes 49160 | tf_op jit(solution)/shard_map/ppermute | solution.py:439
  51.0 1.6 collective-permute-done.3.after
  53.2 10.7 %start.1 = (f32[96,256]{1,0:T(8,128)}, f32[96,256]{1,0:T(8,128)}, f32[96,256]{1,0:T(8,128)}, f32[96,256]{1,0:T(8,128)}, f32[96,256]{1,0:T(8,128)}, /*index=5*/f32[8,256]{1,0:T(8,128)}, f32[8,256]{1,0:T(8,128)}) custom-call(f32[96,256]{1,0:T(8,128)} %get-tuple-element.68.partial_ref, f32[96,256]{1,0:T(8,128)} %get-tuple-element.69.diagonal_ref, ...), custom_call_target="tpu_custom_call" | custom-call | tf_op jit(solution)/shard_map/start/pallas_call | solution.py:497
  63.9 1.9 collective-permute-start.4
  65.9 7.9 %collective-permute-start.5 = (f32[8,256]{1,0:T(8,128)}, f32[8,256]{1,0:T(8,128)S(1)}, u32[]{:S(2)}, u32[]{:S(2)}) collective-permute-start(f32[8,256]{1,0:T(8,128)} %get-tuple-element.79), channel_id=1, source_target_pairs={{1,0},{2,1},{3,2},{4,3},{5,4},{6,5},{7,6},{8,7},{9,8},{10,9},{11,1... | collective-permute-start | bytes 24584 | tf_op jit(solution)/shard_map/ppermute | solution.py:439
  75.9 10.6 %step.6 = (f32[96,256]{1,0:T(8,128)}, f32[96,256]{1,0:T(8,128)}, f32[96,256]{1,0:T(8,128)}, f32[96,256]{1,0:T(8,128)}, f32[8,256]{1,0:T(8,128)}, /*index=5*/f32[8,256]{1,0:T(8,128)}) custom-call(f32[96,256]{1,0:T(8,128)} %get-tuple-element.77.partial_ref, f32[8,256]{1,0:T(8,128)} %copy-done.6, f32[8,256]{1,0:T(8,128)} %copy-done.11, ...), custom_call_target="tpu_custom_call" | custom-call | tf_op jit(solution)/shard_map/step/pallas_call | solution.py:505
  86.5 1.9 collective-permute-start.6
  88.4 7.9 %collective-permute-start.7 = (f32[8,256]{1,0:T(8,128)}, f32[8,256]{1,0:T(8,128)S(1)}, u32[]{:S(2)}, u32[]{:S(2)}) collective-permute-start(f32[8,256]{1,0:T(8,128)} %get-tuple-element.86), channel_id=1, source_target_pairs={{1,0},{2,1},{3,2},{4,3},{5,4},{6,5},{7,6},{8,7},{9,8},{10,9},{11,1... | collective-permute-start | bytes 24584 | tf_op jit(solution)/shard_map/ppermute | solution.py:439
  98.4 10.6 %step.7 = (f32[96,256]{1,0:T(8,128)}, f32[96,256]{1,0:T(8,128)}, f32[96,256]{1,0:T(8,128)}, f32[96,256]{1,0:T(8,128)}, f32[8,256]{1,0:T(8,128)}, /*index=5*/f32[8,256]{1,0:T(8,128)}) custom-call(f32[96,256]{1,0:T(8,128)} %get-tuple-element.84.partial_ref, f32[8,256]{1,0:T(8,128)} %copy-done.7, f32[8,256]{1,0:T(8,128)} %copy-done.12, ...), custom_call_target="tpu_custom_call" | custom-call | tf_op jit(solution)/shard_map/step/pallas_call | solution.py:505
  109.0 1.9 collective-permute-start.8
  110.9 7.9 %collective-permute-start.9 = (f32[8,256]{1,0:T(8,128)}, f32[8,256]{1,0:T(8,128)S(1)}, u32[]{:S(2)}, u32[]{:S(2)}) collective-permute-start(f32[8,256]{1,0:T(8,128)} %get-tuple-element.92), channel_id=1, source_target_pairs={{1,0},{2,1},{3,2},{4,3},{5,4},{6,5},{7,6},{8,7},{9,8},{10,9},{11,1... | collective-permute-start | bytes 24584 | tf_op jit(solution)/shard_map/ppermute | solution.py:439
  120.9 10.6 %step.8 = (f32[96,256]{1,0:T(8,128)}, f32[96,256]{1,0:T(8,128)}, f32[96,256]{1,0:T(8,128)}, f32[96,256]{1,0:T(8,128)}, f32[8,256]{1,0:T(8,128)}, /*index=5*/f32[8,256]{1,0:T(8,128)}) custom-call(f32[96,256]{1,0:T(8,128)} %get-tuple-element.90.partial_ref, f32[8,256]{1,0:T(8,128)} %copy-done.8, f32[8,256]{1,0:T(8,128)} %copy-done.13, ...), custom_call_target="tpu_custom_call" | custom-call | tf_op jit(solution)/shard_map/step/pallas_call | solution.py:505
  131.6 1.9 collective-permute-start.10
  133.5 7.9 %collective-permute-start.11 = (f32[8,256]{1,0:T(8,128)}, f32[8,256]{1,0:T(8,128)S(1)}, u32[]{:S(2)}, u32[]{:S(2)}) collective-permute-start(f32[8,256]{1,0:T(8,128)} %get-tuple-element.98), channel_id=1, source_target_pairs={{1,0},{2,1},{3,2},{4,3},{5,4},{6,5},{7,6},{8,7},{9,8},{10,9},{11,1... | collective-permute-start | bytes 24584 | tf_op jit(solution)/shard_map/ppermute | solution.py:439
  143.5 10.6 %step.9 = (f32[96,256]{1,0:T(8,128)}, f32[96,256]{1,0:T(8,128)}, f32[96,256]{1,0:T(8,128)}, f32[96,256]{1,0:T(8,128)}, f32[8,256]{1,0:T(8,128)}, /*index=5*/f32[8,256]{1,0:T(8,128)}) custom-call(f32[96,256]{1,0:T(8,128)} %get-tuple-element.96.partial_ref, f32[8,256]{1,0:T(8,128)} %copy-done.9, f32[8,256]{1,0:T(8,128)} %copy-done.14, ...), custom_call_target="tpu_custom_call" | custom-call | tf_op jit(solution)/shard_map/step/pallas_call | solution.py:505
  154.1 1.9 collective-permute-start.12
  156.0 8.0 %collective-permute-start.13 = (f32[8,256]{1,0:T(8,128)}, f32[8,256]{1,0:T(8,128)S(1)}, u32[]{:S(2)}, u32[]{:S(2)}) collective-permute-start(f32[8,256]{1,0:T(8,128)} %get-tuple-element.104), channel_id=1, source_target_pairs={{1,0},{2,1},{3,2},{4,3},{5,4},{6,5},{7,6},{8,7},{9,8},{10,9},{11,1... | collective-permute-start | bytes 24584 | tf_op jit(solution)/shard_map/ppermute | solution.py:439
  166.0 10.6 %step.10 = (f32[96,256]{1,0:T(8,128)}, f32[96,256]{1,0:T(8,128)}, f32[96,256]{1,0:T(8,128)}, f32[96,256]{1,0:T(8,128)}, f32[8,256]{1,0:T(8,128)}, /*index=5*/f32[8,256]{1,0:T(8,128)}) custom-call(f32[96,256]{1,0:T(8,128)} %get-tuple-element.102.partial_ref, f32[8,256]{1,0:T(8,128)} %copy-done.10, f32[8,256]{1,0:T(8,128)} %copy-done.15, ...), custom_call_target="tpu_custom_call" | custom-call | tf_op jit(solution)/shard_map/step/pallas_call | solution.py:505
  176.6 1.9 collective-permute-start.14
  178.6 7.9 %collective-permute-start.15 = (f32[8,256]{1,0:T(8,128)}, f32[8,256]{1,0:T(8,128)S(1)}, u32[]{:S(2)}, u32[]{:S(2)}) collective-permute-start(f32[8,256]{1,0:T(8,128)} %get-tuple-element.110), channel_id=1, source_target_pairs={{1,0},{2,1},{3,2},{4,3},{5,4},{6,5},{7,6},{8,7},{9,8},{10,9},{11,1... | collective-permute-start | bytes 24584 | tf_op jit(solution)/shard_map/ppermute | solution.py:439
  188.6 10.6 %step.11 = (f32[96,256]{1,0:T(8,128)}, f32[96,256]{1,0:T(8,128)}, f32[96,256]{1,0:T(8,128)}, f32[96,256]{1,0:T(8,128)}, f32[8,256]{1,0:T(8,128)}, /*index=5*/f32[8,256]{1,0:T(8,128)}) custom-call(f32[96,256]{1,0:T(8,128)} %get-tuple-element.108.partial_ref, f32[8,256]{1,0:T(8,128)} %copy-done.4, f32[8,256]{1,0:T(8,128)} %copy-done.5, ...), custom_call_target="tpu_custom_call" | custom-call | tf_op jit(solution)/shard_map/step/pallas_call | solution.py:505
  199.2 1.9 collective-permute-start.16
  201.1 7.9 %collective-permute-start.17 = (f32[8,256]{1,0:T(8,128)}, f32[8,256]{1,0:T(8,128)S(1)}, u32[]{:S(2)}, u32[]{:S(2)}) collective-permute-start(f32[8,256]{1,0:T(8,128)} %get-tuple-element.116), channel_id=1, source_target_pairs={{1,0},{2,1},{3,2},{4,3},{5,4},{6,5},{7,6},{8,7},{9,8},{10,9},{11,1... | collective-permute-start | bytes 24584 | tf_op jit(solution)/shard_map/ppermute | solution.py:439
  211.1 2.1 last.1
  (59 shorter events, 18.1 us)
Async XLA Ops:
  4.4 10.5 %copy-start.19 = (f32[24,256]{1,0:T(8,128)S(1)}, f32[24,256]{1,0:T(8,128)}, u32[]{:S(2)}) copy-start(f32[24,256]{1,0:T(8,128)} %get-tuple-element.63) | copy-start | bytes 73732
  4.4 12.5 %copy-start.18 = (f32[24,256]{1,0:T(8,128)S(1)}, f32[24,256]{1,0:T(8,128)}, u32[]{:S(2)}) copy-start(f32[24,256]{1,0:T(8,128)} %get-tuple-element.64) | copy-start | bytes 73732
  4.4 28.2 %all-to-all-start = ((f32[128,1,256]{2,1,0:T(1,128)}), f32[128,1,256]{2,1,0:T(1,128)S(1)}, u32[]{:S(2)}, u32[]{:S(2)}) async-start(f32[128,1,256]{2,1,0:T(1,128)} %copy.10), calls=%async_computation | async-start | bytes 262144 | tf_op jit(solution)/shard_map/all_to_all | solution.py:464
  14.9 9.8 %collective-permute-start = (f32[24,256]{1,0:T(8,128)S(1)}, f32[24,256]{1,0:T(8,128)S(1)}, u32[]{:S(2)}, u32[]{:S(2)}) collective-permute-start(f32[24,256]{1,0:T(8,128)S(1)} %copy-done.19), channel_id=1, source_target_pairs={{0,1},{1,2},{2,3},{3,4},{4,5},{5,6},{6,7},{7,8},{8,9},{9,10},{10,1... | collective-permute-start | bytes 73736 | tf_op jit(solution)/shard_map/ppermute | solution.py:438
  16.9 9.3 %collective-permute-start.1 = (f32[24,256]{1,0:T(8,128)S(1)}, f32[24,256]{1,0:T(8,128)S(1)}, u32[]{:S(2)}, u32[]{:S(2)}) collective-permute-start(f32[24,256]{1,0:T(8,128)S(1)} %copy-done.18), channel_id=1, source_target_pairs={{1,0},{2,1},{3,2},{4,3},{5,4},{6,5},{7,6},{8,7},{9,8},{10,9},{11,1... | collective-permute-start | bytes 73736 | tf_op jit(solution)/shard_map/ppermute | solution.py:439
  24.7 1.5 copy-start
  26.2 0.6 copy-start.1
  41.2 9.8 %collective-permute-start.2 = (f32[16,256]{1,0:T(8,128)}, f32[16,256]{1,0:T(8,128)S(1)}, u32[]{:S(2)}, u32[]{:S(2)}) collective-permute-start(f32[16,256]{1,0:T(8,128)} %get-tuple-element.70), channel_id=1, source_target_pairs={{0,1},{1,2},{2,3},{3,4},{4,5},{5,6},{6,7},{7,8},{8,9},{9,10},{10,1... | collective-permute-start | bytes 49160 | tf_op jit(solution)/shard_map/ppermute | solution.py:438
  43.1 9.5 %collective-permute-start.3 = (f32[16,256]{1,0:T(8,128)}, f32[16,256]{1,0:T(8,128)S(1)}, u32[]{:S(2)}, u32[]{:S(2)}) collective-permute-start(f32[16,256]{1,0:T(8,128)} %get-tuple-element.71), channel_id=1, source_target_pairs={{1,0},{2,1},{3,2},{4,3},{5,4},{6,5},{7,6},{8,7},{9,8},{10,9},{11,1... | collective-permute-start | bytes 49160 | tf_op jit(solution)/shard_map/ppermute | solution.py:439
  51.0 1.6 copy-start.2
  52.6 0.6 copy-start.3
  63.9 9.8 %collective-permute-start.4 = (f32[8,256]{1,0:T(8,128)}, f32[8,256]{1,0:T(8,128)S(1)}, u32[]{:S(2)}, u32[]{:S(2)}) collective-permute-start(f32[8,256]{1,0:T(8,128)} %get-tuple-element.78), channel_id=1, source_target_pairs={{0,1},{1,2},{2,3},{3,4},{4,5},{5,6},{6,7},{7,8},{8,9},{9,10},{10,1... | collective-permute-start | bytes 24584 | tf_op jit(solution)/shard_map/ppermute | solution.py:438
  65.9 9.4 %collective-permute-start.5 = (f32[8,256]{1,0:T(8,128)}, f32[8,256]{1,0:T(8,128)S(1)}, u32[]{:S(2)}, u32[]{:S(2)}) collective-permute-start(f32[8,256]{1,0:T(8,128)} %get-tuple-element.79), channel_id=1, source_target_pairs={{1,0},{2,1},{3,2},{4,3},{5,4},{6,5},{7,6},{8,7},{9,8},{10,9},{11,1... | collective-permute-start | bytes 24584 | tf_op jit(solution)/shard_map/ppermute | solution.py:439
  73.7 1.5 copy-start.6
  86.5 9.8 %collective-permute-start.6 = (f32[8,256]{1,0:T(8,128)}, f32[8,256]{1,0:T(8,128)S(1)}, u32[]{:S(2)}, u32[]{:S(2)}) collective-permute-start(f32[8,256]{1,0:T(8,128)} %get-tuple-element.85), channel_id=1, source_target_pairs={{0,1},{1,2},{2,3},{3,4},{4,5},{5,6},{6,7},{7,8},{8,9},{9,10},{10,1... | collective-permute-start | bytes 24584 | tf_op jit(solution)/shard_map/ppermute | solution.py:438
  88.4 9.4 %collective-permute-start.7 = (f32[8,256]{1,0:T(8,128)}, f32[8,256]{1,0:T(8,128)S(1)}, u32[]{:S(2)}, u32[]{:S(2)}) collective-permute-start(f32[8,256]{1,0:T(8,128)} %get-tuple-element.86), channel_id=1, source_target_pairs={{1,0},{2,1},{3,2},{4,3},{5,4},{6,5},{7,6},{8,7},{9,8},{10,9},{11,1... | collective-permute-start | bytes 24584 | tf_op jit(solution)/shard_map/ppermute | solution.py:439
  96.3 1.5 copy-start.7
  109.0 9.8 %collective-permute-start.8 = (f32[8,256]{1,0:T(8,128)}, f32[8,256]{1,0:T(8,128)S(1)}, u32[]{:S(2)}, u32[]{:S(2)}) collective-permute-start(f32[8,256]{1,0:T(8,128)} %get-tuple-element.91), channel_id=1, source_target_pairs={{0,1},{1,2},{2,3},{3,4},{4,5},{5,6},{6,7},{7,8},{8,9},{9,10},{10,1... | collective-permute-start | bytes 24584 | tf_op jit(solution)/shard_map/ppermute | solution.py:438
  110.9 9.4 %collective-permute-start.9 = (f32[8,256]{1,0:T(8,128)}, f32[8,256]{1,0:T(8,128)S(1)}, u32[]{:S(2)}, u32[]{:S(2)}) collective-permute-start(f32[8,256]{1,0:T(8,128)} %get-tuple-element.92), channel_id=1, source_target_pairs={{1,0},{2,1},{3,2},{4,3},{5,4},{6,5},{7,6},{8,7},{9,8},{10,9},{11,1... | collective-permute-start | bytes 24584 | tf_op jit(solution)/shard_map/ppermute | solution.py:439
  118.8 1.5 copy-start.8
  131.6 9.8 %collective-permute-start.10 = (f32[8,256]{1,0:T(8,128)}, f32[8,256]{1,0:T(8,128)S(1)}, u32[]{:S(2)}, u32[]{:S(2)}) collective-permute-start(f32[8,256]{1,0:T(8,128)} %get-tuple-element.97), channel_id=1, source_target_pairs={{0,1},{1,2},{2,3},{3,4},{4,5},{5,6},{6,7},{7,8},{8,9},{9,10},{10,1... | collective-permute-start | bytes 24584 | tf_op jit(solution)/shard_map/ppermute | solution.py:438
  133.5 9.4 %collective-permute-start.11 = (f32[8,256]{1,0:T(8,128)}, f32[8,256]{1,0:T(8,128)S(1)}, u32[]{:S(2)}, u32[]{:S(2)}) collective-permute-start(f32[8,256]{1,0:T(8,128)} %get-tuple-element.98), channel_id=1, source_target_pairs={{1,0},{2,1},{3,2},{4,3},{5,4},{6,5},{7,6},{8,7},{9,8},{10,9},{11,1... | collective-permute-start | bytes 24584 | tf_op jit(solution)/shard_map/ppermute | solution.py:439
  141.3 1.5 copy-start.9
  154.1 10.0 %collective-permute-start.12 = (f32[8,256]{1,0:T(8,128)}, f32[8,256]{1,0:T(8,128)S(1)}, u32[]{:S(2)}, u32[]{:S(2)}) collective-permute-start(f32[8,256]{1,0:T(8,128)} %get-tuple-element.103), channel_id=1, source_target_pairs={{0,1},{1,2},{2,3},{3,4},{4,5},{5,6},{6,7},{7,8},{8,9},{9,10},{10,1... | collective-permute-start | bytes 24584 | tf_op jit(solution)/shard_map/ppermute | solution.py:438
  156.0 9.4 %collective-permute-start.13 = (f32[8,256]{1,0:T(8,128)}, f32[8,256]{1,0:T(8,128)S(1)}, u32[]{:S(2)}, u32[]{:S(2)}) collective-permute-start(f32[8,256]{1,0:T(8,128)} %get-tuple-element.104), channel_id=1, source_target_pairs={{1,0},{2,1},{3,2},{4,3},{5,4},{6,5},{7,6},{8,7},{9,8},{10,9},{11,1... | collective-permute-start | bytes 24584 | tf_op jit(solution)/shard_map/ppermute | solution.py:439
  164.1 1.4 copy-start.10
  176.6 9.8 %collective-permute-start.14 = (f32[8,256]{1,0:T(8,128)}, f32[8,256]{1,0:T(8,128)S(1)}, u32[]{:S(2)}, u32[]{:S(2)}) collective-permute-start(f32[8,256]{1,0:T(8,128)} %get-tuple-element.109), channel_id=1, source_target_pairs={{0,1},{1,2},{2,3},{3,4},{4,5},{5,6},{6,7},{7,8},{8,9},{9,10},{10,1... | collective-permute-start | bytes 24584 | tf_op jit(solution)/shard_map/ppermute | solution.py:438
  178.6 9.4 %collective-permute-start.15 = (f32[8,256]{1,0:T(8,128)}, f32[8,256]{1,0:T(8,128)S(1)}, u32[]{:S(2)}, u32[]{:S(2)}) collective-permute-start(f32[8,256]{1,0:T(8,128)} %get-tuple-element.110), channel_id=1, source_target_pairs={{1,0},{2,1},{3,2},{4,3},{5,4},{6,5},{7,6},{8,7},{9,8},{10,9},{11,1... | collective-permute-start | bytes 24584 | tf_op jit(solution)/shard_map/ppermute | solution.py:439
  186.4 1.5 copy-start.4
  199.2 9.8 %collective-permute-start.16 = (f32[8,256]{1,0:T(8,128)}, f32[8,256]{1,0:T(8,128)S(1)}, u32[]{:S(2)}, u32[]{:S(2)}) collective-permute-start(f32[8,256]{1,0:T(8,128)} %get-tuple-element.115), channel_id=1, source_target_pairs={{0,1},{1,2},{2,3},{3,4},{4,5},{5,6},{6,7},{7,8},{8,9},{9,10},{10,1... | collective-permute-start | bytes 24584 | tf_op jit(solution)/shard_map/ppermute | solution.py:438
  201.1 9.4 %collective-permute-start.17 = (f32[8,256]{1,0:T(8,128)}, f32[8,256]{1,0:T(8,128)S(1)}, u32[]{:S(2)}, u32[]{:S(2)}) collective-permute-start(f32[8,256]{1,0:T(8,128)} %get-tuple-element.116), channel_id=1, source_target_pairs={{1,0},{2,1},{3,2},{4,3},{5,4},{6,5},{7,6},{8,7},{9,8},{10,9},{11,1... | collective-permute-start | bytes 24584 | tf_op jit(solution)/shard_map/ppermute | solution.py:439
  209.0 1.5 copy-start.16
  (7 other events, 4.2 us)

commit v2 on v0

v2 whole, which is shorter than its diff:
```python
import functools

import jax
import jax.numpy as jnp
from jax import lax
from jax.experimental import pallas as pl
from jax.experimental.pallas import tpu as pltpu
from jax.sharding import PartitionSpec as P

NEAR_CAP = 16
DEGREE = 4
SWEEPS = 2
DEVICES = 128
ELEM = 256
DOFS = 192
PER = 64
OWN = 6912
FACE = 192
OWN_ROWS = OWN // 256
OWN_CHUNKS = OWN // 128
SHARED_ROWS = 6
BLOCK = 32

center = 1.125
half_width = 0.875

AXES = ("seg", "sub")
F32 = jnp.float32
BF16 = jnp.bfloat16


def split(x):
    high = x.astype(BF16).astype(F32)
    return high, x - high


def iota(shape, dimension):
    return lax.broadcasted_iota(jnp.int32, shape, dimension)


def lane_pick(rows, lane):
    return jnp.take_along_axis(rows, lane, axis=1)


def gather_own(state_ref, nodes_ref, out_ref, extra_ref=None, extra_out=None):
    def block(b, carry):
        row = pl.multiple_of(b * 8, 8)
        for half in range(2):
            lanes = slice(half * 128, half * 128 + 128)
            index = nodes_ref[pl.ds(row, 8), lanes]
            lane = index & 127
            chunk = index >> 7
            found = [jnp.zeros((8, 128), F32)] * (3 if extra_ref is None else 4)
            for k in range(OWN_CHUNKS):
                here = chunk == k
                part = slice((k % 2) * 128, (k % 2) * 128 + 128)
                for c in range(len(found)):
                    source, line = (state_ref, 32 * c + k // 2) if c < 3 else (extra_ref, k // 2)
                    values = jnp.broadcast_to(source[line : line + 1, part], (8, 128))
                    found[c] = jnp.where(here, lane_pick(values, lane), found[c])
            for c in range(3):
                out_ref[pl.ds(c * PER + row, 8), lanes] = found[c]
            if extra_ref is not None:
                extra_out[pl.ds(row, 8), lanes] = found[3]
        return carry

    lax.fori_loop(0, PER // 8, block, 0)


def gather_shared(shared_ref, index_ref, rows_ref, first_row):
    tables = [
        [
            jnp.broadcast_to(shared_ref[8 * c + r : 8 * c + r + 1, :], (8, 128))
            for r in range(SHARED_ROWS)
        ]
        for c in range(3)
    ]
    for b in range(PER // 8):
        for half in range(2):
            lanes = slice(half * 128, half * 128 + 128)
            index = index_ref[8 * b : 8 * b + 8, lanes]
            lane = index & 127
            chunk = index >> 7
            masks = [chunk == r for r in range(first_row, SHARED_ROWS)]
            for c in range(3):
                rows = slice(c * PER + 8 * b, c * PER + 8 * b + 8)
                found = rows_ref[rows, lanes]
                for r in range(first_row, SHARED_ROWS):
                    found = jnp.where(masks[r - first_row], lane_pick(tables[c][r], lane), found)
                rows_ref[rows, lanes] = found


def scatter_elements(nodes_ref, hot_ref, values_ref, high_ref, low_ref, sums_ref, channels):
    high, low = split(values_ref[...])
    high_ref[...] = high
    low_ref[...] = low
    sums_ref[...] = jnp.zeros_like(sums_ref)
    lines = iota((32, 256), 0).astype(F32).astype(BF16)
    zero = jnp.zeros((), BF16)

    def block(b, carry):
        row = pl.multiple_of(b * BLOCK, BLOCK)
        line = (nodes_ref[pl.ds(row, BLOCK), :] >> 8).astype(F32)
        left = []
        for k in range(BLOCK):
            here = line[k : k + 1, :].astype(BF16) == lines
            left.append(
                jnp.concatenate(
                    [
                        jnp.where(
                            here,
                            jnp.broadcast_to(ref[pl.ds(c * PER + row + k, 1), :], (32, 256)).astype(
                                BF16
                            ),
                            zero,
                        )
                        for ref in (high_ref, low_ref)
                        for c in range(channels)
                    ],
                    axis=0,
                )
            )
        left = jnp.concatenate(left, axis=1)
        right = hot_ref[pl.ds(pl.multiple_of(row * 256, 256), BLOCK * 256), :]
        sums_ref[...] += jnp.dot(left, right, preferred_element_type=F32)
        return carry

    lax.fori_loop(0, PER // BLOCK, block, 0)


def add_parts(sums_ref, first, channels):
    top = 32 * first
    low = top + 32 * channels
    return sums_ref[top : top + 96, :] + sums_ref[low : low + 96, :]


def expand_own_faces(places, channels, parts):
    lines = iota((32, 128), 0)
    lanes = iota((256, 128), 0)
    rows = []
    for values in channels:
        rest = values
        for _ in range(parts):
            high, rest = split(rest)
            rows.append(high)
    left, right = [], []
    for k in range(3):
        here = (places[k : k + 1, :] >> 8) == lines
        left.append(
            jnp.concatenate([jnp.where(here, r[k : k + 1, :], 0.0) for r in rows], axis=0).astype(BF16)
        )
        right.append(jnp.where((places[k : k + 1, :] & 255) == lanes, 1.0, 0.0).astype(BF16))
    sums = lax.dot_general(
        jnp.concatenate(left, axis=1),
        jnp.concatenate(right, axis=1),
        (((1,), (1,)), ((), ())),
        preferred_element_type=F32,
    )
    out = []
    for i in range(len(channels)):
        total = sums[32 * parts * i : 32 * parts * i + 32]
        for q in range(1, parts):
            start = 32 * (parts * i + q)
            total = total + sums[start : start + 32]
        out.append(total)
    return jnp.concatenate(out, axis=0)


def take_shared(state_ref, places, out_ref, base, ghosts):
    found = [[None] * 3 for _ in range(3)]
    line = iota((8, 128), 0)
    for r in range(3):
        place = jnp.broadcast_to(places[r : r + 1, :], (8, 128))
        lane = place & 127
        chunk = place >> 7
        masks = [
            [chunk == 2 * (8 * t + line) + half for half in range(2)] for t in range(4)
        ]
        for c in range(3):
            got = jnp.zeros((8, 128), F32)
            for t in range(4):
                for half in range(2):
                    values = state_ref[
                        32 * c + 8 * t : 32 * c + 8 * t + 8, half * 128 : half * 128 + 128
                    ]
                    got = jnp.where(masks[t][half], lane_pick(values, lane), got)
            found[c][r] = jnp.sum(got, axis=0, keepdims=True)
    for c in range(3):
        top = 32 * c + OWN_ROWS
        if ghosts:
            others = [
                state_ref[top : top + 1, 0:128],
                state_ref[top : top + 1, 128:256],
                state_ref[top + 1 : top + 2, 0:128],
                jnp.zeros((2, 128), F32),
            ]
        else:
            others = [jnp.zeros((5, 128), F32)]
        out_ref[base + 8 * c : base + 8 * c + 8, 0:128] = jnp.concatenate(found[c] + others, axis=0)


def from_neighbours(near_ref, far_ref, base):
    first_core = lax.axis_index("sub") == 0
    left = iota((1, 128), 1) < 64
    out = []
    for c in range(3):
        rows = slice(base + 8 * c, base + 8 * c + 8)
        near = near_ref[rows, 0:128]
        far = far_ref[rows, 0:128]
        before = jnp.where(first_core, far, near)
        after = jnp.where(first_core, near, far)
        before_turned = pltpu.roll(before, 64, 1)
        after_turned = pltpu.roll(after, 64, 1)
        out += [
            before[5:6],
            jnp.where(left, before_turned[4:5], after_turned[4:5]),
            after[3:4],
            before[2:3],
            jnp.where(left, before_turned[1:2], after_turned[1:2]),
            after[0:1],
            jnp.zeros((2, 128), F32),
        ]
    return jnp.concatenate(out, axis=0)


def pack_kernel(
    loads_ref, coefs_ref, move_ref, face_ref, field_ref, far_ref, near_out, other_out, places_ref, state_ref
):
    me = lax.axis_index(AXES)
    first_core = lax.axis_index("sub") == 0
    near = jnp.where(first_core, me + 1, me - 1)
    other = jnp.where(first_core, me - 1, me + 1)
    target = move_ref[0:1, :]
    place = move_ref[2:3, :]
    code = jnp.where(
        target == me,
        -1,
        jnp.where(
            target == near,
            DEVICES + place,
            jnp.where(target == other, DEVICES + NEAR_CAP + place, target),
        ),
    )
    rows = DEVICES + 2 * NEAR_CAP
    chosen = jnp.where(code == iota((rows, ELEM), 0), 1.0, 0.0)
    slot = (move_ref[1:2, :] + 1).astype(F32)
    records = jnp.concatenate(
        [loads_ref[...], coefs_ref[...], slot, jnp.zeros((61, ELEM), F32)], axis=0
    )
    packed = lax.dot_general(
        chosen,
        records,
        (((1,), (1,)), ((), ())),
        precision=lax.Precision.HIGHEST,
        preferred_element_type=F32,
    )
    far_ref[...] = packed[:DEVICES]
    near_out[0:NEAR_CAP, :] = packed[DEVICES : DEVICES + NEAR_CAP]
    other_out[0:NEAR_CAP, :] = packed[DEVICES + NEAR_CAP :]
    near_out[NEAR_CAP:, :] = jnp.zeros((24, 256), F32)
    places_ref[...] = jnp.zeros((8, 128), jnp.int32)
    places_ref[0:1, :] = face_ref[0:1, 0:128]
    places_ref[1:2, 0:64] = face_ref[0:1, 128:192]
    places_ref[1:2, 64:128] = face_ref[1:2, 128:192]
    places_ref[2:3, :] = face_ref[1:2, 0:128]
    state_ref[...] = jnp.zeros_like(state_ref)
    for c in range(3):
        for h in range(OWN_ROWS):
            state_ref[32 * c + h : 32 * c + h + 1, :] = field_ref[c : c + 1, 256 * h : 256 * h + 256]
    take_shared(state_ref, places_ref[...], near_out, NEAR_CAP, False)
    other_out[NEAR_CAP:, :] = near_out[NEAR_CAP:, :]


def index_kernel(
    state_ref,
    places_ref,
    nodes_ref,
    stiff_ref,
    index_ref,
    shared_index_ref,
    unshared_ref,
    hot_ref,
    high_ref,
    low_ref,
    gathered_ref,
    positions,
    found,
):
    nodes = nodes_ref[...]
    ghost = nodes - OWN
    ahead = ghost - FACE
    shared = jnp.where(ahead < 0, ghost, jnp.where(ahead < 128, ahead + 256, ahead + 64))
    index_ref[...] = jnp.where(ghost < 0, nodes, OWN + shared)
    places = places_ref[...]
    numbers = (128 * iota((3, 128), 0) + iota((3, 128), 1) + 1).astype(F32)
    positions[...] = expand_own_faces(places, [numbers], 2)
    line = iota((32, 256), 0)
    unshared_ref[...] = jnp.where((positions[...] == 0.0) & (line < OWN_ROWS), 1.0, 0.0)
    gather_own(state_ref, index_ref, gathered_ref, positions, found)
    shared_index_ref[...] = jnp.where(
        ghost < 0, found[...].astype(jnp.int32) - 1, shared + 3 * 128
    )
    for i in range(2):
        high, low = split(stiff_ref[i])
        high_ref[DOFS * i : DOFS * i + DOFS, :] = high.astype(BF16)
        low_ref[DOFS * i : DOFS * i + DOFS, :] = low.astype(BF16)
    found[...] = (index_ref[...] & 255).astype(F32)
    lanes = iota((16, 256), 1).astype(F32)

    for half in range(2):
        turned = found[:, half * 128 : half * 128 + 128].T
        for b in range(8):
            columns = turned[16 * b : 16 * b + 16]
            for n in range(PER):
                hot_ref[256 * n + half * 128 + 16 * b : 256 * n + half * 128 + 16 * b + 16, :] = (
                    jnp.where(columns[:, n : n + 1] == lanes, 1.0, 0.0).astype(BF16)
                )


def multiply_blocks(high_ref, low_ref, rows_ref):
    high, low = split(rows_ref[...])
    high = high.astype(BF16)
    low = low.astype(BF16)
    return (
        jnp.dot(low_ref[...], high, preferred_element_type=F32)
        + jnp.dot(high_ref[...], low, preferred_element_type=F32)
        + jnp.dot(high_ref[...], high, preferred_element_type=F32)
    )


def place_kernel(
    loads_ref,
    coefs_ref,
    move_ref,
    far_ref,
    near_in,
    other_in,
    field_message,
    stiff_ref,
    gathered_in,
    nodes_ref,
    shared_index_ref,
    places_ref,
    hot_ref,
    high_ref,
    low_ref,
    moved_loads,
    moved_coefs,
    partial_ref,
    diagonal_ref,
    shared_field,
    message,
    gathered,
    values,
    value_high,
    value_low,
    sums,
):
    shared_field[...] = field_message[NEAR_CAP:, 0:128] + from_neighbours(near_in, other_in, NEAR_CAP)
    gathered[...] = gathered_in[...]
    gather_shared(shared_field, shared_index_ref, gathered, 3)
    products = multiply_blocks(high_ref, low_ref, gathered)
    me = lax.axis_index(AXES)
    received = jnp.concatenate(
        [far_ref[...], near_in[0:NEAR_CAP, :], other_in[0:NEAR_CAP, :]], axis=0
    )
    rows = DEVICES + 2 * NEAR_CAP
    slot = received[:, DOFS + 2 : DOFS + 3].astype(jnp.int32)
    chosen = jnp.where(slot == iota((rows, ELEM), 1) + 1, 1.0, 0.0)
    arrived = lax.dot_general(
        received,
        chosen,
        (((0,), (0,)), ((), ())),
        precision=lax.Precision.HIGHEST,
        preferred_element_type=F32,
    )
    stays = move_ref[0:1, :] == me
    loads = jnp.where(stays, loads_ref[...], 0.0) + arrived[:DOFS]
    coefs = jnp.where(stays, coefs_ref[...], 0.0) + arrived[DOFS : DOFS + 2]
    moved_loads[...] = loads
    moved_coefs[...] = coefs
    values[0:DOFS, :] = loads - (products[:DOFS] * coefs[0:1, :] + products[DOFS:] * coefs[1:2, :])
    eye = iota((DOFS, DOFS), 0) == iota((DOFS, DOFS), 1)
    first_diag = jnp.sum(jnp.where(eye, stiff_ref[0], 0.0), axis=1, keepdims=True)
    second_diag = jnp.sum(jnp.where(eye, stiff_ref[1], 0.0), axis=1, keepdims=True)
    values[DOFS:, :] = first_diag * coefs[0:1, :] + second_diag * coefs[1:2, :]
    scatter_elements(nodes_ref, hot_ref, values, value_high, value_low, sums, 6)
    partial_ref[...] = add_parts(sums, 0, 6)
    diagonal_ref[...] = add_parts(sums, 3, 6)
    take_shared(partial_ref, places_ref[...], message, 0, True)
    take_shared(diagonal_ref, places_ref[...], message, 24, True)


def apply_operator(
    shared_update, gathered_in, shared_index_ref, nodes_ref, coefs_ref, places_ref, hot_ref, high_ref,
    low_ref, partial_ref, message, gathered, value_high, value_low, sums,
):
    gathered[...] = gathered_in[...]
    gather_shared(shared_update, shared_index_ref, gathered, 0)
    products = multiply_blocks(high_ref, low_ref, gathered)
    gathered[...] = products[:DOFS] * coefs_ref[0:1, :] + products[DOFS:] * coefs_ref[1:2, :]
    scatter_elements(nodes_ref, hot_ref, gathered, value_high, value_low, sums, 3)
    partial_ref[...] = add_parts(sums, 0, 3)
    take_shared(partial_ref, places_ref[...], message, 0, True)


def inverse_of(diagonal):
    return jnp.where(diagonal == 0.0, 0.0, 1.0 / diagonal)


def begin_unshared(
    step, partial_ref, diagonal_ref, unshared_ref, field_ref, nodes_ref, inverse_out, update_out,
    field_out, gathered_out,
):
    unshared = jnp.concatenate([unshared_ref[...]] * 3, axis=0)
    inverse = jnp.where(unshared > 0.0, inverse_of(diagonal_ref[...]), 0.0)
    update = step[1] * (partial_ref[...] * inverse)
    inverse_out[...] = inverse
    update_out[...] = update
    field_out[...] = field_ref[...] + update
    gather_own(update_out, nodes_ref, gathered_out)


def begin_shared(
    step, message_in, near_in, other_in, shared_field, gathered_in, shared_index_ref, nodes_ref,
    coefs_ref, places_ref, hot_ref, high_ref, low_ref, residual_out, inverse_out, update_out,
    field_out, partial_ref, message, gathered, value_high, value_low, sums,
):
    residual = message_in[0:24, :] + from_neighbours(near_in, other_in, 0)
    inverse = inverse_of(message_in[24:48, :] + from_neighbours(near_in, other_in, 24))
    update = step[1] * (residual * inverse)
    residual_out[...] = residual
    inverse_out[...] = inverse
    update_out[...] = update
    field_out[...] = shared_field[...] + update
    apply_operator(
        update_out, gathered_in, shared_index_ref, nodes_ref, coefs_ref, places_ref, hot_ref,
        high_ref, low_ref, partial_ref, message, gathered, value_high, value_low, sums,
    )


def next_update(step, residual, inverse, update):
    changed = step[1] * (residual * inverse)
    return step[0] * update + changed if step[0] else changed


def step_unshared(
    step, partial_ref, residual_ref, inverse_ref, update_ref, field_ref, nodes_ref, residual_out,
    update_out, field_out, gathered_out,
):
    residual = residual_ref[...] - partial_ref[...]
    update = next_update(step, residual, inverse_ref[...], update_ref[...])
    residual_out[...] = residual
    update_out[...] = update
    field_out[...] = field_ref[...] + update
    gather_own(update_out, nodes_ref, gathered_out)


def step_shared(
    step, message_in, near_in, other_in, residual_ref, inverse_ref, update_ref, field_ref,
    gathered_in, shared_index_ref, nodes_ref, coefs_ref, places_ref, hot_ref, high_ref, low_ref,
    residual_out, update_out, field_out, partial_ref, message, gathered, value_high, value_low, sums,
):
    residual = residual_ref[...] - (message_in[...] + from_neighbours(near_in, other_in, 0))
    update = next_update(step, residual, inverse_ref[...], update_ref[...])
    residual_out[...] = residual
    update_out[...] = update
    field_out[...] = field_ref[...] + update
    apply_operator(
        update_out, gathered_in, shared_index_ref, nodes_ref, coefs_ref, places_ref, hot_ref,
        high_ref, low_ref, partial_ref, message, gathered, value_high, value_low, sums,
    )


def last_unshared(step, partial_ref, residual_ref, inverse_ref, update_ref, field_ref, field_out):
    residual = residual_ref[...] - partial_ref[...]
    field_out[...] = field_ref[...] + next_update(step, residual, inverse_ref[...], update_ref[...])


def last_shared(
    step, message_in, near_in, other_in, residual_ref, inverse_ref, update_ref, shared_field,
    field_ref, unshared_ref, places_ref, out_ref,
):
    residual = residual_ref[...] - (message_in[...] + from_neighbours(near_in, other_in, 0))
    shared = shared_field[...] + next_update(step, residual, inverse_ref[...], update_ref[...])
    faces = expand_own_faces(places_ref[...], [shared[8 * c : 8 * c + 3] for c in range(3)], 3)
    unshared = jnp.concatenate([unshared_ref[...]] * 3, axis=0)
    field = jnp.where(unshared > 0.0, field_ref[...], faces)
    for c in range(3):
        for h in range(OWN_ROWS):
            out_ref[c : c + 1, 256 * h : 256 * h + 256] = field[32 * c + h : 32 * c + h + 1, :]


def shaped(*shape, dtype=F32):
    return jax.ShapeDtypeStruct(shape, dtype)


def steps():
    scaled_center = center / half_width
    found = []
    for _ in range(SWEEPS):
        found.append((0.0, 1.0 / center))
        ratio = 1.0 / scaled_center
        for _ in range(DEGREE - 1):
            ratio_next = 1.0 / (2.0 * scaled_center - ratio)
            found.append((ratio_next * ratio, 2.0 * ratio_next / half_width))
            ratio = ratio_next
    return found


NEAR_PAIRS = [(i, i ^ 1) for i in range(DEVICES)]
OTHER_PAIRS = [
    pair for i in range(1, DEVICES - 1, 2) for pair in ((i, i + 1), (i + 1, i))
]


def exchange(near_message, other_message):
    other = lax.ppermute(other_message, AXES, OTHER_PAIRS)
    near = lax.ppermute(near_message, AXES, NEAR_PAIRS)
    return near, other


def call(kernel, name, outs, scratch=(), limit=6):
    return pl.pallas_call(
        kernel,
        out_shape=outs,
        scratch_shapes=list(scratch),
        compiler_params=pltpu.CompilerParams(vmem_limit_bytes=limit << 20),
        name=name,
    )


STATE = shaped(96, 256)
SHARED = shaped(24, 128)
ELEMENT_ROWS = shaped(DOFS, ELEM)


def rows(count):
    return pltpu.VMEM((count, ELEM), F32)


def local(
    start_field, element_loads, element_coefs, element_nodes, move_list, face_nodes, stiffness
):
    integers = functools.partial(shaped, dtype=jnp.int32)
    far, near, other, places, field = call(
        pack_kernel,
        "pack",
        (shaped(DEVICES, 256), shaped(40, 256), shaped(40, 256), integers(8, 128), STATE),
    )(element_loads, element_coefs, move_list, face_nodes, start_field)
    field_message = near
    near, other = exchange(near, other)
    far = lax.all_to_all(far, AXES, split_axis=0, concat_axis=0, tiled=True)
    nodes, shared_index, unshared, hot, high, low, gathered = call(
        index_kernel,
        "index",
        (
            integers(PER, ELEM),
            integers(PER, ELEM),
            shaped(32, 256),
            shaped(PER * ELEM, 256, dtype=BF16),
            shaped(2 * DOFS, DOFS, dtype=BF16),
            shaped(2 * DOFS, DOFS, dtype=BF16),
            ELEMENT_ROWS,
        ),
        [rows(32), rows(PER)],
        16,
    )(field, places, element_nodes, stiffness)
    moved_loads, moved_coefs, partial, diagonal, shared_field, message = call(
        place_kernel,
        "place",
        (ELEMENT_ROWS, shaped(2, ELEM), STATE, STATE, SHARED, shaped(48, 128)),
        [rows(DOFS), rows(2 * DOFS), rows(2 * DOFS), rows(2 * DOFS), rows(384)],
        20,
    )(
        element_loads, element_coefs, move_list, far, near, other, field_message, stiffness,
        gathered, nodes, shared_index, places, hot, high, low,
    )
    near, other = exchange(message, message)
    plan = steps()
    fixed = (shared_index, nodes, moved_coefs, places, hot, high, low)
    scratch = [rows(DOFS)] * 3 + [rows(192)]
    residual = partial
    inverse, update, field, gathered = call(
        functools.partial(begin_unshared, plan[0]),
        "begin_unshared",
        (STATE, STATE, STATE, ELEMENT_ROWS),
    )(partial, diagonal, unshared, field, nodes)
    shared_residual, shared_inverse, shared_update, shared_field, partial, message = call(
        functools.partial(begin_shared, plan[0]),
        "begin_shared",
        (SHARED, SHARED, SHARED, SHARED, STATE, SHARED),
        scratch,
        16,
    )(message, near, other, shared_field, gathered, *fixed)
    for step in plan[1:-1]:
        near, other = exchange(message, message)
        residual, update, field, gathered = call(
            functools.partial(step_unshared, step),
            "unshared",
            (STATE, STATE, STATE, ELEMENT_ROWS),
        )(partial, residual, inverse, update, field, nodes)
        shared_residual, shared_update, shared_field, partial, message = call(
            functools.partial(step_shared, step),
            "shared",
            (SHARED, SHARED, SHARED, STATE, SHARED),
            scratch,
            16,
        )(
            message, near, other, shared_residual, shared_inverse, shared_update, shared_field,
            gathered, *fixed,
        )
    near, other = exchange(message, message)
    field = call(functools.partial(last_unshared, plan[-1]), "last_unshared", STATE)(
        partial, residual, inverse, update, field
    )
    field = call(functools.partial(last_shared, plan[-1]), "last_shared", shaped(3, OWN))(
        message, near, other, shared_residual, shared_inverse, shared_update, shared_field, field,
        unshared, places,
    )
    return field, moved_loads, moved_coefs


def solution(mesh):
    split_columns = P(None, AXES)
    return jax.shard_map(
        local,
        mesh=mesh,
        in_specs=(split_columns,) * 6 + (P(),),
        out_specs=(split_columns,) * 3,
        check_vma=False,
    )
```

time: 1890 us -> 149 us (0.08)
  other arithmetic: 912 us -> 0 us
  local copies, waits for them, and re-layouts: 751 us -> 17.1 us
  starting transfers between devices: 148 us -> 50.9 us
  Pallas kernels: 0 us -> 61.3 us
  waiting for transfers between devices: 53.9 us -> 18.2 us
    scatter-add x27 -> x0, other arithmetic: 901 us -> none  [the longest x9 807 us: assemble(): partial_sums = jnp.zeros((channels, owned_count + 2 * face_count), jnp.fl...]
    gather x47 -> x0, local copies, waits for them, and re-layouts: 544 us -> none  [the longest x16 495 us: operate(): gathered = extend_field(field)[:, flat_nodes].reshape(dof_count, slot_count)]
    ppermute x34 -> x18, starting transfers between devices: 127 us -> 40.4 us  [the longest x9 39.6 us: exchange(): other = lax.ppermute(other_message, AXES, OTHER_PAIRS)]
    pallas_call x0 -> x19, Pallas kernels: none -> 61.3 us  [the longest x6 20.5 us: local(): call(functools.partial(step_unshared, step), 'unshared', (STATE, STATE, S...]
    slice x21 -> x0, local copies, waits for them, and re-layouts: 52.6 us -> none  [the longest x9 35.9 us: assemble(): partial_sums[:, :owned_count].at[:, ahead_list].add(from_after)]
    reshape x26 -> x0, local copies, waits for them, and re-layouts: 48.1 us -> none  [the longest x18 46.9 us: assemble(): values.reshape(channels, -1)]
    ppermute x34 -> x18, waiting for transfers between devices: 49.2 us -> 18.2 us  [the longest x9 18.2 us: exchange(): other = lax.ppermute(other_message, AXES, OTHER_PAIRS)]
    scatter x5 -> x0, local copies, waits for them, and re-layouts: 21.3 us -> none  [the longest x1 9.16 us: local(): records[0].at[:, where_to].set(received[0], mode='drop')]
  transfers between devices with their start and end apart: 37 -> 19, of which waited for: 8 -> 8; matrix products, arithmetic and copies ran while one was open for 16% -> 0% of each run, Pallas kernels for 0% -> 22%
where the time goes in v2:
time: 149 us
  Pallas kernels  61.3 us (41%)
  starting transfers between devices  50.9 us (34%)
  waiting for transfers between devices  18.2 us (12%)
  local copies, waits for them, and re-layouts  17.1 us (11%)
    ppermute x9, starting transfers between devices, exchange(): other = lax.ppermute(other_message, AXES, OTHER_PAIRS)  39.6 us
    pallas_call x6, Pallas kernels, local(): call(functools.partial(step_unshared, step), 'unshared', (STATE, STATE, S...  20.5 us
    pallas_call x6, Pallas kernels, local(): call(functools.partial(step_shared, step), 'shared', (SHARED, SHARED, SHA...  19.2 us
    ppermute x9, waiting for transfers between devices, exchange(): other = lax.ppermute(other_message, AXES, OTHER_PAIRS)  18.2 us
    unnamed x33, local copies, waits for them, and re-layouts  16.3 us
    all_to_all x1, starting transfers between devices, local(): far = lax.all_to_all(far, AXES, split_axis=0, concat_axis=0, tiled=True)  10.5 us
    pallas_call x1, Pallas kernels, local(): call(index_kernel, 'index', (integers(PER, ELEM), integers(PER, ELEM), sh...  8.19 us
    pallas_call x1, Pallas kernels, local(): call(place_kernel, 'place', (ELEMENT_ROWS, shaped(2, ELEM), STATE, STATE,...  5.32 us
  transfers between devices with their start and end apart: 19, of which 8 were waited for; matrix products, arithmetic and copies ran while one was open for 0% of the time, Pallas kernels for 22%

profile of v2, /device:TPU:6, one launch (start us, length us, event | category | flops | bytes accessed | tf_op | source)
XLA Modules:
  0.0 148.5 jit_solution(12276635464522838885)
XLA Ops:
  5.7 10.5 %all-to-all-start = ((f32[128,1,256]{2,1,0:T(1,128)}), f32[128,1,256]{2,1,0:T(1,128)S(1)}, u32[]{:S(2)}, u32[]{:S(2)}) async-start(f32[128,1,256]{2,1,0:T(1,128)} %copy.10), calls=%async_computation | async-start | bytes 262144 | tf_op jit(solution)/shard_map/all_to_all | solution.py:553
  16.3 7.9 %collective-permute-start.1 = (f32[40,256]{1,0:T(8,128)S(1)}, f32[40,256]{1,0:T(8,128)S(1)}, u32[]{:S(2)}, u32[]{:S(2)}) collective-permute-start(f32[40,256]{1,0:T(8,128)S(1)} %get-tuple-element.87), channel_id=1, source_target_pairs={{1,2},{2,1},{3,4},{4,3},{5,6},{6,5},{7,8},{8,7},{9,10},{10,9},{11,... | collective-permute-start | bytes 122888 | tf_op jit(solution)/shard_map/ppermute | solution.py:518
  26.1 8.2 %index.1 = (s32[64,256]{1,0:T(8,128)S(1)}, s32[64,256]{1,0:T(8,128)S(1)}, f32[32,256]{1,0:T(8,128)S(1)}, bf16[16384,256]{1,0:T(8,128)(2,1)S(1)}, bf16[384,192]{1...) custom-call(f32[96,256]{1,0:T(8,128)S(1)} %get-tuple-element.88.state_ref.field_ref, ...), custom_call_target="tpu_custom_call" | custom-call | tf_op jit(solution)/shard_map/index/pallas_call | solution.py:554
  34.3 3.3 %copy-done = bf16[16384,256]{1,0:T(8,128)(2,1)} copy-done((bf16[16384,256]{1,0:T(8,128)(2,1)}, bf16[16384,256]{1,0:T(8,128)(2,1)S(1)}, u32[]{:S(2)}) %copy-start) | copy-done | bytes 8388632
  37.6 3.4 %copy-done.1 = bf16[16384,256]{1,0:T(8,128)(2,1)S(1)} copy-done((bf16[16384,256]{1,0:T(8,128)(2,1)S(1)}, bf16[16384,256]{1,0:T(8,128)(2,1)}, u32[]{:S(2)}) %copy-start.1) | copy-done | bytes 8388632
  44.3 5.3 %place.1 = (f32[192,256]{1,0:T(8,128)}, f32[2,256]{1,0:T(2,128)}, f32[96,256]{1,0:T(8,128)S(1)}, f32[96,256]{1,0:T(8,128)S(1)}, f32[24,128]{1,0:T(8,128)S(1)}, /*index=5*/f32[48,128]{1,0:T(8,128)S(1)}) custom-call(f32[192,256]{1,0:T(8,128)S(1)} %copy-done.6, f32[2,256]{1,0:T(2,128)S(1)} %copy-done.14, s32[3,256]{1,0:T(4,128)S(1)} %copy-done.12, ...), custom_call_target="tpu_custom_call" | custom-call | tf_op jit(solution)/shard_map/place/pallas_call | solution.py:569
  49.6 2.6 %collective-permute-start.3 = (f32[48,128]{1,0:T(8,128)S(1)}, f32[48,128]{1,0:T(8,128)S(1)}, u32[]{:S(2)}, u32[]{:S(2)}) collective-permute-start(f32[48,128]{1,0:T(8,128)S(1)} %get-tuple-element.96.message_in), channel_id=1, source_target_pairs={{1,2},{2,1},{3,4},{4,3},{5,6},{6,5},{7,8},{8,7},{9,10},{10,9},{11,... | collective-permute-start | bytes 73736 | tf_op jit(solution)/shard_map/ppermute | solution.py:518
  52.2 3.4 %begin_unshared.1 = (f32[96,256]{1,0:T(8,128)S(1)}, f32[96,256]{1,0:T(8,128)S(1)}, f32[96,256]{1,0:T(8,128)S(1)}, f32[192,256]{1,0:T(8,128)S(1)}) custom-call(f32[96,256]{1,0:T(8,128)S(1)} %get-tuple-element.98.partial_ref.residual_ref, f32[96,256]{1,0:T(8,128)S(1)} %get-tuple-element.99.diagonal_ref, f32[32,256]{1,0:T(8,128)S(1)} %get-tuple-element.100.unshared_ref, ...), custom_call_target="tpu_custom_call" | custom-call | tf_op jit(solution)/shard_map/begin_unshared/pallas_call | solution.py:584
  55.6 3.4 %collective-permute-done.3.other_in = f32[48,128]{1,0:T(8,128)S(1)} collective-permute-done((f32[48,128]{1,0:T(8,128)S(1)}, f32[48,128]{1,0:T(8,128)S(1)}, u32[]{:S(2)}, u32[]{:S(2)}) %collective-permute-start.3) | collective-permute-done | bytes 24608 | tf_op jit(solution)/shard_map/ppermute | solution.py:518
  59.8 3.2 %begin_shared.1 = (f32[24,128]{1,0:T(8,128)S(1)}, f32[24,128]{1,0:T(8,128)S(1)}, f32[24,128]{1,0:T(8,128)S(1)}, f32[24,128]{1,0:T(8,128)S(1)}, f32[96,256]{1,0:T(8,128)S(1)}, /*index=5*/f32[24,128]{1,0:T(8,128)S(1)}) custom-call(f32[48,128]{1,0:T(8,128)S(1)} %get-tuple-element.96.message_in, f32[48,128]{1,0:T(8,128)S(1)} %collective-permute-done.2.near_in, ...), custom_call_target="tpu_custom_call" | custom-call | tf_op jit(solution)/shard_map/begin_shared/pallas_call | solution.py:589
  63.1 4.1 %collective-permute-start.5 = (f32[24,128]{1,0:T(8,128)S(1)}, f32[24,128]{1,0:T(8,128)S(1)}, u32[]{:S(2)}, u32[]{:S(2)}) collective-permute-start(f32[24,128]{1,0:T(8,128)S(1)} %get-tuple-element.103.message_in), channel_id=1, source_target_pairs={{1,2},{2,1},{3,4},{4,3},{5,6},{6,5},{7,8},{8,7},{9,10},{10,9},{11,... | collective-permute-start | bytes 36872 | tf_op jit(solution)/shard_map/ppermute | solution.py:518
  67.1 3.4 %unshared.6 = (f32[96,256]{1,0:T(8,128)S(1)}, f32[96,256]{1,0:T(8,128)S(1)}, f32[96,256]{1,0:T(8,128)S(1)}, f32[192,256]{1,0:T(8,128)S(1)}) custom-call(f32[96,256]{1,0:T(8,128)S(1)} %get-tuple-element.108.partial_ref, f32[96,256]{1,0:T(8,128)S(1)} %get-tuple-element.98.partial_ref.residual_ref, f32[96,256]{1,0:T(8,128)S(1)} %get-tuple-element.109.inverse_ref, ...), custom_call_target="tpu_custom_call" | custom-call | tf_op jit(solution)/shard_map/unshared/pallas_call | solution.py:598
  70.6 1.7 %collective-permute-done.5.other_in = f32[24,128]{1,0:T(8,128)S(1)} collective-permute-done((f32[24,128]{1,0:T(8,128)S(1)}, f32[24,128]{1,0:T(8,128)S(1)}, u32[]{:S(2)}, u32[]{:S(2)}) %collective-permute-start.5) | collective-permute-done | bytes 12320 | tf_op jit(solution)/shard_map/ppermute | solution.py:518
  72.3 3.2 %shared.6 = (f32[24,128]{1,0:T(8,128)S(1)}, f32[24,128]{1,0:T(8,128)S(1)}, f32[24,128]{1,0:T(8,128)S(1)}, f32[96,256]{1,0:T(8,128)S(1)}, f32[24,128]{1,0:T(8,128)S(1)}) custom-call(f32[24,128]{1,0:T(8,128)S(1)} %get-tuple-element.103.message_in, f32[24,128]{1,0:T(8,128)S(1)} %collective-permute-done.4.near_in, ...), custom_call_target="tpu_custom_call" | custom-call | tf_op jit(solution)/shard_map/shared/pallas_call | solution.py:603
  75.6 4.2 %collective-permute-start.7 = (f32[24,128]{1,0:T(8,128)S(1)}, f32[24,128]{1,0:T(8,128)S(1)}, u32[]{:S(2)}, u32[]{:S(2)}) collective-permute-start(f32[24,128]{1,0:T(8,128)S(1)} %get-tuple-element.113.message_in), channel_id=1, source_target_pairs={{1,2},{2,1},{3,4},{4,3},{5,6},{6,5},{7,8},{8,7},{9,10},{10,9},{11,... | collective-permute-start | bytes 36872 | tf_op jit(solution)/shard_map/ppermute | solution.py:518
  79.8 3.4 %unshared.7 = (f32[96,256]{1,0:T(8,128)S(1)}, f32[96,256]{1,0:T(8,128)S(1)}, f32[96,256]{1,0:T(8,128)S(1)}, f32[192,256]{1,0:T(8,128)S(1)}) custom-call(f32[96,256]{1,0:T(8,128)S(1)} %get-tuple-element.117.partial_ref, f32[96,256]{1,0:T(8,128)S(1)} %get-tuple-element.118.residual_ref, f32[96,256]{1,0:T(8,128)S(1)} %get-tuple-element.109.inverse_ref, ...), custom_call_target="tpu_custom_call" | custom-call | tf_op jit(solution)/shard_map/unshared/pallas_call | solution.py:598
  84.9 3.2 %shared.7 = (f32[24,128]{1,0:T(8,128)S(1)}, f32[24,128]{1,0:T(8,128)S(1)}, f32[24,128]{1,0:T(8,128)S(1)}, f32[96,256]{1,0:T(8,128)S(1)}, f32[24,128]{1,0:T(8,128)S(1)}) custom-call(f32[24,128]{1,0:T(8,128)S(1)} %get-tuple-element.113.message_in, f32[24,128]{1,0:T(8,128)S(1)} %collective-permute-done.6.near_in, ...), custom_call_target="tpu_custom_call" | custom-call | tf_op jit(solution)/shard_map/shared/pallas_call | solution.py:603
  88.2 4.2 %collective-permute-start.9 = (f32[24,128]{1,0:T(8,128)S(1)}, f32[24,128]{1,0:T(8,128)S(1)}, u32[]{:S(2)}, u32[]{:S(2)}) collective-permute-start(f32[24,128]{1,0:T(8,128)S(1)} %get-tuple-element.122.message_in), channel_id=1, source_target_pairs={{1,2},{2,1},{3,4},{4,3},{5,6},{6,5},{7,8},{8,7},{9,10},{10,9},{11,... | collective-permute-start | bytes 36872 | tf_op jit(solution)/shard_map/ppermute | solution.py:518
  92.4 3.4 %unshared.8 = (f32[96,256]{1,0:T(8,128)S(1)}, f32[96,256]{1,0:T(8,128)S(1)}, f32[96,256]{1,0:T(8,128)S(1)}, f32[192,256]{1,0:T(8,128)S(1)}) custom-call(f32[96,256]{1,0:T(8,128)S(1)} %get-tuple-element.126.partial_ref, f32[96,256]{1,0:T(8,128)S(1)} %get-tuple-element.127.residual_ref, f32[96,256]{1,0:T(8,128)S(1)} %get-tuple-element.109.inverse_ref, ...), custom_call_target="tpu_custom_call" | custom-call | tf_op jit(solution)/shard_map/unshared/pallas_call | solution.py:598
  97.4 3.2 %shared.8 = (f32[24,128]{1,0:T(8,128)S(1)}, f32[24,128]{1,0:T(8,128)S(1)}, f32[24,128]{1,0:T(8,128)S(1)}, f32[96,256]{1,0:T(8,128)S(1)}, f32[24,128]{1,0:T(8,128)S(1)}) custom-call(f32[24,128]{1,0:T(8,128)S(1)} %get-tuple-element.122.message_in, f32[24,128]{1,0:T(8,128)S(1)} %collective-permute-done.8.near_in, ...), custom_call_target="tpu_custom_call" | custom-call | tf_op jit(solution)/shard_map/shared/pallas_call | solution.py:603
  100.7 4.2 %collective-permute-start.11 = (f32[24,128]{1,0:T(8,128)S(1)}, f32[24,128]{1,0:T(8,128)S(1)}, u32[]{:S(2)}, u32[]{:S(2)}) collective-permute-start(f32[24,128]{1,0:T(8,128)S(1)} %get-tuple-element.131.message_in), channel_id=1, source_target_pairs={{1,2},{2,1},{3,4},{4,3},{5,6},{6,5},{7,8},{8,7},{9,10},{10,9},{11,... | collective-permute-start | bytes 36872 | tf_op jit(solution)/shard_map/ppermute | solution.py:518
  104.9 3.4 %unshared.9 = (f32[96,256]{1,0:T(8,128)S(1)}, f32[96,256]{1,0:T(8,128)S(1)}, f32[96,256]{1,0:T(8,128)S(1)}, f32[192,256]{1,0:T(8,128)S(1)}) custom-call(f32[96,256]{1,0:T(8,128)S(1)} %get-tuple-element.135.partial_ref, f32[96,256]{1,0:T(8,128)S(1)} %get-tuple-element.136.residual_ref, f32[96,256]{1,0:T(8,128)S(1)} %get-tuple-element.109.inverse_ref, ...), custom_call_target="tpu_custom_call" | custom-call | tf_op jit(solution)/shard_map/unshared/pallas_call | solution.py:598
  108.3 1.6 %collective-permute-done.11.other_in = f32[24,128]{1,0:T(8,128)S(1)} collective-permute-done((f32[24,128]{1,0:T(8,128)S(1)}, f32[24,128]{1,0:T(8,128)S(1)}, u32[]{:S(2)}, u32[]{:S(2)}) %collective-permute-start.11) | collective-permute-done | bytes 12320 | tf_op jit(solution)/shard_map/ppermute | solution.py:518
  109.9 3.2 %shared.9 = (f32[24,128]{1,0:T(8,128)S(1)}, f32[24,128]{1,0:T(8,128)S(1)}, f32[24,128]{1,0:T(8,128)S(1)}, f32[96,256]{1,0:T(8,128)S(1)}, f32[24,128]{1,0:T(8,128)S(1)}) custom-call(f32[24,128]{1,0:T(8,128)S(1)} %get-tuple-element.131.message_in, f32[24,128]{1,0:T(8,128)S(1)} %collective-permute-done.10.near_in, ...), custom_call_target="tpu_custom_call" | custom-call | tf_op jit(solution)/shard_map/shared/pallas_call | solution.py:603
  113.2 4.2 %collective-permute-start.13 = (f32[24,128]{1,0:T(8,128)S(1)}, f32[24,128]{1,0:T(8,128)S(1)}, u32[]{:S(2)}, u32[]{:S(2)}) collective-permute-start(f32[24,128]{1,0:T(8,128)S(1)} %get-tuple-element.140.message_in), channel_id=1, source_target_pairs={{1,2},{2,1},{3,4},{4,3},{5,6},{6,5},{7,8},{8,7},{9,10},{10,9},{11,... | collective-permute-start | bytes 36872 | tf_op jit(solution)/shard_map/ppermute | solution.py:518
  117.4 3.4 %unshared.10 = (f32[96,256]{1,0:T(8,128)S(1)}, f32[96,256]{1,0:T(8,128)S(1)}, f32[96,256]{1,0:T(8,128)S(1)}, f32[192,256]{1,0:T(8,128)S(1)}) custom-call(f32[96,256]{1,0:T(8,128)S(1)} %get-tuple-element.144.partial_ref, f32[96,256]{1,0:T(8,128)S(1)} %get-tuple-element.145.residual_ref, f32[96,256]{1,0:T(8,128)S(1)} %get-tuple-element.109.inverse_ref, ...), custom_call_target="tpu_custom_call" | custom-call | tf_op jit(solution)/shard_map/unshared/pallas_call | solution.py:598
  122.5 3.2 %shared.10 = (f32[24,128]{1,0:T(8,128)S(1)}, f32[24,128]{1,0:T(8,128)S(1)}, f32[24,128]{1,0:T(8,128)S(1)}, f32[96,256]{1,0:T(8,128)S(1)}, f32[24,128]{1,0:T(8,128)S(1)}) custom-call(f32[24,128]{1,0:T(8,128)S(1)} %get-tuple-element.140.message_in, f32[24,128]{1,0:T(8,128)S(1)} %collective-permute-done.12.near_in, ...), custom_call_target="tpu_custom_call" | custom-call | tf_op jit(solution)/shard_map/shared/pallas_call | solution.py:603
  125.8 4.2 %collective-permute-start.15 = (f32[24,128]{1,0:T(8,128)S(1)}, f32[24,128]{1,0:T(8,128)S(1)}, u32[]{:S(2)}, u32[]{:S(2)}) collective-permute-start(f32[24,128]{1,0:T(8,128)S(1)} %get-tuple-element.149.message_in), channel_id=1, source_target_pairs={{1,2},{2,1},{3,4},{4,3},{5,6},{6,5},{7,8},{8,7},{9,10},{10,9},{11,... | collective-permute-start | bytes 36872 | tf_op jit(solution)/shard_map/ppermute | solution.py:518
  130.0 3.4 %unshared.11 = (f32[96,256]{1,0:T(8,128)S(1)}, f32[96,256]{1,0:T(8,128)S(1)}, f32[96,256]{1,0:T(8,128)S(1)}, f32[192,256]{1,0:T(8,128)S(1)}) custom-call(f32[96,256]{1,0:T(8,128)S(1)} %get-tuple-element.153.partial_ref, f32[96,256]{1,0:T(8,128)S(1)} %get-tuple-element.154.residual_ref, f32[96,256]{1,0:T(8,128)S(1)} %get-tuple-element.109.inverse_ref, ...), custom_call_target="tpu_custom_call" | custom-call | tf_op jit(solution)/shard_map/unshared/pallas_call | solution.py:598
  135.0 3.2 %shared.11 = (f32[24,128]{1,0:T(8,128)S(1)}, f32[24,128]{1,0:T(8,128)S(1)}, f32[24,128]{1,0:T(8,128)S(1)}, f32[96,256]{1,0:T(8,128)S(1)}, f32[24,128]{1,0:T(8,128)S(1)}) custom-call(f32[24,128]{1,0:T(8,128)S(1)} %get-tuple-element.149.message_in, f32[24,128]{1,0:T(8,128)S(1)} %collective-permute-done.14.near_in, ...), custom_call_target="tpu_custom_call" | custom-call | tf_op jit(solution)/shard_map/shared/pallas_call | solution.py:603
  138.3 4.2 %collective-permute-start.17 = (f32[24,128]{1,0:T(8,128)S(1)}, f32[24,128]{1,0:T(8,128)S(1)}, u32[]{:S(2)}, u32[]{:S(2)}) collective-permute-start(f32[24,128]{1,0:T(8,128)S(1)} %get-tuple-element.158.message_in), channel_id=1, source_target_pairs={{1,2},{2,1},{3,4},{4,3},{5,6},{6,5},{7,8},{8,7},{9,10},{10,9},{11,... | collective-permute-start | bytes 36872 | tf_op jit(solution)/shard_map/ppermute | solution.py:518
  142.6 5.0 %collective-permute-done.17.other_in = f32[24,128]{1,0:T(8,128)S(1)} collective-permute-done((f32[24,128]{1,0:T(8,128)S(1)}, f32[24,128]{1,0:T(8,128)S(1)}, u32[]{:S(2)}, u32[]{:S(2)}) %collective-permute-start.17) | collective-permute-done | bytes 12320 | tf_op jit(solution)/shard_map/ppermute | solution.py:518
  (59 shorter events, 19.1 us)
Async XLA Ops:
  0.6 0.9 copy-start.5
  1.6 0.9 copy-start.7
  2.5 0.7 copy-start.11
  5.7 31.9 %all-to-all-start = ((f32[128,1,256]{2,1,0:T(1,128)}), f32[128,1,256]{2,1,0:T(1,128)S(1)}, u32[]{:S(2)}, u32[]{:S(2)}) async-start(f32[128,1,256]{2,1,0:T(1,128)} %copy.10), calls=%async_computation | async-start | bytes 262144 | tf_op jit(solution)/shard_map/all_to_all | solution.py:553
  16.2 21.4 %collective-permute-start = (f32[40,256]{1,0:T(8,128)S(1)}, f32[40,256]{1,0:T(8,128)S(1)}, u32[]{:S(2)}, u32[]{:S(2)}) collective-permute-start(f32[40,256]{1,0:T(8,128)S(1)} %get-tuple-element.86.field_message), channel_id=1, source_target_pairs={{0,1},{1,0},{2,3},{3,2},{4,5},{5,4},{6,7},{7,6},{8,9},{9,8},{10,11... | collective-permute-start | bytes 122888 | tf_op jit(solution)/shard_map/ppermute | solution.py:519
  16.3 21.2 %collective-permute-start.1 = (f32[40,256]{1,0:T(8,128)S(1)}, f32[40,256]{1,0:T(8,128)S(1)}, u32[]{:S(2)}, u32[]{:S(2)}) collective-permute-start(f32[40,256]{1,0:T(8,128)S(1)} %get-tuple-element.87), channel_id=1, source_target_pairs={{1,2},{2,1},{3,4},{4,3},{5,6},{6,5},{7,8},{8,7},{9,10},{10,9},{11,... | collective-permute-start | bytes 122888 | tf_op jit(solution)/shard_map/ppermute | solution.py:518
  24.2 1.0 copy-start.3
  25.2 0.8 copy-start.10
  34.3 3.3 %copy-start = (bf16[16384,256]{1,0:T(8,128)(2,1)}, bf16[16384,256]{1,0:T(8,128)(2,1)S(1)}, u32[]{:S(2)}) copy-start(bf16[16384,256]{1,0:T(8,128)(2,1)S(1)} %get-tuple-element.93.hot_ref) | copy-start | bytes 25165828
  37.6 3.4 %copy-start.1 = (bf16[16384,256]{1,0:T(8,128)(2,1)S(1)}, bf16[16384,256]{1,0:T(8,128)(2,1)}, u32[]{:S(2)}) copy-start(bf16[16384,256]{1,0:T(8,128)(2,1)} %copy-done) | copy-start | bytes 25165828
  41.0 1.0 copy-start.4
  42.0 0.9 copy-start.6
  42.9 0.7 copy-start.12
  44.3 14.8 %copy-start.2 = (bf16[16384,256]{1,0:T(8,128)(2,1)S(1)}, bf16[16384,256]{1,0:T(8,128)(2,1)}, u32[]{:S(2)}) copy-start(bf16[16384,256]{1,0:T(8,128)(2,1)} %copy-done) | copy-start | bytes 25165828
  49.6 22.7 %copy-start.9 = (f32[2,256]{1,0:T(2,128)S(1)}, f32[2,256]{1,0:T(2,128)}, u32[]{:S(2)}) copy-start(f32[2,256]{1,0:T(2,128)} %get-tuple-element.84.coefs_ref) | copy-start | bytes 6148
  49.6 6.0 %collective-permute-start.2 = (f32[48,128]{1,0:T(8,128)S(1)}, f32[48,128]{1,0:T(8,128)S(1)}, u32[]{:S(2)}, u32[]{:S(2)}) collective-permute-start(f32[48,128]{1,0:T(8,128)S(1)} %get-tuple-element.96.message_in), channel_id=1, source_target_pairs={{0,1},{1,0},{2,3},{3,2},{4,5},{5,4},{6,7},{7,6},{8,9},{9,8},{10,11... | collective-permute-start | bytes 73736 | tf_op jit(solution)/shard_map/ppermute | solution.py:519
  49.6 9.5 %collective-permute-start.3 = (f32[48,128]{1,0:T(8,128)S(1)}, f32[48,128]{1,0:T(8,128)S(1)}, u32[]{:S(2)}, u32[]{:S(2)}) collective-permute-start(f32[48,128]{1,0:T(8,128)S(1)} %get-tuple-element.96.message_in), channel_id=1, source_target_pairs={{1,2},{2,1},{3,4},{4,3},{5,6},{6,5},{7,8},{8,7},{9,10},{10,9},{11,... | collective-permute-start | bytes 73736 | tf_op jit(solution)/shard_map/ppermute | solution.py:518
  59.1 0.7 copy-start.8
  63.0 7.6 %collective-permute-start.4 = (f32[24,128]{1,0:T(8,128)S(1)}, f32[24,128]{1,0:T(8,128)S(1)}, u32[]{:S(2)}, u32[]{:S(2)}) collective-permute-start(f32[24,128]{1,0:T(8,128)S(1)} %get-tuple-element.103.message_in), channel_id=1, source_target_pairs={{0,1},{1,0},{2,3},{3,2},{4,5},{5,4},{6,7},{7,6},{8,9},{9,8},{10,11... | collective-permute-start | bytes 36872 | tf_op jit(solution)/shard_map/ppermute | solution.py:519
  63.1 9.2 %collective-permute-start.5 = (f32[24,128]{1,0:T(8,128)S(1)}, f32[24,128]{1,0:T(8,128)S(1)}, u32[]{:S(2)}, u32[]{:S(2)}) collective-permute-start(f32[24,128]{1,0:T(8,128)S(1)} %get-tuple-element.103.message_in), channel_id=1, source_target_pairs={{1,2},{2,1},{3,4},{4,3},{5,6},{6,5},{7,8},{8,7},{9,10},{10,9},{11,... | collective-permute-start | bytes 36872 | tf_op jit(solution)/shard_map/ppermute | solution.py:518
  75.5 7.7 %collective-permute-start.6 = (f32[24,128]{1,0:T(8,128)S(1)}, f32[24,128]{1,0:T(8,128)S(1)}, u32[]{:S(2)}, u32[]{:S(2)}) collective-permute-start(f32[24,128]{1,0:T(8,128)S(1)} %get-tuple-element.113.message_in), channel_id=1, source_target_pairs={{0,1},{1,0},{2,3},{3,2},{4,5},{5,4},{6,7},{7,6},{8,9},{9,8},{10,11... | collective-permute-start | bytes 36872 | tf_op jit(solution)/shard_map/ppermute | solution.py:519
  75.6 9.2 %collective-permute-start.7 = (f32[24,128]{1,0:T(8,128)S(1)}, f32[24,128]{1,0:T(8,128)S(1)}, u32[]{:S(2)}, u32[]{:S(2)}) collective-permute-start(f32[24,128]{1,0:T(8,128)S(1)} %get-tuple-element.113.message_in), channel_id=1, source_target_pairs={{1,2},{2,1},{3,4},{4,3},{5,6},{6,5},{7,8},{8,7},{9,10},{10,9},{11,... | collective-permute-start | bytes 36872 | tf_op jit(solution)/shard_map/ppermute | solution.py:518
  88.1 7.7 %collective-permute-start.8 = (f32[24,128]{1,0:T(8,128)S(1)}, f32[24,128]{1,0:T(8,128)S(1)}, u32[]{:S(2)}, u32[]{:S(2)}) collective-permute-start(f32[24,128]{1,0:T(8,128)S(1)} %get-tuple-element.122.message_in), channel_id=1, source_target_pairs={{0,1},{1,0},{2,3},{3,2},{4,5},{5,4},{6,7},{7,6},{8,9},{9,8},{10,11... | collective-permute-start | bytes 36872 | tf_op jit(solution)/shard_map/ppermute | solution.py:519
  88.2 9.2 %collective-permute-start.9 = (f32[24,128]{1,0:T(8,128)S(1)}, f32[24,128]{1,0:T(8,128)S(1)}, u32[]{:S(2)}, u32[]{:S(2)}) collective-permute-start(f32[24,128]{1,0:T(8,128)S(1)} %get-tuple-element.122.message_in), channel_id=1, source_target_pairs={{1,2},{2,1},{3,4},{4,3},{5,6},{6,5},{7,8},{8,7},{9,10},{10,9},{11,... | collective-permute-start | bytes 36872 | tf_op jit(solution)/shard_map/ppermute | solution.py:518
  100.6 7.7 %collective-permute-start.10 = (f32[24,128]{1,0:T(8,128)S(1)}, f32[24,128]{1,0:T(8,128)S(1)}, u32[]{:S(2)}, u32[]{:S(2)}) collective-permute-start(f32[24,128]{1,0:T(8,128)S(1)} %get-tuple-element.131.message_in), channel_id=1, source_target_pairs={{0,1},{1,0},{2,3},{3,2},{4,5},{5,4},{6,7},{7,6},{8,9},{9,8},{10,11... | collective-permute-start | bytes 36872 | tf_op jit(solution)/shard_map/ppermute | solution.py:519
  100.7 9.2 %collective-permute-start.11 = (f32[24,128]{1,0:T(8,128)S(1)}, f32[24,128]{1,0:T(8,128)S(1)}, u32[]{:S(2)}, u32[]{:S(2)}) collective-permute-start(f32[24,128]{1,0:T(8,128)S(1)} %get-tuple-element.131.message_in), channel_id=1, source_target_pairs={{1,2},{2,1},{3,4},{4,3},{5,6},{6,5},{7,8},{8,7},{9,10},{10,9},{11,... | collective-permute-start | bytes 36872 | tf_op jit(solution)/shard_map/ppermute | solution.py:518
  113.1 7.7 %collective-permute-start.12 = (f32[24,128]{1,0:T(8,128)S(1)}, f32[24,128]{1,0:T(8,128)S(1)}, u32[]{:S(2)}, u32[]{:S(2)}) collective-permute-start(f32[24,128]{1,0:T(8,128)S(1)} %get-tuple-element.140.message_in), channel_id=1, source_target_pairs={{0,1},{1,0},{2,3},{3,2},{4,5},{5,4},{6,7},{7,6},{8,9},{9,8},{10,11... | collective-permute-start | bytes 36872 | tf_op jit(solution)/shard_map/ppermute | solution.py:519
  113.2 9.2 %collective-permute-start.13 = (f32[24,128]{1,0:T(8,128)S(1)}, f32[24,128]{1,0:T(8,128)S(1)}, u32[]{:S(2)}, u32[]{:S(2)}) collective-permute-start(f32[24,128]{1,0:T(8,128)S(1)} %get-tuple-element.140.message_in), channel_id=1, source_target_pairs={{1,2},{2,1},{3,4},{4,3},{5,6},{6,5},{7,8},{8,7},{9,10},{10,9},{11,... | collective-permute-start | bytes 36872 | tf_op jit(solution)/shard_map/ppermute | solution.py:518
  125.7 7.7 %collective-permute-start.14 = (f32[24,128]{1,0:T(8,128)S(1)}, f32[24,128]{1,0:T(8,128)S(1)}, u32[]{:S(2)}, u32[]{:S(2)}) collective-permute-start(f32[24,128]{1,0:T(8,128)S(1)} %get-tuple-element.149.message_in), channel_id=1, source_target_pairs={{0,1},{1,0},{2,3},{3,2},{4,5},{5,4},{6,7},{7,6},{8,9},{9,8},{10,11... | collective-permute-start | bytes 36872 | tf_op jit(solution)/shard_map/ppermute | solution.py:519
  125.8 9.2 %collective-permute-start.15 = (f32[24,128]{1,0:T(8,128)S(1)}, f32[24,128]{1,0:T(8,128)S(1)}, u32[]{:S(2)}, u32[]{:S(2)}) collective-permute-start(f32[24,128]{1,0:T(8,128)S(1)} %get-tuple-element.149.message_in), channel_id=1, source_target_pairs={{1,2},{2,1},{3,4},{4,3},{5,6},{6,5},{7,8},{8,7},{9,10},{10,9},{11,... | collective-permute-start | bytes 36872 | tf_op jit(solution)/shard_map/ppermute | solution.py:518
  138.2 4.3 %collective-permute-start.16 = (f32[24,128]{1,0:T(8,128)S(1)}, f32[24,128]{1,0:T(8,128)S(1)}, u32[]{:S(2)}, u32[]{:S(2)}) collective-permute-start(f32[24,128]{1,0:T(8,128)S(1)} %get-tuple-element.158.message_in), channel_id=1, source_target_pairs={{0,1},{1,0},{2,3},{3,2},{4,5},{5,4},{6,7},{7,6},{8,9},{9,8},{10,11... | collective-permute-start | bytes 36872 | tf_op jit(solution)/shard_map/ppermute | solution.py:519
  138.3 9.2 %collective-permute-start.17 = (f32[24,128]{1,0:T(8,128)S(1)}, f32[24,128]{1,0:T(8,128)S(1)}, u32[]{:S(2)}, u32[]{:S(2)}) collective-permute-start(f32[24,128]{1,0:T(8,128)S(1)} %get-tuple-element.158.message_in), channel_id=1, source_target_pairs={{1,2},{2,1},{3,4},{4,3},{5,6},{6,5},{7,8},{8,7},{9,10},{10,9},{11,... | collective-permute-start | bytes 36872 | tf_op jit(solution)/shard_map/ppermute | solution.py:518
  (3 other events, 2.0 us)

commit v3 on v2

--- a/solution.py
+++ b/solution.py
@@ -224,8 +224,26 @@
 
 
 def pack_kernel(
-    loads_ref, coefs_ref, move_ref, face_ref, field_ref, far_ref, near_out, other_out, places_ref, state_ref
-):
+    loads_hbm, coefs_hbm, move_hbm, face_hbm, field_hbm, nodes_hbm, stiff_hbm, far_ref, near_out,
+    other_out, places_ref, state_ref, loads_ref, coefs_ref, move_ref, nodes_ref, stiff_ref,
+    face_ref, field_ref, sems,
+):
+    pairs = (
+        (move_hbm, move_ref),
+        (coefs_hbm, coefs_ref),
+        (loads_hbm, loads_ref),
+        (face_hbm, face_ref),
+        (field_hbm, field_ref),
+        (nodes_hbm, nodes_ref),
+        (stiff_hbm, stiff_ref),
+    )
+    copies = [
+        pltpu.make_async_copy(source, target, sems.at[i]) for i, (source, target) in enumerate(pairs)
+    ]
+    for copy in copies:
+        copy.start()
+    for copy in copies:
+        copy.wait()
     me = lax.axis_index(AXES)
     first_core = lax.axis_index("sub") == 0
     near = jnp.where(first_core, me + 1, me - 1)
@@ -254,7 +272,7 @@
         precision=lax.Precision.HIGHEST,
         preferred_element_type=F32,
     )
-    far_ref[...] = packed[:DEVICES]
+    far_ref[:, 0, :] = packed[:DEVICES]
     near_out[0:NEAR_CAP, :] = packed[DEVICES : DEVICES + NEAR_CAP]
     other_out[0:NEAR_CAP, :] = packed[DEVICES + NEAR_CAP :]
     near_out[NEAR_CAP:, :] = jnp.zeros((24, 256), F32)
@@ -279,7 +297,6 @@
     index_ref,
     shared_index_ref,
     unshared_ref,
-    hot_ref,
     high_ref,
     low_ref,
     gathered_ref,
@@ -304,17 +321,21 @@
         high, low = split(stiff_ref[i])
         high_ref[DOFS * i : DOFS * i + DOFS, :] = high.astype(BF16)
         low_ref[DOFS * i : DOFS * i + DOFS, :] = low.astype(BF16)
-    found[...] = (index_ref[...] & 255).astype(F32)
-    lanes = iota((16, 256), 1).astype(F32)
-
+
+
+def build_hot(nodes_ref, hot_ref):
+    low = (nodes_ref[...] & 255).astype(F32)
+    lanes = iota((16, 256), 1).astype(F32).astype(BF16)
+    one = jnp.ones((), BF16)
+    zero = jnp.zeros((), BF16)
     for half in range(2):
-        turned = found[:, half * 128 : half * 128 + 128].T
+        turned = low[:, half * 128 : half * 128 + 128].T.astype(BF16)
         for b in range(8):
             columns = turned[16 * b : 16 * b + 16]
             for n in range(PER):
-                hot_ref[256 * n + half * 128 + 16 * b : 256 * n + half * 128 + 16 * b + 16, :] = (
-                    jnp.where(columns[:, n : n + 1] == lanes, 1.0, 0.0).astype(BF16)
-                )
+                top = 256 * n + half * 128 + 16 * b
+                column = jnp.broadcast_to(columns[:, n : n + 1], (16, 256))
+                hot_ref[top : top + 16, :] = jnp.where(column == lanes, one, zero)
 
 
 def multiply_blocks(high_ref, low_ref, rows_ref):
@@ -341,11 +362,12 @@
     nodes_ref,
     shared_index_ref,
     places_ref,
-    hot_ref,
     high_ref,
     low_ref,
+    hot_ref,
     moved_loads,
     moved_coefs,
+    coefs_out,
     partial_ref,
     diagonal_ref,
     shared_field,
@@ -362,7 +384,7 @@
     products = multiply_blocks(high_ref, low_ref, gathered)
     me = lax.axis_index(AXES)
     received = jnp.concatenate(
-        [far_ref[...], near_in[0:NEAR_CAP, :], other_in[0:NEAR_CAP, :]], axis=0
+        [far_ref[:, 0, :], near_in[0:NEAR_CAP, :], other_in[0:NEAR_CAP, :]], axis=0
     )
     rows = DEVICES + 2 * NEAR_CAP
     slot = received[:, DOFS + 2 : DOFS + 3].astype(jnp.int32)
@@ -379,11 +401,13 @@
     coefs = jnp.where(stays, coefs_ref[...], 0.0) + arrived[DOFS : DOFS + 2]
     moved_loads[...] = loads
     moved_coefs[...] = coefs
+    coefs_out[...] = coefs
     values[0:DOFS, :] = loads - (products[:DOFS] * coefs[0:1, :] + products[DOFS:] * coefs[1:2, :])
     eye = iota((DOFS, DOFS), 0) == iota((DOFS, DOFS), 1)
     first_diag = jnp.sum(jnp.where(eye, stiff_ref[0], 0.0), axis=1, keepdims=True)
     second_diag = jnp.sum(jnp.where(eye, stiff_ref[1], 0.0), axis=1, keepdims=True)
     values[DOFS:, :] = first_diag * coefs[0:1, :] + second_diag * coefs[1:2, :]
+    build_hot(nodes_ref, hot_ref)
     scatter_elements(nodes_ref, hot_ref, values, value_high, value_low, sums, 6)
     partial_ref[...] = add_parts(sums, 0, 6)
     diagonal_ref[...] = add_parts(sums, 3, 6)
@@ -520,13 +544,14 @@
     return near, other
 
 
-def call(kernel, name, outs, scratch=(), limit=6):
+def call(kernel, name, outs, scratch=(), **options):
     return pl.pallas_call(
         kernel,
         out_shape=outs,
         scratch_shapes=list(scratch),
-        compiler_params=pltpu.CompilerParams(vmem_limit_bytes=limit << 20),
+        compiler_params=pltpu.CompilerParams(vmem_limit_bytes=20 << 20),
         name=name,
+        **options,
     )
 
 
@@ -543,42 +568,65 @@
     start_field, element_loads, element_coefs, element_nodes, move_list, face_nodes, stiffness
 ):
     integers = functools.partial(shaped, dtype=jnp.int32)
-    far, near, other, places, field = call(
+    far, near, other, places, field, loads, coefs, moves, nodes, stiff = call(
         pack_kernel,
         "pack",
-        (shaped(DEVICES, 256), shaped(40, 256), shaped(40, 256), integers(8, 128), STATE),
-    )(element_loads, element_coefs, move_list, face_nodes, start_field)
+        (
+            shaped(DEVICES, 1, 256),
+            shaped(40, 256),
+            shaped(40, 256),
+            integers(8, 128),
+            STATE,
+            ELEMENT_ROWS,
+            shaped(2, ELEM),
+            integers(3, ELEM),
+            integers(PER, ELEM),
+            shaped(2, DOFS, DOFS),
+        ),
+        [
+            pltpu.VMEM((2, FACE), jnp.int32),
+            pltpu.VMEM((3, OWN), F32),
+            pltpu.SemaphoreType.DMA((7,)),
+        ],
+        in_specs=[pl.BlockSpec(memory_space=pltpu.HBM)] * 7,
+    )(*[pltpu.with_memory_space_constraint(x, pltpu.HBM) for x in (element_loads, element_coefs, move_list, face_nodes, start_field, element_nodes, stiffness)])
     field_message = near
     near, other = exchange(near, other)
     far = lax.all_to_all(far, AXES, split_axis=0, concat_axis=0, tiled=True)
-    nodes, shared_index, unshared, hot, high, low, gathered = call(
+    nodes, shared_index, unshared, high, low, gathered = call(
         index_kernel,
         "index",
         (
             integers(PER, ELEM),
             integers(PER, ELEM),
             shaped(32, 256),
-            shaped(PER * ELEM, 256, dtype=BF16),
             shaped(2 * DOFS, DOFS, dtype=BF16),
             shaped(2 * DOFS, DOFS, dtype=BF16),
             ELEMENT_ROWS,
         ),
         [rows(32), rows(PER)],
-        16,
-    )(field, places, element_nodes, stiffness)
-    moved_loads, moved_coefs, partial, diagonal, shared_field, message = call(
+    )(field, places, nodes, stiff)
+    hot, moved_loads, moved_coefs, coefs, partial, diagonal, shared_field, message = call(
         place_kernel,
         "place",
-        (ELEMENT_ROWS, shaped(2, ELEM), STATE, STATE, SHARED, shaped(48, 128)),
+        (
+            shaped(PER * ELEM, 256, dtype=BF16),
+            ELEMENT_ROWS,
+            shaped(2, ELEM),
+            shaped(2, ELEM),
+            STATE,
+            STATE,
+            SHARED,
+            shaped(48, 128),
+        ),
         [rows(DOFS), rows(2 * DOFS), rows(2 * DOFS), rows(2 * DOFS), rows(384)],
-        20,
     )(
-        element_loads, element_coefs, move_list, far, near, other, field_message, stiffness,
-        gathered, nodes, shared_index, places, hot, high, low,
+        loads, coefs, moves, far, near, other, field_message, stiff,
+        gathered, nodes, shared_index, places, high, low,
     )
     near, other = exchange(message, message)
     plan = steps()
-    fixed = (shared_index, nodes, moved_coefs, places, hot, high, low)
+    fixed = (shared_index, nodes, coefs, places, hot, high, low)
     scratch = [rows(DOFS)] * 3 + [rows(192)]
     residual = partial
     inverse, update, field, gathered = call(
@@ -591,7 +639,6 @@
         "begin_shared",
         (SHARED, SHARED, SHARED, SHARED, STATE, SHARED),
         scratch,
-        16,
     )(message, near, other, shared_field, gathered, *fixed)
     for step in plan[1:-1]:
         near, other = exchange(message, message)
@@ -605,7 +652,6 @@
             "shared",
             (SHARED, SHARED, SHARED, STATE, SHARED),
             scratch,
-            16,
         )(
             message, near, other, shared_residual, shared_inverse, shared_update, shared_field,
             gathered, *fixed,

time: 149 us -> 130 us (0.87)
  local copies, waits for them, and re-layouts: 17.1 us -> 0 us
  waiting for transfers between devices: 18.2 us -> 11 us
  starting transfers between devices: 50.9 us -> 57.1 us
    unnamed x33 -> x0, local copies, waits for them, and re-layouts: 16.3 us -> none
    ppermute x9, waiting for transfers between devices: 18.2 us -> 11 us  [exchange(): other = lax.ppermute(other_message, AXES, OTHER_PAIRS)]
    ppermute x9, starting transfers between devices: 39.6 us -> 45.7 us  [exchange(): other = lax.ppermute(other_message, AXES, OTHER_PAIRS)]
    pallas_call x1, Pallas kernels: 8.19 us -> 4.64 us  [local(): call(index_kernel, 'index', (integers(PER, ELEM), integers(PER, ELEM), sh...]
    pallas_call x2, Pallas kernels: 5.68 us -> 8.98 us  [the longest x1 6.66 us: local(): call(place_kernel, 'place', (shaped(PER * ELEM, 256, dtype=BF16), ELEMENT...]
where the time goes in v3:
time: 130 us
  Pallas kernels  61 us (47%)
  starting transfers between devices  57.1 us (44%)
  waiting for transfers between devices  11 us (8%)
    ppermute x9, starting transfers between devices, exchange(): other = lax.ppermute(other_message, AXES, OTHER_PAIRS)  45.7 us
    pallas_call x6, Pallas kernels, local(): call(functools.partial(step_unshared, step), 'unshared', (STATE, STATE, S...  20.5 us
    pallas_call x6, Pallas kernels, local(): call(functools.partial(step_shared, step), 'shared', (SHARED, SHARED, SHA...  19.3 us
    ppermute x9, waiting for transfers between devices, exchange(): other = lax.ppermute(other_message, AXES, OTHER_PAIRS)  11 us
    all_to_all x1, starting transfers between devices, local(): far = lax.all_to_all(far, AXES, split_axis=0, concat_axis=0, tiled=True)  10.5 us
    pallas_call x1, Pallas kernels, local(): call(place_kernel, 'place', (shaped(PER * ELEM, 256, dtype=BF16), ELEMENT...  6.66 us
    pallas_call x1, Pallas kernels, local(): call(index_kernel, 'index', (integers(PER, ELEM), integers(PER, ELEM), sh...  4.64 us
    pallas_call x1, Pallas kernels, local(): call(functools.partial(begin_unshared, plan[0]), 'begin_unshared', (STATE...  3.42 us
  transfers between devices with their start and end apart: 19, of which 8 were waited for; matrix products, arithmetic and copies ran while one was open for 0% of the time, Pallas kernels for 22%

profile of v3, /device:TPU:6, one launch (start us, length us, event | category | flops | bytes accessed | tf_op | source)
XLA Modules:
  0.0 130.0 jit_solution(13134011145950409739)
XLA Ops:
  0.6 2.3 %pack.1 = (f32[128,1,256]{2,1,0:T(1,128)}, f32[40,256]{1,0:T(8,128)S(1)}, f32[40,256]{1,0:T(8,128)S(1)}, s32[8,128]{1,0:T(8,128)S(1)}, f32[96,256]{1,0:T(8,128)S...) custom-call(f32[192,256]{1,0:T(8,128)} %loads_hbm.1, ...), custom_call_target="tpu_custom_call" | custom-call | tf_op jit(solution)/shard_map/pack/pallas_call | solution.py:571
  3.0 10.5 %all-to-all-start = ((f32[128,1,256]{2,1,0:T(1,128)}), f32[128,1,256]{2,1,0:T(1,128)S(1)}, u32[]{:S(2)}, u32[]{:S(2)}) async-start(f32[128,1,256]{2,1,0:T(1,128)} %get-tuple-element.94), calls=%async_computation | async-start | bytes 262144 | tf_op jit(solution)/shard_map/all_to_all | solution.py:595
  13.4 7.6 %collective-permute-start.1 = (f32[40,256]{1,0:T(8,128)S(1)}, f32[40,256]{1,0:T(8,128)S(1)}, u32[]{:S(2)}, u32[]{:S(2)}) collective-permute-start(f32[40,256]{1,0:T(8,128)S(1)} %get-tuple-element.96), channel_id=1, source_target_pairs={{1,2},{2,1},{3,4},{4,3},{5,6},{6,5},{7,8},{8,7},{9,10},{10,9},{11,... | collective-permute-start | bytes 122888 | tf_op jit(solution)/shard_map/ppermute | solution.py:542
  21.2 4.6 %index.1 = (s32[64,256]{1,0:T(8,128)S(1)}, s32[64,256]{1,0:T(8,128)S(1)}, f32[32,256]{1,0:T(8,128)S(1)}, bf16[384,192]{1,0:T(8,128)(2,1)S(1)}, bf16[384,192]{1,0:T(8,128)(2,1)S(1)}, /*index=5*/f32[192,256]{1,0:T(8,128)S(1)}) custom-call(f32[96,256]{1,0:T(8,128)S(1)} %get-tuple-element.98.state_ref.field_ref, s32[8,128]{1,0:T(8,128)S(1)} %get-tuple-element.99.places_ref, ...), custom_call_target="tpu_custom_call" | custom-call | tf_op jit(solution)/shard_map/index/pallas_call | solution.py:596
  25.8 6.7 %place.1 = (bf16[16384,256]{1,0:T(8,128)(2,1)S(1)}, f32[192,256]{1,0:T(8,128)}, f32[2,256]{1,0:T(2,128)}, f32[2,256]{1,0:T(2,128)S(1)}, f32[96,256]{1,0:T(8,128)...) custom-call(f32[192,256]{1,0:T(8,128)S(1)} %get-tuple-element.91.loads_ref, ...), custom_call_target="tpu_custom_call" | custom-call | tf_op jit(solution)/shard_map/place/pallas_call | solution.py:609
  32.5 4.8 %collective-permute-start.3 = (f32[48,128]{1,0:T(8,128)S(1)}, f32[48,128]{1,0:T(8,128)S(1)}, u32[]{:S(2)}, u32[]{:S(2)}) collective-permute-start(f32[48,128]{1,0:T(8,128)S(1)} %get-tuple-element.106.message_in), channel_id=1, source_target_pairs={{1,2},{2,1},{3,4},{4,3},{5,6},{6,5},{7,8},{8,7},{9,10},{10,9},{11,... | collective-permute-start | bytes 73736 | tf_op jit(solution)/shard_map/ppermute | solution.py:542
  37.3 3.4 %begin_unshared.1 = (f32[96,256]{1,0:T(8,128)S(1)}, f32[96,256]{1,0:T(8,128)S(1)}, f32[96,256]{1,0:T(8,128)S(1)}, f32[192,256]{1,0:T(8,128)S(1)}) custom-call(f32[96,256]{1,0:T(8,128)S(1)} %get-tuple-element.108.partial_ref.residual_ref, f32[96,256]{1,0:T(8,128)S(1)} %get-tuple-element.109.diagonal_ref, f32[32,256]{1,0:T(8,128)S(1)} %get-tuple-element.110.unshared_ref, ...), custom_call_target="tpu_custom_call" | custom-call | tf_op jit(solution)/shard_map/begin_unshared/pallas_call | solution.py:632
  40.8 1.1 collective-permute-done.3.other_in
  41.8 3.2 %begin_shared.1 = (f32[24,128]{1,0:T(8,128)S(1)}, f32[24,128]{1,0:T(8,128)S(1)}, f32[24,128]{1,0:T(8,128)S(1)}, f32[24,128]{1,0:T(8,128)S(1)}, f32[96,256]{1,0:T(8,128)S(1)}, /*index=5*/f32[24,128]{1,0:T(8,128)S(1)}) custom-call(f32[48,128]{1,0:T(8,128)S(1)} %get-tuple-element.106.message_in, f32[48,128]{1,0:T(8,128)S(1)} %collective-permute-done.2.near_in, ...), custom_call_target="tpu_custom_call" | custom-call | tf_op jit(solution)/shard_map/begin_shared/pallas_call | solution.py:637
  45.1 4.8 %collective-permute-start.5 = (f32[24,128]{1,0:T(8,128)S(1)}, f32[24,128]{1,0:T(8,128)S(1)}, u32[]{:S(2)}, u32[]{:S(2)}) collective-permute-start(f32[24,128]{1,0:T(8,128)S(1)} %get-tuple-element.114.message_in), channel_id=1, source_target_pairs={{1,2},{2,1},{3,4},{4,3},{5,6},{6,5},{7,8},{8,7},{9,10},{10,9},{11,... | collective-permute-start | bytes 36872 | tf_op jit(solution)/shard_map/ppermute | solution.py:542
  49.9 3.4 %unshared.6 = (f32[96,256]{1,0:T(8,128)S(1)}, f32[96,256]{1,0:T(8,128)S(1)}, f32[96,256]{1,0:T(8,128)S(1)}, f32[192,256]{1,0:T(8,128)S(1)}) custom-call(f32[96,256]{1,0:T(8,128)S(1)} %get-tuple-element.119.partial_ref, f32[96,256]{1,0:T(8,128)S(1)} %get-tuple-element.108.partial_ref.residual_ref, f32[96,256]{1,0:T(8,128)S(1)} %get-tuple-element.120.inverse_ref, ...), custom_call_target="tpu_custom_call" | custom-call | tf_op jit(solution)/shard_map/unshared/pallas_call | solution.py:645
  54.3 3.2 %shared.6 = (f32[24,128]{1,0:T(8,128)S(1)}, f32[24,128]{1,0:T(8,128)S(1)}, f32[24,128]{1,0:T(8,128)S(1)}, f32[96,256]{1,0:T(8,128)S(1)}, f32[24,128]{1,0:T(8,128)S(1)}) custom-call(f32[24,128]{1,0:T(8,128)S(1)} %get-tuple-element.114.message_in, f32[24,128]{1,0:T(8,128)S(1)} %collective-permute-done.4.near_in, ...), custom_call_target="tpu_custom_call" | custom-call | tf_op jit(solution)/shard_map/shared/pallas_call | solution.py:650
  57.5 4.8 %collective-permute-start.7 = (f32[24,128]{1,0:T(8,128)S(1)}, f32[24,128]{1,0:T(8,128)S(1)}, u32[]{:S(2)}, u32[]{:S(2)}) collective-permute-start(f32[24,128]{1,0:T(8,128)S(1)} %get-tuple-element.124.message_in), channel_id=1, source_target_pairs={{1,2},{2,1},{3,4},{4,3},{5,6},{6,5},{7,8},{8,7},{9,10},{10,9},{11,... | collective-permute-start | bytes 36872 | tf_op jit(solution)/shard_map/ppermute | solution.py:542
  62.6 3.4 %unshared.7 = (f32[96,256]{1,0:T(8,128)S(1)}, f32[96,256]{1,0:T(8,128)S(1)}, f32[96,256]{1,0:T(8,128)S(1)}, f32[192,256]{1,0:T(8,128)S(1)}) custom-call(f32[96,256]{1,0:T(8,128)S(1)} %get-tuple-element.128.partial_ref, f32[96,256]{1,0:T(8,128)S(1)} %get-tuple-element.129.residual_ref, f32[96,256]{1,0:T(8,128)S(1)} %get-tuple-element.120.inverse_ref, ...), custom_call_target="tpu_custom_call" | custom-call | tf_op jit(solution)/shard_map/unshared/pallas_call | solution.py:645
  66.8 3.2 %shared.7 = (f32[24,128]{1,0:T(8,128)S(1)}, f32[24,128]{1,0:T(8,128)S(1)}, f32[24,128]{1,0:T(8,128)S(1)}, f32[96,256]{1,0:T(8,128)S(1)}, f32[24,128]{1,0:T(8,128)S(1)}) custom-call(f32[24,128]{1,0:T(8,128)S(1)} %get-tuple-element.124.message_in, f32[24,128]{1,0:T(8,128)S(1)} %collective-permute-done.6.near_in, ...), custom_call_target="tpu_custom_call" | custom-call | tf_op jit(solution)/shard_map/shared/pallas_call | solution.py:650
  70.0 4.8 %collective-permute-start.9 = (f32[24,128]{1,0:T(8,128)S(1)}, f32[24,128]{1,0:T(8,128)S(1)}, u32[]{:S(2)}, u32[]{:S(2)}) collective-permute-start(f32[24,128]{1,0:T(8,128)S(1)} %get-tuple-element.133.message_in), channel_id=1, source_target_pairs={{1,2},{2,1},{3,4},{4,3},{5,6},{6,5},{7,8},{8,7},{9,10},{10,9},{11,... | collective-permute-start | bytes 36872 | tf_op jit(solution)/shard_map/ppermute | solution.py:542
  74.9 3.4 %unshared.8 = (f32[96,256]{1,0:T(8,128)S(1)}, f32[96,256]{1,0:T(8,128)S(1)}, f32[96,256]{1,0:T(8,128)S(1)}, f32[192,256]{1,0:T(8,128)S(1)}) custom-call(f32[96,256]{1,0:T(8,128)S(1)} %get-tuple-element.137.partial_ref, f32[96,256]{1,0:T(8,128)S(1)} %get-tuple-element.138.residual_ref, f32[96,256]{1,0:T(8,128)S(1)} %get-tuple-element.120.inverse_ref, ...), custom_call_target="tpu_custom_call" | custom-call | tf_op jit(solution)/shard_map/unshared/pallas_call | solution.py:645
  79.2 3.2 %shared.8 = (f32[24,128]{1,0:T(8,128)S(1)}, f32[24,128]{1,0:T(8,128)S(1)}, f32[24,128]{1,0:T(8,128)S(1)}, f32[96,256]{1,0:T(8,128)S(1)}, f32[24,128]{1,0:T(8,128)S(1)}) custom-call(f32[24,128]{1,0:T(8,128)S(1)} %get-tuple-element.133.message_in, f32[24,128]{1,0:T(8,128)S(1)} %collective-permute-done.8.near_in, ...), custom_call_target="tpu_custom_call" | custom-call | tf_op jit(solution)/shard_map/shared/pallas_call | solution.py:650
  82.4 4.8 %collective-permute-start.11 = (f32[24,128]{1,0:T(8,128)S(1)}, f32[24,128]{1,0:T(8,128)S(1)}, u32[]{:S(2)}, u32[]{:S(2)}) collective-permute-start(f32[24,128]{1,0:T(8,128)S(1)} %get-tuple-element.142.message_in), channel_id=1, source_target_pairs={{1,2},{2,1},{3,4},{4,3},{5,6},{6,5},{7,8},{8,7},{9,10},{10,9},{11,... | collective-permute-start | bytes 36872 | tf_op jit(solution)/shard_map/ppermute | solution.py:542
  87.3 3.4 %unshared.9 = (f32[96,256]{1,0:T(8,128)S(1)}, f32[96,256]{1,0:T(8,128)S(1)}, f32[96,256]{1,0:T(8,128)S(1)}, f32[192,256]{1,0:T(8,128)S(1)}) custom-call(f32[96,256]{1,0:T(8,128)S(1)} %get-tuple-element.146.partial_ref, f32[96,256]{1,0:T(8,128)S(1)} %get-tuple-element.147.residual_ref, f32[96,256]{1,0:T(8,128)S(1)} %get-tuple-element.120.inverse_ref, ...), custom_call_target="tpu_custom_call" | custom-call | tf_op jit(solution)/shard_map/unshared/pallas_call | solution.py:645
  90.7 1.0 collective-permute-done.11.other_in
  91.7 3.2 %shared.9 = (f32[24,128]{1,0:T(8,128)S(1)}, f32[24,128]{1,0:T(8,128)S(1)}, f32[24,128]{1,0:T(8,128)S(1)}, f32[96,256]{1,0:T(8,128)S(1)}, f32[24,128]{1,0:T(8,128)S(1)}) custom-call(f32[24,128]{1,0:T(8,128)S(1)} %get-tuple-element.142.message_in, f32[24,128]{1,0:T(8,128)S(1)} %collective-permute-done.10.near_in, ...), custom_call_target="tpu_custom_call" | custom-call | tf_op jit(solution)/shard_map/shared/pallas_call | solution.py:650
  94.9 4.8 %collective-permute-start.13 = (f32[24,128]{1,0:T(8,128)S(1)}, f32[24,128]{1,0:T(8,128)S(1)}, u32[]{:S(2)}, u32[]{:S(2)}) collective-permute-start(f32[24,128]{1,0:T(8,128)S(1)} %get-tuple-element.151.message_in), channel_id=1, source_target_pairs={{1,2},{2,1},{3,4},{4,3},{5,6},{6,5},{7,8},{8,7},{9,10},{10,9},{11,... | collective-permute-start | bytes 36872 | tf_op jit(solution)/shard_map/ppermute | solution.py:542
  99.8 3.4 %unshared.10 = (f32[96,256]{1,0:T(8,128)S(1)}, f32[96,256]{1,0:T(8,128)S(1)}, f32[96,256]{1,0:T(8,128)S(1)}, f32[192,256]{1,0:T(8,128)S(1)}) custom-call(f32[96,256]{1,0:T(8,128)S(1)} %get-tuple-element.155.partial_ref, f32[96,256]{1,0:T(8,128)S(1)} %get-tuple-element.156.residual_ref, f32[96,256]{1,0:T(8,128)S(1)} %get-tuple-element.120.inverse_ref, ...), custom_call_target="tpu_custom_call" | custom-call | tf_op jit(solution)/shard_map/unshared/pallas_call | solution.py:645
  104.1 3.2 %shared.10 = (f32[24,128]{1,0:T(8,128)S(1)}, f32[24,128]{1,0:T(8,128)S(1)}, f32[24,128]{1,0:T(8,128)S(1)}, f32[96,256]{1,0:T(8,128)S(1)}, f32[24,128]{1,0:T(8,128)S(1)}) custom-call(f32[24,128]{1,0:T(8,128)S(1)} %get-tuple-element.151.message_in, f32[24,128]{1,0:T(8,128)S(1)} %collective-permute-done.12.near_in, ...), custom_call_target="tpu_custom_call" | custom-call | tf_op jit(solution)/shard_map/shared/pallas_call | solution.py:650
  107.4 4.8 %collective-permute-start.15 = (f32[24,128]{1,0:T(8,128)S(1)}, f32[24,128]{1,0:T(8,128)S(1)}, u32[]{:S(2)}, u32[]{:S(2)}) collective-permute-start(f32[24,128]{1,0:T(8,128)S(1)} %get-tuple-element.160.message_in), channel_id=1, source_target_pairs={{1,2},{2,1},{3,4},{4,3},{5,6},{6,5},{7,8},{8,7},{9,10},{10,9},{11,... | collective-permute-start | bytes 36872 | tf_op jit(solution)/shard_map/ppermute | solution.py:542
  112.2 3.4 %unshared.11 = (f32[96,256]{1,0:T(8,128)S(1)}, f32[96,256]{1,0:T(8,128)S(1)}, f32[96,256]{1,0:T(8,128)S(1)}, f32[192,256]{1,0:T(8,128)S(1)}) custom-call(f32[96,256]{1,0:T(8,128)S(1)} %get-tuple-element.164.partial_ref, f32[96,256]{1,0:T(8,128)S(1)} %get-tuple-element.165.residual_ref, f32[96,256]{1,0:T(8,128)S(1)} %get-tuple-element.120.inverse_ref, ...), custom_call_target="tpu_custom_call" | custom-call | tf_op jit(solution)/shard_map/unshared/pallas_call | solution.py:645
  115.6 1.0 collective-permute-done.15.other_in
  116.6 3.2 %shared.11 = (f32[24,128]{1,0:T(8,128)S(1)}, f32[24,128]{1,0:T(8,128)S(1)}, f32[24,128]{1,0:T(8,128)S(1)}, f32[96,256]{1,0:T(8,128)S(1)}, f32[24,128]{1,0:T(8,128)S(1)}) custom-call(f32[24,128]{1,0:T(8,128)S(1)} %get-tuple-element.160.message_in, f32[24,128]{1,0:T(8,128)S(1)} %collective-permute-done.14.near_in, ...), custom_call_target="tpu_custom_call" | custom-call | tf_op jit(solution)/shard_map/shared/pallas_call | solution.py:650
  119.8 4.8 %collective-permute-start.17 = (f32[24,128]{1,0:T(8,128)S(1)}, f32[24,128]{1,0:T(8,128)S(1)}, u32[]{:S(2)}, u32[]{:S(2)}) collective-permute-start(f32[24,128]{1,0:T(8,128)S(1)} %get-tuple-element.169.message_in), channel_id=1, source_target_pairs={{1,2},{2,1},{3,4},{4,3},{5,6},{6,5},{7,8},{8,7},{9,10},{10,9},{11,... | collective-permute-start | bytes 36872 | tf_op jit(solution)/shard_map/ppermute | solution.py:542
  124.7 4.3 %collective-permute-done.17.other_in = f32[24,128]{1,0:T(8,128)S(1)} collective-permute-done((f32[24,128]{1,0:T(8,128)S(1)}, f32[24,128]{1,0:T(8,128)S(1)}, u32[]{:S(2)}, u32[]{:S(2)}) %collective-permute-start.17) | collective-permute-done | bytes 12320 | tf_op jit(solution)/shard_map/ppermute | solution.py:542
  129.1 1.0 last_shared.1
  (25 shorter events, 4.6 us)
Async XLA Ops:
  3.0 22.9 %all-to-all-start = ((f32[128,1,256]{2,1,0:T(1,128)}), f32[128,1,256]{2,1,0:T(1,128)S(1)}, u32[]{:S(2)}, u32[]{:S(2)}) async-start(f32[128,1,256]{2,1,0:T(1,128)} %get-tuple-element.94), calls=%async_computation | async-start | bytes 262144 | tf_op jit(solution)/shard_map/all_to_all | solution.py:595
  13.4 12.4 %collective-permute-start.1 = (f32[40,256]{1,0:T(8,128)S(1)}, f32[40,256]{1,0:T(8,128)S(1)}, u32[]{:S(2)}, u32[]{:S(2)}) collective-permute-start(f32[40,256]{1,0:T(8,128)S(1)} %get-tuple-element.96), channel_id=1, source_target_pairs={{1,2},{2,1},{3,4},{4,3},{5,6},{6,5},{7,8},{8,7},{9,10},{10,9},{11,... | collective-permute-start | bytes 122888 | tf_op jit(solution)/shard_map/ppermute | solution.py:542
  21.1 4.7 %collective-permute-start = (f32[40,256]{1,0:T(8,128)S(1)}, f32[40,256]{1,0:T(8,128)S(1)}, u32[]{:S(2)}, u32[]{:S(2)}) collective-permute-start(f32[40,256]{1,0:T(8,128)S(1)} %get-tuple-element.95.field_message), channel_id=1, source_target_pairs={{0,1},{1,0},{2,3},{3,2},{4,5},{5,4},{6,7},{7,6},{8,9},{9,8},{10,11... | collective-permute-start | bytes 122888 | tf_op jit(solution)/shard_map/ppermute | solution.py:543
  32.5 9.4 %collective-permute-start.3 = (f32[48,128]{1,0:T(8,128)S(1)}, f32[48,128]{1,0:T(8,128)S(1)}, u32[]{:S(2)}, u32[]{:S(2)}) collective-permute-start(f32[48,128]{1,0:T(8,128)S(1)} %get-tuple-element.106.message_in), channel_id=1, source_target_pairs={{1,2},{2,1},{3,4},{4,3},{5,6},{6,5},{7,8},{8,7},{9,10},{10,9},{11,... | collective-permute-start | bytes 73736 | tf_op jit(solution)/shard_map/ppermute | solution.py:542
  37.3 4.6 %collective-permute-start.2 = (f32[48,128]{1,0:T(8,128)S(1)}, f32[48,128]{1,0:T(8,128)S(1)}, u32[]{:S(2)}, u32[]{:S(2)}) collective-permute-start(f32[48,128]{1,0:T(8,128)S(1)} %get-tuple-element.106.message_in), channel_id=1, source_target_pairs={{0,1},{1,0},{2,3},{3,2},{4,5},{5,4},{6,7},{7,6},{8,9},{9,8},{10,11... | collective-permute-start | bytes 73736 | tf_op jit(solution)/shard_map/ppermute | solution.py:543
  45.1 9.2 %collective-permute-start.5 = (f32[24,128]{1,0:T(8,128)S(1)}, f32[24,128]{1,0:T(8,128)S(1)}, u32[]{:S(2)}, u32[]{:S(2)}) collective-permute-start(f32[24,128]{1,0:T(8,128)S(1)} %get-tuple-element.114.message_in), channel_id=1, source_target_pairs={{1,2},{2,1},{3,4},{4,3},{5,6},{6,5},{7,8},{8,7},{9,10},{10,9},{11,... | collective-permute-start | bytes 36872 | tf_op jit(solution)/shard_map/ppermute | solution.py:542
  49.8 4.5 %collective-permute-start.4 = (f32[24,128]{1,0:T(8,128)S(1)}, f32[24,128]{1,0:T(8,128)S(1)}, u32[]{:S(2)}, u32[]{:S(2)}) collective-permute-start(f32[24,128]{1,0:T(8,128)S(1)} %get-tuple-element.114.message_in), channel_id=1, source_target_pairs={{0,1},{1,0},{2,3},{3,2},{4,5},{5,4},{6,7},{7,6},{8,9},{9,8},{10,11... | collective-permute-start | bytes 36872 | tf_op jit(solution)/shard_map/ppermute | solution.py:543
  57.5 9.2 %collective-permute-start.7 = (f32[24,128]{1,0:T(8,128)S(1)}, f32[24,128]{1,0:T(8,128)S(1)}, u32[]{:S(2)}, u32[]{:S(2)}) collective-permute-start(f32[24,128]{1,0:T(8,128)S(1)} %get-tuple-element.124.message_in), channel_id=1, source_target_pairs={{1,2},{2,1},{3,4},{4,3},{5,6},{6,5},{7,8},{8,7},{9,10},{10,9},{11,... | collective-permute-start | bytes 36872 | tf_op jit(solution)/shard_map/ppermute | solution.py:542
  62.3 4.5 %collective-permute-start.6 = (f32[24,128]{1,0:T(8,128)S(1)}, f32[24,128]{1,0:T(8,128)S(1)}, u32[]{:S(2)}, u32[]{:S(2)}) collective-permute-start(f32[24,128]{1,0:T(8,128)S(1)} %get-tuple-element.124.message_in), channel_id=1, source_target_pairs={{0,1},{1,0},{2,3},{3,2},{4,5},{5,4},{6,7},{7,6},{8,9},{9,8},{10,11... | collective-permute-start | bytes 36872 | tf_op jit(solution)/shard_map/ppermute | solution.py:543
  70.0 9.2 %collective-permute-start.9 = (f32[24,128]{1,0:T(8,128)S(1)}, f32[24,128]{1,0:T(8,128)S(1)}, u32[]{:S(2)}, u32[]{:S(2)}) collective-permute-start(f32[24,128]{1,0:T(8,128)S(1)} %get-tuple-element.133.message_in), channel_id=1, source_target_pairs={{1,2},{2,1},{3,4},{4,3},{5,6},{6,5},{7,8},{8,7},{9,10},{10,9},{11,... | collective-permute-start | bytes 36872 | tf_op jit(solution)/shard_map/ppermute | solution.py:542
  74.8 4.5 %collective-permute-start.8 = (f32[24,128]{1,0:T(8,128)S(1)}, f32[24,128]{1,0:T(8,128)S(1)}, u32[]{:S(2)}, u32[]{:S(2)}) collective-permute-start(f32[24,128]{1,0:T(8,128)S(1)} %get-tuple-element.133.message_in), channel_id=1, source_target_pairs={{0,1},{1,0},{2,3},{3,2},{4,5},{5,4},{6,7},{7,6},{8,9},{9,8},{10,11... | collective-permute-start | bytes 36872 | tf_op jit(solution)/shard_map/ppermute | solution.py:543
  82.4 9.2 %collective-permute-start.11 = (f32[24,128]{1,0:T(8,128)S(1)}, f32[24,128]{1,0:T(8,128)S(1)}, u32[]{:S(2)}, u32[]{:S(2)}) collective-permute-start(f32[24,128]{1,0:T(8,128)S(1)} %get-tuple-element.142.message_in), channel_id=1, source_target_pairs={{1,2},{2,1},{3,4},{4,3},{5,6},{6,5},{7,8},{8,7},{9,10},{10,9},{11,... | collective-permute-start | bytes 36872 | tf_op jit(solution)/shard_map/ppermute | solution.py:542
  87.2 4.5 %collective-permute-start.10 = (f32[24,128]{1,0:T(8,128)S(1)}, f32[24,128]{1,0:T(8,128)S(1)}, u32[]{:S(2)}, u32[]{:S(2)}) collective-permute-start(f32[24,128]{1,0:T(8,128)S(1)} %get-tuple-element.142.message_in), channel_id=1, source_target_pairs={{0,1},{1,0},{2,3},{3,2},{4,5},{5,4},{6,7},{7,6},{8,9},{9,8},{10,11... | collective-permute-start | bytes 36872 | tf_op jit(solution)/shard_map/ppermute | solution.py:543
  94.9 9.2 %collective-permute-start.13 = (f32[24,128]{1,0:T(8,128)S(1)}, f32[24,128]{1,0:T(8,128)S(1)}, u32[]{:S(2)}, u32[]{:S(2)}) collective-permute-start(f32[24,128]{1,0:T(8,128)S(1)} %get-tuple-element.151.message_in), channel_id=1, source_target_pairs={{1,2},{2,1},{3,4},{4,3},{5,6},{6,5},{7,8},{8,7},{9,10},{10,9},{11,... | collective-permute-start | bytes 36872 | tf_op jit(solution)/shard_map/ppermute | solution.py:542
  99.7 4.5 %collective-permute-start.12 = (f32[24,128]{1,0:T(8,128)S(1)}, f32[24,128]{1,0:T(8,128)S(1)}, u32[]{:S(2)}, u32[]{:S(2)}) collective-permute-start(f32[24,128]{1,0:T(8,128)S(1)} %get-tuple-element.151.message_in), channel_id=1, source_target_pairs={{0,1},{1,0},{2,3},{3,2},{4,5},{5,4},{6,7},{7,6},{8,9},{9,8},{10,11... | collective-permute-start | bytes 36872 | tf_op jit(solution)/shard_map/ppermute | solution.py:543
  107.4 9.2 %collective-permute-start.15 = (f32[24,128]{1,0:T(8,128)S(1)}, f32[24,128]{1,0:T(8,128)S(1)}, u32[]{:S(2)}, u32[]{:S(2)}) collective-permute-start(f32[24,128]{1,0:T(8,128)S(1)} %get-tuple-element.160.message_in), channel_id=1, source_target_pairs={{1,2},{2,1},{3,4},{4,3},{5,6},{6,5},{7,8},{8,7},{9,10},{10,9},{11,... | collective-permute-start | bytes 36872 | tf_op jit(solution)/shard_map/ppermute | solution.py:542
  112.1 4.5 %collective-permute-start.14 = (f32[24,128]{1,0:T(8,128)S(1)}, f32[24,128]{1,0:T(8,128)S(1)}, u32[]{:S(2)}, u32[]{:S(2)}) collective-permute-start(f32[24,128]{1,0:T(8,128)S(1)} %get-tuple-element.160.message_in), channel_id=1, source_target_pairs={{0,1},{1,0},{2,3},{3,2},{4,5},{5,4},{6,7},{7,6},{8,9},{9,8},{10,11... | collective-permute-start | bytes 36872 | tf_op jit(solution)/shard_map/ppermute | solution.py:543
  119.8 9.2 %collective-permute-start.17 = (f32[24,128]{1,0:T(8,128)S(1)}, f32[24,128]{1,0:T(8,128)S(1)}, u32[]{:S(2)}, u32[]{:S(2)}) collective-permute-start(f32[24,128]{1,0:T(8,128)S(1)} %get-tuple-element.169.message_in), channel_id=1, source_target_pairs={{1,2},{2,1},{3,4},{4,3},{5,6},{6,5},{7,8},{8,7},{9,10},{10,9},{11,... | collective-permute-start | bytes 36872 | tf_op jit(solution)/shard_map/ppermute | solution.py:542
  124.6 4.5 %collective-permute-start.16 = (f32[24,128]{1,0:T(8,128)S(1)}, f32[24,128]{1,0:T(8,128)S(1)}, u32[]{:S(2)}, u32[]{:S(2)}) collective-permute-start(f32[24,128]{1,0:T(8,128)S(1)} %get-tuple-element.169.message_in), channel_id=1, source_target_pairs={{0,1},{1,0},{2,3},{3,2},{4,5},{5,4},{6,7},{7,6},{8,9},{9,8},{10,11... | collective-permute-start | bytes 36872 | tf_op jit(solution)/shard_map/ppermute | solution.py:543

commit v4 on v3

--- a/solution.py
+++ b/solution.py
@@ -67,7 +67,47 @@
     lax.fori_loop(0, PER // 8, block, 0)
 
 
-def gather_shared(shared_ref, index_ref, rows_ref, first_row):
+def gather_mixed(state_ref, nodes_ref, hot_ref, out_ref):
+    table = jnp.concatenate(split(state_ref[...]), axis=0).astype(BF16)
+    line = iota((32, 256), 0)
+    half_rows = PER // 2
+
+    def block(b, carry):
+        row = pl.multiple_of(b * 8, 8)
+        for half in range(2):
+            lanes = slice(half * 128, half * 128 + 128)
+            index = nodes_ref[pl.ds(row, 8), lanes]
+            lane = index & 127
+            chunk = index >> 7
+            found = [jnp.zeros((8, 128), F32)] * 3
+            for k in range(OWN_CHUNKS):
+                here = chunk == k
+                part = slice((k % 2) * 128, (k % 2) * 128 + 128)
+                for c in range(3):
+                    source = 32 * c + k // 2
+                    values = jnp.broadcast_to(state_ref[source : source + 1, part], (8, 128))
+                    found[c] = jnp.where(here, lane_pick(values, lane), found[c])
+            for c in range(3):
+                out_ref[pl.ds(c * PER + row, 8), lanes] = found[c]
+        other = pl.multiple_of(b * 8 + half_rows, 8)
+        lines = nodes_ref[pl.ds(other, 8), :] >> 8
+        for k in range(8):
+            hot = hot_ref[pl.ds(pl.multiple_of((other + k) * 256, 256), 256), :]
+            got = lax.dot_general(
+                table, hot, (((1,), (1,)), ((), ())), preferred_element_type=F32
+            )
+            here = lines[k : k + 1, :] == line
+            for c in range(3):
+                both = got[32 * c : 32 * c + 32] + got[96 + 32 * c : 128 + 32 * c]
+                out_ref[pl.ds(c * PER + other + k, 1), :] = jnp.sum(
+                    jnp.where(here, both, 0.0), axis=0, keepdims=True
+                )
+        return carry
+
+    lax.fori_loop(0, half_rows // 8, block, 0)
+
+
+def gather_shared(shared_ref, index_ref, rows_ref, out_ref, first_row):
     tables = [
         [
             jnp.broadcast_to(shared_ref[8 * c + r : 8 * c + r + 1, :], (8, 128))
@@ -87,7 +127,7 @@
                 found = rows_ref[rows, lanes]
                 for r in range(first_row, SHARED_ROWS):
                     found = jnp.where(masks[r - first_row], lane_pick(tables[c][r], lane), found)
-                rows_ref[rows, lanes] = found
+                out_ref[rows, lanes] = found
 
 
 def scatter_elements(nodes_ref, hot_ref, values_ref, high_ref, low_ref, sums_ref, channels):
@@ -126,6 +166,42 @@
         return carry
 
     lax.fori_loop(0, PER // BLOCK, block, 0)
+
+
+def scatter_shared(index_ref, hot_ref, values_ref, high_ref, low_ref, sums_ref, out_ref):
+    high, low = split(values_ref[...])
+    high_ref[...] = high
+    low_ref[...] = low
+    sums_ref[...] = jnp.zeros_like(sums_ref)
+    lines = iota((8, 256), 0)
+
+    def block(b, carry):
+        row = pl.multiple_of(b * BLOCK, BLOCK)
+        line = index_ref[pl.ds(row, BLOCK), :] >> 7
+        left = []
+        for k in range(BLOCK):
+            here = line[k : k + 1, :] == lines
+            left.append(
+                jnp.concatenate(
+                    [
+                        jnp.where(
+                            here,
+                            jnp.broadcast_to(ref[pl.ds(c * PER + row + k, 1), :], (8, 256)),
+                            0.0,
+                        )
+                        for ref in (high_ref, low_ref)
+                        for c in range(3)
+                    ],
+                    axis=0,
+                ).astype(BF16)
+            )
+        left = jnp.concatenate(left, axis=1)
+        right = hot_ref[pl.ds(pl.multiple_of(row * 256, 256), BLOCK * 256), :]
+        sums_ref[...] += jnp.dot(left, right, preferred_element_type=F32)
+        return carry
+
+    lax.fori_loop(0, PER // BLOCK, block, 0)
+    out_ref[...] = sums_ref[0:24, :] + sums_ref[24:48, :]
 
 
 def add_parts(sums_ref, first, channels):
@@ -242,7 +318,7 @@
     ]
     for copy in copies:
         copy.start()
-    for copy in copies:
+    for copy in copies[:3]:
         copy.wait()
     me = lax.axis_index(AXES)
     first_core = lax.axis_index("sub") == 0
@@ -276,6 +352,8 @@
     near_out[0:NEAR_CAP, :] = packed[DEVICES : DEVICES + NEAR_CAP]
     other_out[0:NEAR_CAP, :] = packed[DEVICES + NEAR_CAP :]
     near_out[NEAR_CAP:, :] = jnp.zeros((24, 256), F32)
+    for copy in copies[3:]:
+        copy.wait()
     places_ref[...] = jnp.zeros((8, 128), jnp.int32)
     places_ref[0:1, :] = face_ref[0:1, 0:128]
     places_ref[1:2, 0:64] = face_ref[0:1, 128:192]
@@ -323,9 +401,9 @@
         low_ref[DOFS * i : DOFS * i + DOFS, :] = low.astype(BF16)
 
 
-def build_hot(nodes_ref, hot_ref):
-    low = (nodes_ref[...] & 255).astype(F32)
-    lanes = iota((16, 256), 1).astype(F32).astype(BF16)
+def build_hot(index_ref, hot_ref, width):
+    low = (index_ref[...] & (width - 1)).astype(F32)
+    lanes = iota((16, width), 1).astype(F32).astype(BF16)
     one = jnp.ones((), BF16)
     zero = jnp.zeros((), BF16)
     for half in range(2):
@@ -334,7 +412,7 @@
             columns = turned[16 * b : 16 * b + 16]
             for n in range(PER):
                 top = 256 * n + half * 128 + 16 * b
-                column = jnp.broadcast_to(columns[:, n : n + 1], (16, 256))
+                column = jnp.broadcast_to(columns[:, n : n + 1], (16, width))
                 hot_ref[top : top + 16, :] = jnp.where(column == lanes, one, zero)
 
 
@@ -379,8 +457,7 @@
     sums,
 ):
     shared_field[...] = field_message[NEAR_CAP:, 0:128] + from_neighbours(near_in, other_in, NEAR_CAP)
-    gathered[...] = gathered_in[...]
-    gather_shared(shared_field, shared_index_ref, gathered, 3)
+    gather_shared(shared_field, shared_index_ref, gathered_in, gathered, 3)
     products = multiply_blocks(high_ref, low_ref, gathered)
     me = lax.axis_index(AXES)
     received = jnp.concatenate(
@@ -407,7 +484,7 @@
     first_diag = jnp.sum(jnp.where(eye, stiff_ref[0], 0.0), axis=1, keepdims=True)
     second_diag = jnp.sum(jnp.where(eye, stiff_ref[1], 0.0), axis=1, keepdims=True)
     values[DOFS:, :] = first_diag * coefs[0:1, :] + second_diag * coefs[1:2, :]
-    build_hot(nodes_ref, hot_ref)
+    build_hot(nodes_ref, hot_ref, 256)
     scatter_elements(nodes_ref, hot_ref, values, value_high, value_low, sums, 6)
     partial_ref[...] = add_parts(sums, 0, 6)
     diagonal_ref[...] = add_parts(sums, 3, 6)
@@ -416,16 +493,13 @@
 
 
 def apply_operator(
-    shared_update, gathered_in, shared_index_ref, nodes_ref, coefs_ref, places_ref, hot_ref, high_ref,
-    low_ref, partial_ref, message, gathered, value_high, value_low, sums,
-):
-    gathered[...] = gathered_in[...]
-    gather_shared(shared_update, shared_index_ref, gathered, 0)
+    shared_update, gathered_in, shared_index_ref, coefs_ref, hot_ref, high_ref, low_ref, values_ref,
+    message, gathered, value_high, value_low, sums,
+):
+    gather_shared(shared_update, shared_index_ref, gathered_in, gathered, 0)
     products = multiply_blocks(high_ref, low_ref, gathered)
-    gathered[...] = products[:DOFS] * coefs_ref[0:1, :] + products[DOFS:] * coefs_ref[1:2, :]
-    scatter_elements(nodes_ref, hot_ref, gathered, value_high, value_low, sums, 3)
-    partial_ref[...] = add_parts(sums, 0, 3)
-    take_shared(partial_ref, places_ref[...], message, 0, True)
+    values_ref[...] = products[:DOFS] * coefs_ref[0:1, :] + products[DOFS:] * coefs_ref[1:2, :]
+    scatter_shared(shared_index_ref, hot_ref, values_ref, value_high, value_low, sums, message)
 
 
 def inverse_of(diagonal):
@@ -433,22 +507,22 @@
 
 
 def begin_unshared(
-    step, partial_ref, diagonal_ref, unshared_ref, field_ref, nodes_ref, inverse_out, update_out,
-    field_out, gathered_out,
-):
+    step, partial_ref, diagonal_ref, unshared_ref, field_ref, nodes_ref, hot_ref, shared_index_ref,
+    inverse_out, update_out, field_out, gathered_out, hot_shared_ref,
+):
+    build_hot(shared_index_ref, hot_shared_ref, 128)
     unshared = jnp.concatenate([unshared_ref[...]] * 3, axis=0)
     inverse = jnp.where(unshared > 0.0, inverse_of(diagonal_ref[...]), 0.0)
     update = step[1] * (partial_ref[...] * inverse)
     inverse_out[...] = inverse
     update_out[...] = update
     field_out[...] = field_ref[...] + update
-    gather_own(update_out, nodes_ref, gathered_out)
+    gather_mixed(update_out, nodes_ref, hot_ref, gathered_out)
 
 
 def begin_shared(
-    step, message_in, near_in, other_in, shared_field, gathered_in, shared_index_ref, nodes_ref,
-    coefs_ref, places_ref, hot_ref, high_ref, low_ref, residual_out, inverse_out, update_out,
-    field_out, partial_ref, message, gathered, value_high, value_low, sums,
+    step, message_in, near_in, other_in, shared_field, gathered_in, shared_index_ref, coefs_ref,
+    hot_ref, high_ref, low_ref, residual_out, inverse_out, update_out, field_out, values_ref, message, gathered, value_high, value_low, sums,
 ):
     residual = message_in[0:24, :] + from_neighbours(near_in, other_in, 0)
     inverse = inverse_of(message_in[24:48, :] + from_neighbours(near_in, other_in, 24))
@@ -458,8 +532,8 @@
     update_out[...] = update
     field_out[...] = shared_field[...] + update
     apply_operator(
-        update_out, gathered_in, shared_index_ref, nodes_ref, coefs_ref, places_ref, hot_ref,
-        high_ref, low_ref, partial_ref, message, gathered, value_high, value_low, sums,
+        update_out, gathered_in, shared_index_ref, coefs_ref, hot_ref, high_ref, low_ref, values_ref,
+        message, gathered, value_high, value_low, sums,
     )
 
 
@@ -469,21 +543,22 @@
 
 
 def step_unshared(
-    step, partial_ref, residual_ref, inverse_ref, update_ref, field_ref, nodes_ref, residual_out,
-    update_out, field_out, gathered_out,
-):
-    residual = residual_ref[...] - partial_ref[...]
+    step, values_ref, residual_ref, inverse_ref, update_ref, field_ref, nodes_ref, hot_ref,
+    residual_out, update_out, field_out, gathered_out, value_high, value_low, sums,
+):
+    scatter_elements(nodes_ref, hot_ref, values_ref, value_high, value_low, sums, 3)
+    residual = residual_ref[...] - add_parts(sums, 0, 3)
     update = next_update(step, residual, inverse_ref[...], update_ref[...])
     residual_out[...] = residual
     update_out[...] = update
     field_out[...] = field_ref[...] + update
-    gather_own(update_out, nodes_ref, gathered_out)
+    gather_mixed(update_out, nodes_ref, hot_ref, gathered_out)
 
 
 def step_shared(
     step, message_in, near_in, other_in, residual_ref, inverse_ref, update_ref, field_ref,
-    gathered_in, shared_index_ref, nodes_ref, coefs_ref, places_ref, hot_ref, high_ref, low_ref,
-    residual_out, update_out, field_out, partial_ref, message, gathered, value_high, value_low, sums,
+    gathered_in, shared_index_ref, coefs_ref, hot_ref, high_ref, low_ref, residual_out, update_out,
+    field_out, values_ref, message, gathered, value_high, value_low, sums,
 ):
     residual = residual_ref[...] - (message_in[...] + from_neighbours(near_in, other_in, 0))
     update = next_update(step, residual, inverse_ref[...], update_ref[...])
@@ -491,13 +566,17 @@
     update_out[...] = update
     field_out[...] = field_ref[...] + update
     apply_operator(
-        update_out, gathered_in, shared_index_ref, nodes_ref, coefs_ref, places_ref, hot_ref,
-        high_ref, low_ref, partial_ref, message, gathered, value_high, value_low, sums,
-    )
-
-
-def last_unshared(step, partial_ref, residual_ref, inverse_ref, update_ref, field_ref, field_out):
-    residual = residual_ref[...] - partial_ref[...]
+        update_out, gathered_in, shared_index_ref, coefs_ref, hot_ref, high_ref, low_ref, values_ref,
+        message, gathered, value_high, value_low, sums,
+    )
+
+
+def last_unshared(
+    step, values_ref, residual_ref, inverse_ref, update_ref, field_ref, nodes_ref, hot_ref, field_out,
+    value_high, value_low, sums,
+):
+    scatter_elements(nodes_ref, hot_ref, values_ref, value_high, value_low, sums, 3)
+    residual = residual_ref[...] - add_parts(sums, 0, 3)
     field_out[...] = field_ref[...] + next_update(step, residual, inverse_ref[...], update_ref[...])
 
 
@@ -626,18 +705,19 @@
     )
     near, other = exchange(message, message)
     plan = steps()
-    fixed = (shared_index, nodes, coefs, places, hot, high, low)
-    scratch = [rows(DOFS)] * 3 + [rows(192)]
+    scratch = [rows(DOFS)] * 3 + [pltpu.VMEM((48, 128), F32)]
+    window_scratch = [rows(DOFS)] * 2 + [rows(192)]
     residual = partial
-    inverse, update, field, gathered = call(
+    inverse, update, field, gathered, hot_shared = call(
         functools.partial(begin_unshared, plan[0]),
         "begin_unshared",
-        (STATE, STATE, STATE, ELEMENT_ROWS),
-    )(partial, diagonal, unshared, field, nodes)
-    shared_residual, shared_inverse, shared_update, shared_field, partial, message = call(
+        (STATE, STATE, STATE, ELEMENT_ROWS, shaped(PER * ELEM, 128, dtype=BF16)),
+    )(partial, diagonal, unshared, field, nodes, hot, shared_index)
+    fixed = (shared_index, coefs, hot_shared, high, low)
+    shared_residual, shared_inverse, shared_update, shared_field, values, message = call(
         functools.partial(begin_shared, plan[0]),
         "begin_shared",
-        (SHARED, SHARED, SHARED, SHARED, STATE, SHARED),
+        (SHARED, SHARED, SHARED, SHARED, ELEMENT_ROWS, SHARED),
         scratch,
     )(message, near, other, shared_field, gathered, *fixed)
     for step in plan[1:-1]:
@@ -646,20 +726,21 @@
             functools.partial(step_unshared, step),
             "unshared",
             (STATE, STATE, STATE, ELEMENT_ROWS),
-        )(partial, residual, inverse, update, field, nodes)
-        shared_residual, shared_update, shared_field, partial, message = call(
+            window_scratch,
+        )(values, residual, inverse, update, field, nodes, hot)
+        shared_residual, shared_update, shared_field, values, message = call(
             functools.partial(step_shared, step),
             "shared",
-            (SHARED, SHARED, SHARED, STATE, SHARED),
+            (SHARED, SHARED, SHARED, ELEMENT_ROWS, SHARED),
             scratch,
         )(
             message, near, other, shared_residual, shared_inverse, shared_update, shared_field,
             gathered, *fixed,
         )
     near, other = exchange(message, message)
-    field = call(functools.partial(last_unshared, plan[-1]), "last_unshared", STATE)(
-        partial, residual, inverse, update, field
-    )
+    field = call(
+        functools.partial(last_unshared, plan[-1]), "last_unshared", STATE, window_scratch
+    )(values, residual, inverse, update, field, nodes, hot)
     field = call(functools.partial(last_shared, plan[-1]), "last_shared", shaped(3, OWN))(
         message, near, other, shared_residual, shared_inverse, shared_update, shared_field, field,
         unshared, places,

time: 130 us -> 123 us (0.946)
  waiting for transfers between devices: 11 us -> 3.06 us
  starting transfers between devices: 57.1 us -> 58.6 us
  Pallas kernels: 61 us -> 59.6 us
    ppermute x9, waiting for transfers between devices: 11 us -> 3.04 us  [exchange(): other = lax.ppermute(other_message, AXES, OTHER_PAIRS)]
    pallas_call x6, Pallas kernels: 19.3 us -> 11.8 us  [local(): call(functools.partial(step_shared, step), 'shared', (SHARED, SHARED, SHA...]
    pallas_call x6, Pallas kernels: 20.5 us -> 25.3 us  [local(): call(functools.partial(step_unshared, step), 'unshared', (STATE, STATE, S...]
    pallas_call x1, Pallas kernels: 0.04 us -> 2.08 us  [local(): call(functools.partial(last_unshared, plan[-1]), 'last_unshared', STATE,...]
    ppermute x9, starting transfers between devices: 45.7 us -> 47.4 us  [exchange(): other = lax.ppermute(other_message, AXES, OTHER_PAIRS)]
  transfers between devices with their start and end apart: 19 -> 19, of which waited for: 8 -> 6; matrix products, arithmetic and copies ran while one was open for 0% -> 0% of each run, Pallas kernels for 22% -> 29%
where the time goes in v4:
time: 123 us; the launch traced here: 122 us
  Pallas kernels  59.6 us (48%)
  starting transfers between devices  58.6 us (48%)
  waiting for transfers between devices  3.06 us (2%)
    ppermute x9, starting transfers between devices, exchange(): other = lax.ppermute(other_message, AXES, OTHER_PAIRS)  47.4 us
    pallas_call x6, Pallas kernels, local(): call(functools.partial(step_unshared, step), 'unshared', (STATE, STATE, S...  25.3 us
    pallas_call x6, Pallas kernels, local(): call(functools.partial(step_shared, step), 'shared', (SHARED, SHARED, SHA...  11.8 us
    all_to_all x1, starting transfers between devices, local(): far = lax.all_to_all(far, AXES, split_axis=0, concat_axis=0, tiled=True)  10.5 us
    pallas_call x1, Pallas kernels, local(): call(place_kernel, 'place', (shaped(PER * ELEM, 256, dtype=BF16), ELEMENT...  6.67 us
    pallas_call x1, Pallas kernels, local(): call(index_kernel, 'index', (integers(PER, ELEM), integers(PER, ELEM), sh...  4.57 us
    pallas_call x1, Pallas kernels, local(): call(functools.partial(begin_unshared, plan[0]), 'begin_unshared', (STATE...  4.07 us
    ppermute x9, waiting for transfers between devices, exchange(): other = lax.ppermute(other_message, AXES, OTHER_PAIRS)  3.04 us
  transfers between devices with their start and end apart: 19, of which 6 were waited for; matrix products, arithmetic and copies ran while one was open for 0% of the time, Pallas kernels for 29%

profile of v4, /device:TPU:6, one launch (start us, length us, event | category | flops | bytes accessed | tf_op | source)
XLA Modules:
  0.0 122.3 jit_solution(6571123556433225290)
XLA Ops:
  0.6 2.1 %pack.1 = (f32[128,1,256]{2,1,0:T(1,128)}, f32[40,256]{1,0:T(8,128)S(1)}, f32[40,256]{1,0:T(8,128)S(1)}, s32[8,128]{1,0:T(8,128)S(1)}, f32[96,256]{1,0:T(8,128)S...) custom-call(f32[192,256]{1,0:T(8,128)} %loads_hbm.1, ...), custom_call_target="tpu_custom_call" | custom-call | tf_op jit(solution)/shard_map/pack/pallas_call | solution.py:650
  2.8 10.5 %all-to-all-start = ((f32[128,1,256]{2,1,0:T(1,128)}), f32[128,1,256]{2,1,0:T(1,128)S(1)}, u32[]{:S(2)}, u32[]{:S(2)}) async-start(f32[128,1,256]{2,1,0:T(1,128)} %get-tuple-element.95), calls=%async_computation | async-start | bytes 262144 | tf_op jit(solution)/shard_map/all_to_all | solution.py:674
  13.2 0.2 collective-permute-start
  13.4 7.9 %collective-permute-start.1 = (f32[40,256]{1,0:T(8,128)S(1)}, f32[40,256]{1,0:T(8,128)S(1)}, u32[]{:S(2)}, u32[]{:S(2)}) collective-permute-start(f32[40,256]{1,0:T(8,128)S(1)} %get-tuple-element.97), channel_id=1, source_target_pairs={{1,2},{2,1},{3,4},{4,3},{5,6},{6,5},{7,8},{8,7},{9,10},{10,9},{11,... | collective-permute-start | bytes 122888 | tf_op jit(solution)/shard_map/ppermute | solution.py:621
  21.3 4.6 %index.1 = (s32[64,256]{1,0:T(8,128)S(1)}, s32[64,256]{1,0:T(8,128)S(1)}, f32[32,256]{1,0:T(8,128)S(1)}, bf16[384,192]{1,0:T(8,128)(2,1)S(1)}, bf16[384,192]{1,0:T(8,128)(2,1)S(1)}, /*index=5*/f32[192,256]{1,0:T(8,128)S(1)}) custom-call(f32[96,256]{1,0:T(8,128)S(1)} %get-tuple-element.99.state_ref.field_ref, s32[8,128]{1,0:T(8,128)S(1)} %get-tuple-element.100.places_ref, ...), custom_call_target="tpu_custom_call" | custom-call | tf_op jit(solution)/shard_map/index/pallas_call | solution.py:675
  25.9 6.7 %place.1 = (bf16[16384,256]{1,0:T(8,128)(2,1)S(1)}, f32[192,256]{1,0:T(8,128)}, f32[2,256]{1,0:T(2,128)}, f32[2,256]{1,0:T(2,128)S(1)}, f32[96,256]{1,0:T(8,128)...) custom-call(f32[192,256]{1,0:T(8,128)S(1)} %get-tuple-element.92.loads_ref, ...), custom_call_target="tpu_custom_call" | custom-call | tf_op jit(solution)/shard_map/place/pallas_call | solution.py:688
  32.6 4.9 %collective-permute-start.3 = (f32[48,128]{1,0:T(8,128)S(1)}, f32[48,128]{1,0:T(8,128)S(1)}, u32[]{:S(2)}, u32[]{:S(2)}) collective-permute-start(f32[48,128]{1,0:T(8,128)S(1)} %get-tuple-element.107.message_in), channel_id=1, source_target_pairs={{1,2},{2,1},{3,4},{4,3},{5,6},{6,5},{7,8},{8,7},{9,10},{10,9},{11,... | collective-permute-start | bytes 73736 | tf_op jit(solution)/shard_map/ppermute | solution.py:621
  37.5 4.1 %begin_unshared.1 = (f32[96,256]{1,0:T(8,128)S(1)}, f32[96,256]{1,0:T(8,128)S(1)}, f32[96,256]{1,0:T(8,128)S(1)}, f32[192,256]{1,0:T(8,128)S(1)}, bf16[16384,128]{1,0:T(8,128)(2,1)S(1)}) custom-call(f32[96,256]{1,0:T(8,128)S(1)} %get-tuple-element.109.partial_ref.residual_ref, f32[96,256]{1,0:T(8,128)S(1)} %get-tuple-element.110.diagonal_ref, ...), custom_call_target="tpu_custom_call" | custom-call | tf_op jit(solution)/shard_map/begin_unshared/pallas_call | solution.py:711
  41.6 0.4 collective-permute-done.3.other_in
  41.9 2.0 %begin_shared.1 = (f32[24,128]{1,0:T(8,128)S(1)}, f32[24,128]{1,0:T(8,128)S(1)}, f32[24,128]{1,0:T(8,128)S(1)}, f32[24,128]{1,0:T(8,128)S(1)}, f32[192,256]{1,0:T(8,128)S(1)}, /*index=5*/f32[24,128]{1,0:T(8,128)S(1)}) custom-call(f32[48,128]{1,0:T(8,128)S(1)} %get-tuple-element.107.message_in, f32[48,128]{1,0:T(8,128)S(1)} %collective-permute-done.2.near_in, ...), custom_call_target="tpu_custom_call" | custom-call | tf_op jit(solution)/shard_map/begin_shared/pallas_call | solution.py:717
  44.0 5.1 %collective-permute-start.5 = (f32[24,128]{1,0:T(8,128)S(1)}, f32[24,128]{1,0:T(8,128)S(1)}, u32[]{:S(2)}, u32[]{:S(2)}) collective-permute-start(f32[24,128]{1,0:T(8,128)S(1)} %get-tuple-element.116.message_in), channel_id=1, source_target_pairs={{1,2},{2,1},{3,4},{4,3},{5,6},{6,5},{7,8},{8,7},{9,10},{10,9},{11,... | collective-permute-start | bytes 36872 | tf_op jit(solution)/shard_map/ppermute | solution.py:621
  49.1 4.2 %unshared.6 = (f32[96,256]{1,0:T(8,128)S(1)}, f32[96,256]{1,0:T(8,128)S(1)}, f32[96,256]{1,0:T(8,128)S(1)}, f32[192,256]{1,0:T(8,128)S(1)}) custom-call(f32[192,256]{1,0:T(8,128)S(1)} %get-tuple-element.121.values_ref, f32[96,256]{1,0:T(8,128)S(1)} %get-tuple-element.109.partial_ref.residual_ref, f32[96,256]{1,0:T(8,128)S(1)} %get-tuple-element.122.inverse_ref, ...), custom_call_target="tpu_custom_call" | custom-call | tf_op jit(solution)/shard_map/unshared/pallas_call | solution.py:725
  53.4 2.0 %shared.6 = (f32[24,128]{1,0:T(8,128)S(1)}, f32[24,128]{1,0:T(8,128)S(1)}, f32[24,128]{1,0:T(8,128)S(1)}, f32[192,256]{1,0:T(8,128)S(1)}, f32[24,128]{1,0:T(8,128)S(1)}) custom-call(f32[24,128]{1,0:T(8,128)S(1)} %get-tuple-element.116.message_in, f32[24,128]{1,0:T(8,128)S(1)} %collective-permute-done.4.near_in, ...), custom_call_target="tpu_custom_call" | custom-call | tf_op jit(solution)/shard_map/shared/pallas_call | solution.py:731
  55.4 4.9 %collective-permute-start.7 = (f32[24,128]{1,0:T(8,128)S(1)}, f32[24,128]{1,0:T(8,128)S(1)}, u32[]{:S(2)}, u32[]{:S(2)}) collective-permute-start(f32[24,128]{1,0:T(8,128)S(1)} %get-tuple-element.126.message_in), channel_id=1, source_target_pairs={{1,2},{2,1},{3,4},{4,3},{5,6},{6,5},{7,8},{8,7},{9,10},{10,9},{11,... | collective-permute-start | bytes 36872 | tf_op jit(solution)/shard_map/ppermute | solution.py:621
  60.3 4.2 %unshared.7 = (f32[96,256]{1,0:T(8,128)S(1)}, f32[96,256]{1,0:T(8,128)S(1)}, f32[96,256]{1,0:T(8,128)S(1)}, f32[192,256]{1,0:T(8,128)S(1)}) custom-call(f32[192,256]{1,0:T(8,128)S(1)} %get-tuple-element.130.values_ref, f32[96,256]{1,0:T(8,128)S(1)} %get-tuple-element.131.residual_ref, f32[96,256]{1,0:T(8,128)S(1)} %get-tuple-element.122.inverse_ref, ...), custom_call_target="tpu_custom_call" | custom-call | tf_op jit(solution)/shard_map/unshared/pallas_call | solution.py:725
  64.7 2.0 %shared.7 = (f32[24,128]{1,0:T(8,128)S(1)}, f32[24,128]{1,0:T(8,128)S(1)}, f32[24,128]{1,0:T(8,128)S(1)}, f32[192,256]{1,0:T(8,128)S(1)}, f32[24,128]{1,0:T(8,128)S(1)}) custom-call(f32[24,128]{1,0:T(8,128)S(1)} %get-tuple-element.126.message_in, f32[24,128]{1,0:T(8,128)S(1)} %collective-permute-done.6.near_in, ...), custom_call_target="tpu_custom_call" | custom-call | tf_op jit(solution)/shard_map/shared/pallas_call | solution.py:731
  66.7 4.9 %collective-permute-start.9 = (f32[24,128]{1,0:T(8,128)S(1)}, f32[24,128]{1,0:T(8,128)S(1)}, u32[]{:S(2)}, u32[]{:S(2)}) collective-permute-start(f32[24,128]{1,0:T(8,128)S(1)} %get-tuple-element.135.message_in), channel_id=1, source_target_pairs={{1,2},{2,1},{3,4},{4,3},{5,6},{6,5},{7,8},{8,7},{9,10},{10,9},{11,... | collective-permute-start | bytes 36872 | tf_op jit(solution)/shard_map/ppermute | solution.py:621
  71.6 4.2 %unshared.8 = (f32[96,256]{1,0:T(8,128)S(1)}, f32[96,256]{1,0:T(8,128)S(1)}, f32[96,256]{1,0:T(8,128)S(1)}, f32[192,256]{1,0:T(8,128)S(1)}) custom-call(f32[192,256]{1,0:T(8,128)S(1)} %get-tuple-element.139.values_ref, f32[96,256]{1,0:T(8,128)S(1)} %get-tuple-element.140.residual_ref, f32[96,256]{1,0:T(8,128)S(1)} %get-tuple-element.122.inverse_ref, ...), custom_call_target="tpu_custom_call" | custom-call | tf_op jit(solution)/shard_map/unshared/pallas_call | solution.py:725
  76.0 2.0 %shared.8 = (f32[24,128]{1,0:T(8,128)S(1)}, f32[24,128]{1,0:T(8,128)S(1)}, f32[24,128]{1,0:T(8,128)S(1)}, f32[192,256]{1,0:T(8,128)S(1)}, f32[24,128]{1,0:T(8,128)S(1)}) custom-call(f32[24,128]{1,0:T(8,128)S(1)} %get-tuple-element.135.message_in, f32[24,128]{1,0:T(8,128)S(1)} %collective-permute-done.8.near_in, ...), custom_call_target="tpu_custom_call" | custom-call | tf_op jit(solution)/shard_map/shared/pallas_call | solution.py:731
  78.0 4.9 %collective-permute-start.11 = (f32[24,128]{1,0:T(8,128)S(1)}, f32[24,128]{1,0:T(8,128)S(1)}, u32[]{:S(2)}, u32[]{:S(2)}) collective-permute-start(f32[24,128]{1,0:T(8,128)S(1)} %get-tuple-element.144.message_in), channel_id=1, source_target_pairs={{1,2},{2,1},{3,4},{4,3},{5,6},{6,5},{7,8},{8,7},{9,10},{10,9},{11,... | collective-permute-start | bytes 36872 | tf_op jit(solution)/shard_map/ppermute | solution.py:621
  82.9 4.2 %unshared.9 = (f32[96,256]{1,0:T(8,128)S(1)}, f32[96,256]{1,0:T(8,128)S(1)}, f32[96,256]{1,0:T(8,128)S(1)}, f32[192,256]{1,0:T(8,128)S(1)}) custom-call(f32[192,256]{1,0:T(8,128)S(1)} %get-tuple-element.148.values_ref, f32[96,256]{1,0:T(8,128)S(1)} %get-tuple-element.149.residual_ref, f32[96,256]{1,0:T(8,128)S(1)} %get-tuple-element.122.inverse_ref, ...), custom_call_target="tpu_custom_call" | custom-call | tf_op jit(solution)/shard_map/unshared/pallas_call | solution.py:725
  87.3 2.0 %shared.9 = (f32[24,128]{1,0:T(8,128)S(1)}, f32[24,128]{1,0:T(8,128)S(1)}, f32[24,128]{1,0:T(8,128)S(1)}, f32[192,256]{1,0:T(8,128)S(1)}, f32[24,128]{1,0:T(8,128)S(1)}) custom-call(f32[24,128]{1,0:T(8,128)S(1)} %get-tuple-element.144.message_in, f32[24,128]{1,0:T(8,128)S(1)} %collective-permute-done.10.near_in, ...), custom_call_target="tpu_custom_call" | custom-call | tf_op jit(solution)/shard_map/shared/pallas_call | solution.py:731
  89.3 5.1 %collective-permute-start.13 = (f32[24,128]{1,0:T(8,128)S(1)}, f32[24,128]{1,0:T(8,128)S(1)}, u32[]{:S(2)}, u32[]{:S(2)}) collective-permute-start(f32[24,128]{1,0:T(8,128)S(1)} %get-tuple-element.153.message_in), channel_id=1, source_target_pairs={{1,2},{2,1},{3,4},{4,3},{5,6},{6,5},{7,8},{8,7},{9,10},{10,9},{11,... | collective-permute-start | bytes 36872 | tf_op jit(solution)/shard_map/ppermute | solution.py:621
  94.5 4.2 %unshared.10 = (f32[96,256]{1,0:T(8,128)S(1)}, f32[96,256]{1,0:T(8,128)S(1)}, f32[96,256]{1,0:T(8,128)S(1)}, f32[192,256]{1,0:T(8,128)S(1)}) custom-call(f32[192,256]{1,0:T(8,128)S(1)} %get-tuple-element.157.values_ref, f32[96,256]{1,0:T(8,128)S(1)} %get-tuple-element.158.residual_ref, f32[96,256]{1,0:T(8,128)S(1)} %get-tuple-element.122.inverse_ref, ...), custom_call_target="tpu_custom_call" | custom-call | tf_op jit(solution)/shard_map/unshared/pallas_call | solution.py:725
  98.7 2.0 %shared.10 = (f32[24,128]{1,0:T(8,128)S(1)}, f32[24,128]{1,0:T(8,128)S(1)}, f32[24,128]{1,0:T(8,128)S(1)}, f32[192,256]{1,0:T(8,128)S(1)}, f32[24,128]{1,0:T(8,128)S(1)}) custom-call(f32[24,128]{1,0:T(8,128)S(1)} %get-tuple-element.153.message_in, f32[24,128]{1,0:T(8,128)S(1)} %collective-permute-done.12.near_in, ...), custom_call_target="tpu_custom_call" | custom-call | tf_op jit(solution)/shard_map/shared/pallas_call | solution.py:731
  100.8 4.9 %collective-permute-start.15 = (f32[24,128]{1,0:T(8,128)S(1)}, f32[24,128]{1,0:T(8,128)S(1)}, u32[]{:S(2)}, u32[]{:S(2)}) collective-permute-start(f32[24,128]{1,0:T(8,128)S(1)} %get-tuple-element.162.message_in), channel_id=1, source_target_pairs={{1,2},{2,1},{3,4},{4,3},{5,6},{6,5},{7,8},{8,7},{9,10},{10,9},{11,... | collective-permute-start | bytes 36872 | tf_op jit(solution)/shard_map/ppermute | solution.py:621
  105.7 4.2 %unshared.11 = (f32[96,256]{1,0:T(8,128)S(1)}, f32[96,256]{1,0:T(8,128)S(1)}, f32[96,256]{1,0:T(8,128)S(1)}, f32[192,256]{1,0:T(8,128)S(1)}) custom-call(f32[192,256]{1,0:T(8,128)S(1)} %get-tuple-element.166.values_ref, f32[96,256]{1,0:T(8,128)S(1)} %get-tuple-element.167.residual_ref, f32[96,256]{1,0:T(8,128)S(1)} %get-tuple-element.122.inverse_ref, ...), custom_call_target="tpu_custom_call" | custom-call | tf_op jit(solution)/shard_map/unshared/pallas_call | solution.py:725
  110.0 2.0 %shared.11 = (f32[24,128]{1,0:T(8,128)S(1)}, f32[24,128]{1,0:T(8,128)S(1)}, f32[24,128]{1,0:T(8,128)S(1)}, f32[192,256]{1,0:T(8,128)S(1)}, f32[24,128]{1,0:T(8,128)S(1)}) custom-call(f32[24,128]{1,0:T(8,128)S(1)} %get-tuple-element.162.message_in, f32[24,128]{1,0:T(8,128)S(1)} %collective-permute-done.14.near_in, ...), custom_call_target="tpu_custom_call" | custom-call | tf_op jit(solution)/shard_map/shared/pallas_call | solution.py:731
  112.1 4.9 %collective-permute-start.17 = (f32[24,128]{1,0:T(8,128)S(1)}, f32[24,128]{1,0:T(8,128)S(1)}, u32[]{:S(2)}, u32[]{:S(2)}) collective-permute-start(f32[24,128]{1,0:T(8,128)S(1)} %get-tuple-element.171.message_in), channel_id=1, source_target_pairs={{1,2},{2,1},{3,4},{4,3},{5,6},{6,5},{7,8},{8,7},{9,10},{10,9},{11,... | collective-permute-start | bytes 36872 | tf_op jit(solution)/shard_map/ppermute | solution.py:621
  117.0 2.1 %last_unshared.1.field_ref = f32[96,256]{1,0:T(8,128)S(1)} custom-call(f32[192,256]{1,0:T(8,128)S(1)} %get-tuple-element.175.values_ref, f32[96,256]{1,0:T(8,128)S(1)} %get-tuple-element.176.residual_ref, f32[96,256]{1,0:T(8,128)S(1)} %get-tuple-element.122.inverse_ref, f32[96,256]{1,0:T(8,128)S(1)} %get-tuple-element.177.update_ref, ...), custom_call_target="tpu_custom_call" | custom-call | tf_op jit(solution)/shard_map/last_unshared/pallas_call | solution.py:741
  119.1 2.2 %collective-permute-done.17.other_in = f32[24,128]{1,0:T(8,128)S(1)} collective-permute-done((f32[24,128]{1,0:T(8,128)S(1)}, f32[24,128]{1,0:T(8,128)S(1)}, u32[]{:S(2)}, u32[]{:S(2)}) %collective-permute-start.17) | collective-permute-done | bytes 12320 | tf_op jit(solution)/shard_map/ppermute | solution.py:621
  121.3 1.0 last_shared.1
  (25 shorter events, 1.1 us)
Async XLA Ops:
  2.8 23.2 %all-to-all-start = ((f32[128,1,256]{2,1,0:T(1,128)}), f32[128,1,256]{2,1,0:T(1,128)S(1)}, u32[]{:S(2)}, u32[]{:S(2)}) async-start(f32[128,1,256]{2,1,0:T(1,128)} %get-tuple-element.95), calls=%async_computation | async-start | bytes 262144 | tf_op jit(solution)/shard_map/all_to_all | solution.py:674
  13.2 12.6 %collective-permute-start = (f32[40,256]{1,0:T(8,128)S(1)}, f32[40,256]{1,0:T(8,128)S(1)}, u32[]{:S(2)}, u32[]{:S(2)}) collective-permute-start(f32[40,256]{1,0:T(8,128)S(1)} %get-tuple-element.96.field_message), channel_id=1, source_target_pairs={{0,1},{1,0},{2,3},{3,2},{4,5},{5,4},{6,7},{7,6},{8,9},{9,8},{10,11... | collective-permute-start | bytes 122888 | tf_op jit(solution)/shard_map/ppermute | solution.py:622
  13.4 12.5 %collective-permute-start.1 = (f32[40,256]{1,0:T(8,128)S(1)}, f32[40,256]{1,0:T(8,128)S(1)}, u32[]{:S(2)}, u32[]{:S(2)}) collective-permute-start(f32[40,256]{1,0:T(8,128)S(1)} %get-tuple-element.97), channel_id=1, source_target_pairs={{1,2},{2,1},{3,4},{4,3},{5,6},{6,5},{7,8},{8,7},{9,10},{10,9},{11,... | collective-permute-start | bytes 122888 | tf_op jit(solution)/shard_map/ppermute | solution.py:621
  32.6 9.0 %collective-permute-start.2 = (f32[48,128]{1,0:T(8,128)S(1)}, f32[48,128]{1,0:T(8,128)S(1)}, u32[]{:S(2)}, u32[]{:S(2)}) collective-permute-start(f32[48,128]{1,0:T(8,128)S(1)} %get-tuple-element.107.message_in), channel_id=1, source_target_pairs={{0,1},{1,0},{2,3},{3,2},{4,5},{5,4},{6,7},{7,6},{8,9},{9,8},{10,11... | collective-permute-start | bytes 73736 | tf_op jit(solution)/shard_map/ppermute | solution.py:622
  32.6 9.4 %collective-permute-start.3 = (f32[48,128]{1,0:T(8,128)S(1)}, f32[48,128]{1,0:T(8,128)S(1)}, u32[]{:S(2)}, u32[]{:S(2)}) collective-permute-start(f32[48,128]{1,0:T(8,128)S(1)} %get-tuple-element.107.message_in), channel_id=1, source_target_pairs={{1,2},{2,1},{3,4},{4,3},{5,6},{6,5},{7,8},{8,7},{9,10},{10,9},{11,... | collective-permute-start | bytes 73736 | tf_op jit(solution)/shard_map/ppermute | solution.py:621
  43.9 9.4 %collective-permute-start.4 = (f32[24,128]{1,0:T(8,128)S(1)}, f32[24,128]{1,0:T(8,128)S(1)}, u32[]{:S(2)}, u32[]{:S(2)}) collective-permute-start(f32[24,128]{1,0:T(8,128)S(1)} %get-tuple-element.116.message_in), channel_id=1, source_target_pairs={{0,1},{1,0},{2,3},{3,2},{4,5},{5,4},{6,7},{7,6},{8,9},{9,8},{10,11... | collective-permute-start | bytes 36872 | tf_op jit(solution)/shard_map/ppermute | solution.py:622
  44.0 9.3 %collective-permute-start.5 = (f32[24,128]{1,0:T(8,128)S(1)}, f32[24,128]{1,0:T(8,128)S(1)}, u32[]{:S(2)}, u32[]{:S(2)}) collective-permute-start(f32[24,128]{1,0:T(8,128)S(1)} %get-tuple-element.116.message_in), channel_id=1, source_target_pairs={{1,2},{2,1},{3,4},{4,3},{5,6},{6,5},{7,8},{8,7},{9,10},{10,9},{11,... | collective-permute-start | bytes 36872 | tf_op jit(solution)/shard_map/ppermute | solution.py:621
  55.4 9.2 %collective-permute-start.6 = (f32[24,128]{1,0:T(8,128)S(1)}, f32[24,128]{1,0:T(8,128)S(1)}, u32[]{:S(2)}, u32[]{:S(2)}) collective-permute-start(f32[24,128]{1,0:T(8,128)S(1)} %get-tuple-element.126.message_in), channel_id=1, source_target_pairs={{0,1},{1,0},{2,3},{3,2},{4,5},{5,4},{6,7},{7,6},{8,9},{9,8},{10,11... | collective-permute-start | bytes 36872 | tf_op jit(solution)/shard_map/ppermute | solution.py:622
  55.4 9.2 %collective-permute-start.7 = (f32[24,128]{1,0:T(8,128)S(1)}, f32[24,128]{1,0:T(8,128)S(1)}, u32[]{:S(2)}, u32[]{:S(2)}) collective-permute-start(f32[24,128]{1,0:T(8,128)S(1)} %get-tuple-element.126.message_in), channel_id=1, source_target_pairs={{1,2},{2,1},{3,4},{4,3},{5,6},{6,5},{7,8},{8,7},{9,10},{10,9},{11,... | collective-permute-start | bytes 36872 | tf_op jit(solution)/shard_map/ppermute | solution.py:621
  66.7 9.2 %collective-permute-start.8 = (f32[24,128]{1,0:T(8,128)S(1)}, f32[24,128]{1,0:T(8,128)S(1)}, u32[]{:S(2)}, u32[]{:S(2)}) collective-permute-start(f32[24,128]{1,0:T(8,128)S(1)} %get-tuple-element.135.message_in), channel_id=1, source_target_pairs={{0,1},{1,0},{2,3},{3,2},{4,5},{5,4},{6,7},{7,6},{8,9},{9,8},{10,11... | collective-permute-start | bytes 36872 | tf_op jit(solution)/shard_map/ppermute | solution.py:622
  66.7 9.2 %collective-permute-start.9 = (f32[24,128]{1,0:T(8,128)S(1)}, f32[24,128]{1,0:T(8,128)S(1)}, u32[]{:S(2)}, u32[]{:S(2)}) collective-permute-start(f32[24,128]{1,0:T(8,128)S(1)} %get-tuple-element.135.message_in), channel_id=1, source_target_pairs={{1,2},{2,1},{3,4},{4,3},{5,6},{6,5},{7,8},{8,7},{9,10},{10,9},{11,... | collective-permute-start | bytes 36872 | tf_op jit(solution)/shard_map/ppermute | solution.py:621
  78.0 9.2 %collective-permute-start.10 = (f32[24,128]{1,0:T(8,128)S(1)}, f32[24,128]{1,0:T(8,128)S(1)}, u32[]{:S(2)}, u32[]{:S(2)}) collective-permute-start(f32[24,128]{1,0:T(8,128)S(1)} %get-tuple-element.144.message_in), channel_id=1, source_target_pairs={{0,1},{1,0},{2,3},{3,2},{4,5},{5,4},{6,7},{7,6},{8,9},{9,8},{10,11... | collective-permute-start | bytes 36872 | tf_op jit(solution)/shard_map/ppermute | solution.py:622
  78.0 9.2 %collective-permute-start.11 = (f32[24,128]{1,0:T(8,128)S(1)}, f32[24,128]{1,0:T(8,128)S(1)}, u32[]{:S(2)}, u32[]{:S(2)}) collective-permute-start(f32[24,128]{1,0:T(8,128)S(1)} %get-tuple-element.144.message_in), channel_id=1, source_target_pairs={{1,2},{2,1},{3,4},{4,3},{5,6},{6,5},{7,8},{8,7},{9,10},{10,9},{11,... | collective-permute-start | bytes 36872 | tf_op jit(solution)/shard_map/ppermute | solution.py:621
  89.3 9.4 %collective-permute-start.12 = (f32[24,128]{1,0:T(8,128)S(1)}, f32[24,128]{1,0:T(8,128)S(1)}, u32[]{:S(2)}, u32[]{:S(2)}) collective-permute-start(f32[24,128]{1,0:T(8,128)S(1)} %get-tuple-element.153.message_in), channel_id=1, source_target_pairs={{0,1},{1,0},{2,3},{3,2},{4,5},{5,4},{6,7},{7,6},{8,9},{9,8},{10,11... | collective-permute-start | bytes 36872 | tf_op jit(solution)/shard_map/ppermute | solution.py:622
  89.3 9.3 %collective-permute-start.13 = (f32[24,128]{1,0:T(8,128)S(1)}, f32[24,128]{1,0:T(8,128)S(1)}, u32[]{:S(2)}, u32[]{:S(2)}) collective-permute-start(f32[24,128]{1,0:T(8,128)S(1)} %get-tuple-element.153.message_in), channel_id=1, source_target_pairs={{1,2},{2,1},{3,4},{4,3},{5,6},{6,5},{7,8},{8,7},{9,10},{10,9},{11,... | collective-permute-start | bytes 36872 | tf_op jit(solution)/shard_map/ppermute | solution.py:621
  100.7 9.2 %collective-permute-start.14 = (f32[24,128]{1,0:T(8,128)S(1)}, f32[24,128]{1,0:T(8,128)S(1)}, u32[]{:S(2)}, u32[]{:S(2)}) collective-permute-start(f32[24,128]{1,0:T(8,128)S(1)} %get-tuple-element.162.message_in), channel_id=1, source_target_pairs={{0,1},{1,0},{2,3},{3,2},{4,5},{5,4},{6,7},{7,6},{8,9},{9,8},{10,11... | collective-permute-start | bytes 36872 | tf_op jit(solution)/shard_map/ppermute | solution.py:622
  100.8 9.2 %collective-permute-start.15 = (f32[24,128]{1,0:T(8,128)S(1)}, f32[24,128]{1,0:T(8,128)S(1)}, u32[]{:S(2)}, u32[]{:S(2)}) collective-permute-start(f32[24,128]{1,0:T(8,128)S(1)} %get-tuple-element.162.message_in), channel_id=1, source_target_pairs={{1,2},{2,1},{3,4},{4,3},{5,6},{6,5},{7,8},{8,7},{9,10},{10,9},{11,... | collective-permute-start | bytes 36872 | tf_op jit(solution)/shard_map/ppermute | solution.py:621
  112.0 7.1 %collective-permute-start.16 = (f32[24,128]{1,0:T(8,128)S(1)}, f32[24,128]{1,0:T(8,128)S(1)}, u32[]{:S(2)}, u32[]{:S(2)}) collective-permute-start(f32[24,128]{1,0:T(8,128)S(1)} %get-tuple-element.171.message_in), channel_id=1, source_target_pairs={{0,1},{1,0},{2,3},{3,2},{4,5},{5,4},{6,7},{7,6},{8,9},{9,8},{10,11... | collective-permute-start | bytes 36872 | tf_op jit(solution)/shard_map/ppermute | solution.py:622
  112.1 9.2 %collective-permute-start.17 = (f32[24,128]{1,0:T(8,128)S(1)}, f32[24,128]{1,0:T(8,128)S(1)}, u32[]{:S(2)}, u32[]{:S(2)}) collective-permute-start(f32[24,128]{1,0:T(8,128)S(1)} %get-tuple-element.171.message_in), channel_id=1, source_target_pairs={{1,2},{2,1},{3,4},{4,3},{5,6},{6,5},{7,8},{8,7},{9,10},{10,9},{11,... | collective-permute-start | bytes 36872 | tf_op jit(solution)/shard_map/ppermute | solution.py:621

commit v5 on v4

--- a/solution.py
+++ b/solution.py
@@ -6,6 +6,7 @@
 from jax.experimental import pallas as pl
 from jax.experimental.pallas import tpu as pltpu
 from jax.sharding import PartitionSpec as P
+
 
 NEAR_CAP = 16
 DEGREE = 4
@@ -168,40 +169,33 @@
     lax.fori_loop(0, PER // BLOCK, block, 0)
 
 
-def scatter_shared(index_ref, hot_ref, values_ref, high_ref, low_ref, sums_ref, out_ref):
+def scatter_shared(index_ref, hot_ref, values_ref, high_ref, low_ref, out_ref):
     high, low = split(values_ref[...])
     high_ref[...] = high
     low_ref[...] = low
-    sums_ref[...] = jnp.zeros_like(sums_ref)
     lines = iota((8, 256), 0)
-
-    def block(b, carry):
-        row = pl.multiple_of(b * BLOCK, BLOCK)
-        line = index_ref[pl.ds(row, BLOCK), :] >> 7
-        left = []
-        for k in range(BLOCK):
-            here = line[k : k + 1, :] == lines
-            left.append(
-                jnp.concatenate(
-                    [
-                        jnp.where(
-                            here,
-                            jnp.broadcast_to(ref[pl.ds(c * PER + row + k, 1), :], (8, 256)),
-                            0.0,
-                        )
-                        for ref in (high_ref, low_ref)
-                        for c in range(3)
-                    ],
-                    axis=0,
-                ).astype(BF16)
-            )
-        left = jnp.concatenate(left, axis=1)
-        right = hot_ref[pl.ds(pl.multiple_of(row * 256, 256), BLOCK * 256), :]
-        sums_ref[...] += jnp.dot(left, right, preferred_element_type=F32)
-        return carry
-
-    lax.fori_loop(0, PER // BLOCK, block, 0)
-    out_ref[...] = sums_ref[0:24, :] + sums_ref[24:48, :]
+    line = index_ref[...] >> 7
+    left = []
+    for n in range(PER):
+        here = line[n : n + 1, :] == lines
+        left.append(
+            jnp.concatenate(
+                [
+                    jnp.where(
+                        here,
+                        jnp.broadcast_to(ref[c * PER + n : c * PER + n + 1, :], (8, 256)),
+                        0.0,
+                    )
+                    for ref in (high_ref, low_ref)
+                    for c in range(3)
+                ],
+                axis=0,
+            ).astype(BF16)
+        )
+    sums = jnp.dot(
+        jnp.concatenate(left, axis=1), hot_ref[...], preferred_element_type=F32
+    )
+    out_ref[...] = sums[0:24, :] + sums[24:48, :]
 
 
 def add_parts(sums_ref, first, channels):
@@ -300,9 +294,9 @@
 
 
 def pack_kernel(
-    loads_hbm, coefs_hbm, move_hbm, face_hbm, field_hbm, nodes_hbm, stiff_hbm, far_ref, near_out,
+    loads_hbm, coefs_hbm, move_hbm, face_hbm, field_hbm, nodes_hbm, stiff_hbm, far_hbm, near_out,
     other_out, places_ref, state_ref, loads_ref, coefs_ref, move_ref, nodes_ref, stiff_ref,
-    face_ref, field_ref, sems,
+    face_ref, field_ref, far_rows, sems,
 ):
     pairs = (
         (move_hbm, move_ref),
@@ -348,11 +342,13 @@
         precision=lax.Precision.HIGHEST,
         preferred_element_type=F32,
     )
-    far_ref[:, 0, :] = packed[:DEVICES]
+    far_rows[:, 0, :] = packed[:DEVICES]
+    far_copy = pltpu.make_async_copy(far_rows, far_hbm, sems.at[7])
+    far_copy.start()
     near_out[0:NEAR_CAP, :] = packed[DEVICES : DEVICES + NEAR_CAP]
     other_out[0:NEAR_CAP, :] = packed[DEVICES + NEAR_CAP :]
     near_out[NEAR_CAP:, :] = jnp.zeros((24, 256), F32)
-    for copy in copies[3:]:
+    for copy in copies[3:5]:
         copy.wait()
     places_ref[...] = jnp.zeros((8, 128), jnp.int32)
     places_ref[0:1, :] = face_ref[0:1, 0:128]
@@ -365,6 +361,9 @@
             state_ref[32 * c + h : 32 * c + h + 1, :] = field_ref[c : c + 1, 256 * h : 256 * h + 256]
     take_shared(state_ref, places_ref[...], near_out, NEAR_CAP, False)
     other_out[NEAR_CAP:, :] = near_out[NEAR_CAP:, :]
+    for copy in copies[5:]:
+        copy.wait()
+    far_copy.wait()
 
 
 def index_kernel(
@@ -375,8 +374,7 @@
     index_ref,
     shared_index_ref,
     unshared_ref,
-    high_ref,
-    low_ref,
+    blocks_ref,
     gathered_ref,
     positions,
     found,
@@ -397,8 +395,10 @@
     )
     for i in range(2):
         high, low = split(stiff_ref[i])
-        high_ref[DOFS * i : DOFS * i + DOFS, :] = high.astype(BF16)
-        low_ref[DOFS * i : DOFS * i + DOFS, :] = low.astype(BF16)
+        high = high.astype(BF16)
+        blocks_ref[DOFS * i : DOFS * i + DOFS, :] = jnp.concatenate(
+            [low.astype(BF16), high, high], axis=1
+        )
 
 
 def build_hot(index_ref, hot_ref, width):
@@ -416,14 +416,12 @@
                 hot_ref[top : top + 16, :] = jnp.where(column == lanes, one, zero)
 
 
-def multiply_blocks(high_ref, low_ref, rows_ref):
+def multiply_blocks(blocks_ref, rows_ref):
     high, low = split(rows_ref[...])
     high = high.astype(BF16)
     low = low.astype(BF16)
-    return (
-        jnp.dot(low_ref[...], high, preferred_element_type=F32)
-        + jnp.dot(high_ref[...], low, preferred_element_type=F32)
-        + jnp.dot(high_ref[...], high, preferred_element_type=F32)
+    return jnp.dot(
+        blocks_ref[...], jnp.concatenate([high, low, high], axis=0), preferred_element_type=F32
     )
 
 
@@ -440,8 +438,7 @@
     nodes_ref,
     shared_index_ref,
     places_ref,
-    high_ref,
-    low_ref,
+    blocks_ref,
     hot_ref,
     moved_loads,
     moved_coefs,
@@ -455,10 +452,12 @@
     value_high,
     value_low,
     sums,
+    kept_loads,
+    sems,
 ):
     shared_field[...] = field_message[NEAR_CAP:, 0:128] + from_neighbours(near_in, other_in, NEAR_CAP)
     gather_shared(shared_field, shared_index_ref, gathered_in, gathered, 3)
-    products = multiply_blocks(high_ref, low_ref, gathered)
+    products = multiply_blocks(blocks_ref, gathered)
     me = lax.axis_index(AXES)
     received = jnp.concatenate(
         [far_ref[:, 0, :], near_in[0:NEAR_CAP, :], other_in[0:NEAR_CAP, :]], axis=0
@@ -476,9 +475,14 @@
     stays = move_ref[0:1, :] == me
     loads = jnp.where(stays, loads_ref[...], 0.0) + arrived[:DOFS]
     coefs = jnp.where(stays, coefs_ref[...], 0.0) + arrived[DOFS : DOFS + 2]
-    moved_loads[...] = loads
-    moved_coefs[...] = coefs
+    kept_loads[...] = loads
     coefs_out[...] = coefs
+    copies = (
+        pltpu.make_async_copy(kept_loads, moved_loads, sems.at[0]),
+        pltpu.make_async_copy(coefs_out, moved_coefs, sems.at[1]),
+    )
+    for copy in copies:
+        copy.start()
     values[0:DOFS, :] = loads - (products[:DOFS] * coefs[0:1, :] + products[DOFS:] * coefs[1:2, :])
     eye = iota((DOFS, DOFS), 0) == iota((DOFS, DOFS), 1)
     first_diag = jnp.sum(jnp.where(eye, stiff_ref[0], 0.0), axis=1, keepdims=True)
@@ -490,16 +494,18 @@
     diagonal_ref[...] = add_parts(sums, 3, 6)
     take_shared(partial_ref, places_ref[...], message, 0, True)
     take_shared(diagonal_ref, places_ref[...], message, 24, True)
+    for copy in copies:
+        copy.wait()
 
 
 def apply_operator(
-    shared_update, gathered_in, shared_index_ref, coefs_ref, hot_ref, high_ref, low_ref, values_ref,
-    message, gathered, value_high, value_low, sums,
+    shared_update, gathered_in, shared_index_ref, coefs_ref, hot_ref, blocks_ref, values_ref,
+    message, gathered, value_high, value_low,
 ):
     gather_shared(shared_update, shared_index_ref, gathered_in, gathered, 0)
-    products = multiply_blocks(high_ref, low_ref, gathered)
+    products = multiply_blocks(blocks_ref, gathered)
     values_ref[...] = products[:DOFS] * coefs_ref[0:1, :] + products[DOFS:] * coefs_ref[1:2, :]
-    scatter_shared(shared_index_ref, hot_ref, values_ref, value_high, value_low, sums, message)
+    scatter_shared(shared_index_ref, hot_ref, values_ref, value_high, value_low, message)
 
 
 def inverse_of(diagonal):
@@ -522,7 +528,8 @@
 
 def begin_shared(
     step, message_in, near_in, other_in, shared_field, gathered_in, shared_index_ref, coefs_ref,
-    hot_ref, high_ref, low_ref, residual_out, inverse_out, update_out, field_out, values_ref, message, gathered, value_high, value_low, sums,
+    hot_ref, blocks_ref, residual_out, inverse_out, update_out, field_out, values_ref, message,
+    gathered, value_high, value_low,
 ):
     residual = message_in[0:24, :] + from_neighbours(near_in, other_in, 0)
     inverse = inverse_of(message_in[24:48, :] + from_neighbours(near_in, other_in, 24))
@@ -532,8 +539,8 @@
     update_out[...] = update
     field_out[...] = shared_field[...] + update
     apply_operator(
-        update_out, gathered_in, shared_index_ref, coefs_ref, hot_ref, high_ref, low_ref, values_ref,
-        message, gathered, value_high, value_low, sums,
+        update_out, gathered_in, shared_index_ref, coefs_ref, hot_ref, blocks_ref, values_ref,
+        message, gathered, value_high, value_low,
     )
 
 
@@ -557,8 +564,8 @@
 
 def step_shared(
     step, message_in, near_in, other_in, residual_ref, inverse_ref, update_ref, field_ref,
-    gathered_in, shared_index_ref, coefs_ref, hot_ref, high_ref, low_ref, residual_out, update_out,
-    field_out, values_ref, message, gathered, value_high, value_low, sums,
+    gathered_in, shared_index_ref, coefs_ref, hot_ref, blocks_ref, residual_out, update_out,
+    field_out, values_ref, message, gathered, value_high, value_low,
 ):
     residual = residual_ref[...] - (message_in[...] + from_neighbours(near_in, other_in, 0))
     update = next_update(step, residual, inverse_ref[...], update_ref[...])
@@ -566,8 +573,8 @@
     update_out[...] = update
     field_out[...] = field_ref[...] + update
     apply_operator(
-        update_out, gathered_in, shared_index_ref, coefs_ref, hot_ref, high_ref, low_ref, values_ref,
-        message, gathered, value_high, value_low, sums,
+        update_out, gathered_in, shared_index_ref, coefs_ref, hot_ref, blocks_ref, values_ref,
+        message, gathered, value_high, value_low,
     )
 
 
@@ -623,13 +630,12 @@
     return near, other
 
 
-def call(kernel, name, outs, scratch=(), **options):
+def call(kernel, outs, scratch=(), **options):
     return pl.pallas_call(
         kernel,
         out_shape=outs,
         scratch_shapes=list(scratch),
         compiler_params=pltpu.CompilerParams(vmem_limit_bytes=20 << 20),
-        name=name,
         **options,
     )
 
@@ -649,7 +655,6 @@
     integers = functools.partial(shaped, dtype=jnp.int32)
     far, near, other, places, field, loads, coefs, moves, nodes, stiff = call(
         pack_kernel,
-        "pack",
         (
             shaped(DEVICES, 1, 256),
             shaped(40, 256),
@@ -665,29 +670,29 @@
         [
             pltpu.VMEM((2, FACE), jnp.int32),
             pltpu.VMEM((3, OWN), F32),
-            pltpu.SemaphoreType.DMA((7,)),
+            pltpu.VMEM((DEVICES, 1, 256), F32),
+            pltpu.SemaphoreType.DMA((8,)),
         ],
         in_specs=[pl.BlockSpec(memory_space=pltpu.HBM)] * 7,
+        out_specs=[pl.BlockSpec(memory_space=pltpu.HBM)]
+        + [pl.BlockSpec(memory_space=pltpu.VMEM)] * 9,
     )(*[pltpu.with_memory_space_constraint(x, pltpu.HBM) for x in (element_loads, element_coefs, move_list, face_nodes, start_field, element_nodes, stiffness)])
     field_message = near
     near, other = exchange(near, other)
     far = lax.all_to_all(far, AXES, split_axis=0, concat_axis=0, tiled=True)
-    nodes, shared_index, unshared, high, low, gathered = call(
+    nodes, shared_index, unshared, blocks, gathered = call(
         index_kernel,
-        "index",
         (
             integers(PER, ELEM),
             integers(PER, ELEM),
             shaped(32, 256),
-            shaped(2 * DOFS, DOFS, dtype=BF16),
-            shaped(2 * DOFS, DOFS, dtype=BF16),
+            shaped(2 * DOFS, 3 * DOFS, dtype=BF16),
             ELEMENT_ROWS,
         ),
         [rows(32), rows(PER)],
     )(field, places, nodes, stiff)
     hot, moved_loads, moved_coefs, coefs, partial, diagonal, shared_field, message = call(
         place_kernel,
-        "place",
         (
             shaped(PER * ELEM, 256, dtype=BF16),
             ELEMENT_ROWS,
@@ -698,25 +703,27 @@
             SHARED,
             shaped(48, 128),
         ),
-        [rows(DOFS), rows(2 * DOFS), rows(2 * DOFS), rows(2 * DOFS), rows(384)],
+        [rows(DOFS), rows(2 * DOFS), rows(2 * DOFS), rows(2 * DOFS), rows(384), rows(DOFS)]
+        + [pltpu.SemaphoreType.DMA((2,))],
+        out_specs=[
+            pl.BlockSpec(memory_space=pltpu.HBM if i in (1, 2) else pltpu.VMEM) for i in range(8)
+        ],
     )(
         loads, coefs, moves, far, near, other, field_message, stiff,
-        gathered, nodes, shared_index, places, high, low,
+        gathered, nodes, shared_index, places, blocks,
     )
     near, other = exchange(message, message)
     plan = steps()
-    scratch = [rows(DOFS)] * 3 + [pltpu.VMEM((48, 128), F32)]
+    scratch = [rows(DOFS)] * 3
     window_scratch = [rows(DOFS)] * 2 + [rows(192)]
     residual = partial
     inverse, update, field, gathered, hot_shared = call(
         functools.partial(begin_unshared, plan[0]),
-        "begin_unshared",
         (STATE, STATE, STATE, ELEMENT_ROWS, shaped(PER * ELEM, 128, dtype=BF16)),
     )(partial, diagonal, unshared, field, nodes, hot, shared_index)
-    fixed = (shared_index, coefs, hot_shared, high, low)
+    fixed = (shared_index, coefs, hot_shared, blocks)
     shared_residual, shared_inverse, shared_update, shared_field, values, message = call(
         functools.partial(begin_shared, plan[0]),
-        "begin_shared",
         (SHARED, SHARED, SHARED, SHARED, ELEMENT_ROWS, SHARED),
         scratch,
     )(message, near, other, shared_field, gathered, *fixed)
@@ -724,13 +731,11 @@
         near, other = exchange(message, message)
         residual, update, field, gathered = call(
             functools.partial(step_unshared, step),
-            "unshared",
             (STATE, STATE, STATE, ELEMENT_ROWS),
             window_scratch,
         )(values, residual, inverse, update, field, nodes, hot)
         shared_residual, shared_update, shared_field, values, message = call(
             functools.partial(step_shared, step),
-            "shared",
             (SHARED, SHARED, SHARED, ELEMENT_ROWS, SHARED),
             scratch,
         )(
@@ -739,9 +744,9 @@
         )
     near, other = exchange(message, message)
     field = call(
-        functools.partial(last_unshared, plan[-1]), "last_unshared", STATE, window_scratch
+        functools.partial(last_unshared, plan[-1]), STATE, window_scratch
     )(values, residual, inverse, update, field, nodes, hot)
-    field = call(functools.partial(last_shared, plan[-1]), "last_shared", shaped(3, OWN))(
+    field = call(functools.partial(last_shared, plan[-1]), shaped(3, OWN))(
         message, near, other, shared_residual, shared_inverse, shared_update, shared_field, field,
         unshared, places,
     )

time: 123 us -> 125 us (1.016)
  Pallas kernels: 59.6 us -> 61.6 us
    pallas_call x19, Pallas kernels: 59.6 us -> 61.6 us  [the longest x6 25.3 us: local(): call(functools.partial(step_unshared, step), (STATE, STATE, STATE, ELEMEN...]
where the time goes in v5:
time: 125 us; the launch traced here: 124 us
  Pallas kernels  61.6 us (49%)
  starting transfers between devices  58.7 us (47%)
  waiting for transfers between devices  3.09 us (2%)
    ppermute x9, starting transfers between devices, exchange(): other = lax.ppermute(other_message, AXES, OTHER_PAIRS)  47.3 us
    pallas_call x6, Pallas kernels, local(): call(functools.partial(step_unshared, step), (STATE, STATE, STATE, ELEMEN...  25.3 us
    pallas_call x6, Pallas kernels, local(): call(functools.partial(step_shared, step), (SHARED, SHARED, SHARED, ELEME...  13.8 us
    all_to_all x1, starting transfers between devices, local(): far = lax.all_to_all(far, AXES, split_axis=0, concat_axis=0, tiled=True)  10.5 us
    pallas_call x1, Pallas kernels, local(): call(place_kernel, (shaped(PER * ELEM, 256, dtype=BF16), ELEMENT_ROWS, sh...  6.39 us
    pallas_call x1, Pallas kernels, local(): call(index_kernel, (integers(PER, ELEM), integers(PER, ELEM), shaped(32,...  4.62 us
    pallas_call x1, Pallas kernels, local(): call(functools.partial(begin_unshared, plan[0]), (STATE, STATE, STATE, EL...  4.07 us
    ppermute x9, waiting for transfers between devices, exchange(): other = lax.ppermute(other_message, AXES, OTHER_PAIRS)  3.06 us
  transfers between devices with their start and end apart: 19, of which 6 were waited for; matrix products, arithmetic and copies ran while one was open for 0% of the time, Pallas kernels for 29%

profile of v5, /device:TPU:6, one launch (start us, length us, event | category | flops | bytes accessed | tf_op | source)
XLA Modules:
  0.0 124.4 jit_solution(6816824374208340634)
XLA Ops:
  0.6 2.0 %shard_map.94 = (f32[128,1,256]{2,1,0:T(1,128)}, f32[40,256]{1,0:T(8,128)S(1)}, f32[40,256]{1,0:T(8,128)S(1)}, s32[8,128]{1,0:T(8,128)S(1)}, f32[96,256]{1,0:T(8...) custom-call(f32[192,256]{1,0:T(8,128)} %loads_hbm.1, ...), custom_call_target="tpu_custom_call" | custom-call | tf_op jit(solution)/shard_map/pallas_call | solution.py:656
  2.7 10.5 %all-to-all-start = ((f32[128,1,256]{2,1,0:T(1,128)}), f32[128,1,256]{2,1,0:T(1,128)S(1)}, u32[]{:S(2)}, u32[]{:S(2)}) async-start(f32[128,1,256]{2,1,0:T(1,128)} %get-tuple-element.94), calls=%async_computation | async-start | bytes 262144 | tf_op jit(solution)/shard_map/all_to_all | solution.py:682
  13.2 0.2 collective-permute-start
  13.4 7.9 %collective-permute-start.1 = (f32[40,256]{1,0:T(8,128)S(1)}, f32[40,256]{1,0:T(8,128)S(1)}, u32[]{:S(2)}, u32[]{:S(2)}) collective-permute-start(f32[40,256]{1,0:T(8,128)S(1)} %get-tuple-element.96), channel_id=1, source_target_pairs={{1,2},{2,1},{3,4},{4,3},{5,6},{6,5},{7,8},{8,7},{9,10},{10,9},{11,... | collective-permute-start | bytes 122888 | tf_op jit(solution)/shard_map/ppermute | solution.py:628
  21.2 4.6 %shard_map.95 = (s32[64,256]{1,0:T(8,128)S(1)}, s32[64,256]{1,0:T(8,128)S(1)}, f32[32,256]{1,0:T(8,128)S(1)}, bf16[384,576]{1,0:T(8,128)(2,1)S(1)}, f32[192,256]{1,0:T(8,128)S(1)}) custom-call(f32[96,256]{1,0:T(8,128)S(1)} %get-tuple-element.98.state_ref.field_ref, s32[8,128]{1,0:T(8,128)S(1)} %get-tuple-element.99.places_ref, ...), custom_call_target="tpu_custom_call" | custom-call | tf_op jit(solution)/shard_map/pallas_call | solution.py:683
  25.9 6.4 %shard_map.96 = (bf16[16384,256]{1,0:T(8,128)(2,1)S(1)}, f32[192,256]{1,0:T(8,128)}, f32[2,256]{1,0:T(2,128)}, f32[2,256]{1,0:T(2,128)S(1)}, f32[96,256]{1,0:T(8...) custom-call(f32[192,256]{1,0:T(8,128)S(1)} %get-tuple-element.91.loads_ref, ...), custom_call_target="tpu_custom_call" | custom-call | tf_op jit(solution)/shard_map/pallas_call | solution.py:694
  32.4 4.9 %collective-permute-start.3 = (f32[48,128]{1,0:T(8,128)S(1)}, f32[48,128]{1,0:T(8,128)S(1)}, u32[]{:S(2)}, u32[]{:S(2)}) collective-permute-start(f32[48,128]{1,0:T(8,128)S(1)} %get-tuple-element.105.message_in), channel_id=1, source_target_pairs={{1,2},{2,1},{3,4},{4,3},{5,6},{6,5},{7,8},{8,7},{9,10},{10,9},{11,... | collective-permute-start | bytes 73736 | tf_op jit(solution)/shard_map/ppermute | solution.py:628
  37.3 4.1 %shard_map.97 = (f32[96,256]{1,0:T(8,128)S(1)}, f32[96,256]{1,0:T(8,128)S(1)}, f32[96,256]{1,0:T(8,128)S(1)}, f32[192,256]{1,0:T(8,128)S(1)}, bf16[16384,128]{1,0:T(8,128)(2,1)S(1)}) custom-call(f32[96,256]{1,0:T(8,128)S(1)} %get-tuple-element.107.partial_ref.residual_ref, f32[96,256]{1,0:T(8,128)S(1)} %get-tuple-element.108.diagonal_ref, ...), custom_call_target="tpu_custom_call" | custom-call | tf_op jit(solution)/shard_map/pallas_call | solution.py:720
  41.4 0.4 collective-permute-done.3.other_in
  41.7 2.3 %shard_map.98 = (f32[24,128]{1,0:T(8,128)S(1)}, f32[24,128]{1,0:T(8,128)S(1)}, f32[24,128]{1,0:T(8,128)S(1)}, f32[24,128]{1,0:T(8,128)S(1)}, f32[192,256]{1,0:T(8,128)S(1)}, /*index=5*/f32[24,128]{1,0:T(8,128)S(1)}) custom-call(f32[48,128]{1,0:T(8,128)S(1)} %get-tuple-element.105.message_in, f32[48,128]{1,0:T(8,128)S(1)} %collective-permute-done.2.near_in, ...), custom_call_target="tpu_custom_call" | custom-call | tf_op jit(solution)/shard_map/pallas_call | solution.py:725
  44.2 5.1 %collective-permute-start.5 = (f32[24,128]{1,0:T(8,128)S(1)}, f32[24,128]{1,0:T(8,128)S(1)}, u32[]{:S(2)}, u32[]{:S(2)}) collective-permute-start(f32[24,128]{1,0:T(8,128)S(1)} %get-tuple-element.114.message_in), channel_id=1, source_target_pairs={{1,2},{2,1},{3,4},{4,3},{5,6},{6,5},{7,8},{8,7},{9,10},{10,9},{11,... | collective-permute-start | bytes 36872 | tf_op jit(solution)/shard_map/ppermute | solution.py:628
  49.2 4.2 %shard_map.99 = (f32[96,256]{1,0:T(8,128)S(1)}, f32[96,256]{1,0:T(8,128)S(1)}, f32[96,256]{1,0:T(8,128)S(1)}, f32[192,256]{1,0:T(8,128)S(1)}) custom-call(f32[192,256]{1,0:T(8,128)S(1)} %get-tuple-element.119.values_ref, f32[96,256]{1,0:T(8,128)S(1)} %get-tuple-element.107.partial_ref.residual_ref, f32[96,256]{1,0:T(8,128)S(1)} %get-tuple-element.120.inverse_ref, ...), custom_call_target="tpu_custom_call" | custom-call | tf_op jit(solution)/shard_map/pallas_call | solution.py:732
  53.5 2.3 %shard_map.100 = (f32[24,128]{1,0:T(8,128)S(1)}, f32[24,128]{1,0:T(8,128)S(1)}, f32[24,128]{1,0:T(8,128)S(1)}, f32[192,256]{1,0:T(8,128)S(1)}, f32[24,128]{1,0:T(8,128)S(1)}) custom-call(f32[24,128]{1,0:T(8,128)S(1)} %get-tuple-element.114.message_in, f32[24,128]{1,0:T(8,128)S(1)} %collective-permute-done.4.near_in, ...), custom_call_target="tpu_custom_call" | custom-call | tf_op jit(solution)/shard_map/pallas_call | solution.py:737
  55.9 4.9 %collective-permute-start.7 = (f32[24,128]{1,0:T(8,128)S(1)}, f32[24,128]{1,0:T(8,128)S(1)}, u32[]{:S(2)}, u32[]{:S(2)}) collective-permute-start(f32[24,128]{1,0:T(8,128)S(1)} %get-tuple-element.124.message_in), channel_id=1, source_target_pairs={{1,2},{2,1},{3,4},{4,3},{5,6},{6,5},{7,8},{8,7},{9,10},{10,9},{11,... | collective-permute-start | bytes 36872 | tf_op jit(solution)/shard_map/ppermute | solution.py:628
  60.8 4.2 %shard_map.101 = (f32[96,256]{1,0:T(8,128)S(1)}, f32[96,256]{1,0:T(8,128)S(1)}, f32[96,256]{1,0:T(8,128)S(1)}, f32[192,256]{1,0:T(8,128)S(1)}) custom-call(f32[192,256]{1,0:T(8,128)S(1)} %get-tuple-element.128.values_ref, f32[96,256]{1,0:T(8,128)S(1)} %get-tuple-element.129.residual_ref, f32[96,256]{1,0:T(8,128)S(1)} %get-tuple-element.120.inverse_ref, ...), custom_call_target="tpu_custom_call" | custom-call | tf_op jit(solution)/shard_map/pallas_call | solution.py:732
  65.1 2.3 %shard_map.102 = (f32[24,128]{1,0:T(8,128)S(1)}, f32[24,128]{1,0:T(8,128)S(1)}, f32[24,128]{1,0:T(8,128)S(1)}, f32[192,256]{1,0:T(8,128)S(1)}, f32[24,128]{1,0:T(8,128)S(1)}) custom-call(f32[24,128]{1,0:T(8,128)S(1)} %get-tuple-element.124.message_in, f32[24,128]{1,0:T(8,128)S(1)} %collective-permute-done.6.near_in, ...), custom_call_target="tpu_custom_call" | custom-call | tf_op jit(solution)/shard_map/pallas_call | solution.py:737
  67.5 4.9 %collective-permute-start.9 = (f32[24,128]{1,0:T(8,128)S(1)}, f32[24,128]{1,0:T(8,128)S(1)}, u32[]{:S(2)}, u32[]{:S(2)}) collective-permute-start(f32[24,128]{1,0:T(8,128)S(1)} %get-tuple-element.133.message_in), channel_id=1, source_target_pairs={{1,2},{2,1},{3,4},{4,3},{5,6},{6,5},{7,8},{8,7},{9,10},{10,9},{11,... | collective-permute-start | bytes 36872 | tf_op jit(solution)/shard_map/ppermute | solution.py:628
  72.4 4.2 %shard_map.103 = (f32[96,256]{1,0:T(8,128)S(1)}, f32[96,256]{1,0:T(8,128)S(1)}, f32[96,256]{1,0:T(8,128)S(1)}, f32[192,256]{1,0:T(8,128)S(1)}) custom-call(f32[192,256]{1,0:T(8,128)S(1)} %get-tuple-element.137.values_ref, f32[96,256]{1,0:T(8,128)S(1)} %get-tuple-element.138.residual_ref, f32[96,256]{1,0:T(8,128)S(1)} %get-tuple-element.120.inverse_ref, ...), custom_call_target="tpu_custom_call" | custom-call | tf_op jit(solution)/shard_map/pallas_call | solution.py:732
  76.7 2.3 %shard_map.104 = (f32[24,128]{1,0:T(8,128)S(1)}, f32[24,128]{1,0:T(8,128)S(1)}, f32[24,128]{1,0:T(8,128)S(1)}, f32[192,256]{1,0:T(8,128)S(1)}, f32[24,128]{1,0:T(8,128)S(1)}) custom-call(f32[24,128]{1,0:T(8,128)S(1)} %get-tuple-element.133.message_in, f32[24,128]{1,0:T(8,128)S(1)} %collective-permute-done.8.near_in, ...), custom_call_target="tpu_custom_call" | custom-call | tf_op jit(solution)/shard_map/pallas_call | solution.py:737
  79.1 5.1 %collective-permute-start.11 = (f32[24,128]{1,0:T(8,128)S(1)}, f32[24,128]{1,0:T(8,128)S(1)}, u32[]{:S(2)}, u32[]{:S(2)}) collective-permute-start(f32[24,128]{1,0:T(8,128)S(1)} %get-tuple-element.142.message_in), channel_id=1, source_target_pairs={{1,2},{2,1},{3,4},{4,3},{5,6},{6,5},{7,8},{8,7},{9,10},{10,9},{11,... | collective-permute-start | bytes 36872 | tf_op jit(solution)/shard_map/ppermute | solution.py:628
  84.3 4.2 %shard_map.105 = (f32[96,256]{1,0:T(8,128)S(1)}, f32[96,256]{1,0:T(8,128)S(1)}, f32[96,256]{1,0:T(8,128)S(1)}, f32[192,256]{1,0:T(8,128)S(1)}) custom-call(f32[192,256]{1,0:T(8,128)S(1)} %get-tuple-element.146.values_ref, f32[96,256]{1,0:T(8,128)S(1)} %get-tuple-element.147.residual_ref, f32[96,256]{1,0:T(8,128)S(1)} %get-tuple-element.120.inverse_ref, ...), custom_call_target="tpu_custom_call" | custom-call | tf_op jit(solution)/shard_map/pallas_call | solution.py:732
  88.5 2.3 %shard_map.106 = (f32[24,128]{1,0:T(8,128)S(1)}, f32[24,128]{1,0:T(8,128)S(1)}, f32[24,128]{1,0:T(8,128)S(1)}, f32[192,256]{1,0:T(8,128)S(1)}, f32[24,128]{1,0:T(8,128)S(1)}) custom-call(f32[24,128]{1,0:T(8,128)S(1)} %get-tuple-element.142.message_in, f32[24,128]{1,0:T(8,128)S(1)} %collective-permute-done.10.near_in, ...), custom_call_target="tpu_custom_call" | custom-call | tf_op jit(solution)/shard_map/pallas_call | solution.py:737
  90.9 4.9 %collective-permute-start.13 = (f32[24,128]{1,0:T(8,128)S(1)}, f32[24,128]{1,0:T(8,128)S(1)}, u32[]{:S(2)}, u32[]{:S(2)}) collective-permute-start(f32[24,128]{1,0:T(8,128)S(1)} %get-tuple-element.151.message_in), channel_id=1, source_target_pairs={{1,2},{2,1},{3,4},{4,3},{5,6},{6,5},{7,8},{8,7},{9,10},{10,9},{11,... | collective-permute-start | bytes 36872 | tf_op jit(solution)/shard_map/ppermute | solution.py:628
  95.8 4.2 %shard_map.107 = (f32[96,256]{1,0:T(8,128)S(1)}, f32[96,256]{1,0:T(8,128)S(1)}, f32[96,256]{1,0:T(8,128)S(1)}, f32[192,256]{1,0:T(8,128)S(1)}) custom-call(f32[192,256]{1,0:T(8,128)S(1)} %get-tuple-element.155.values_ref, f32[96,256]{1,0:T(8,128)S(1)} %get-tuple-element.156.residual_ref, f32[96,256]{1,0:T(8,128)S(1)} %get-tuple-element.120.inverse_ref, ...), custom_call_target="tpu_custom_call" | custom-call | tf_op jit(solution)/shard_map/pallas_call | solution.py:732
  100.2 2.3 %shard_map.108 = (f32[24,128]{1,0:T(8,128)S(1)}, f32[24,128]{1,0:T(8,128)S(1)}, f32[24,128]{1,0:T(8,128)S(1)}, f32[192,256]{1,0:T(8,128)S(1)}, f32[24,128]{1,0:T(8,128)S(1)}) custom-call(f32[24,128]{1,0:T(8,128)S(1)} %get-tuple-element.151.message_in, f32[24,128]{1,0:T(8,128)S(1)} %collective-permute-done.12.near_in, ...), custom_call_target="tpu_custom_call" | custom-call | tf_op jit(solution)/shard_map/pallas_call | solution.py:737
  102.6 4.9 %collective-permute-start.15 = (f32[24,128]{1,0:T(8,128)S(1)}, f32[24,128]{1,0:T(8,128)S(1)}, u32[]{:S(2)}, u32[]{:S(2)}) collective-permute-start(f32[24,128]{1,0:T(8,128)S(1)} %get-tuple-element.160.message_in), channel_id=1, source_target_pairs={{1,2},{2,1},{3,4},{4,3},{5,6},{6,5},{7,8},{8,7},{9,10},{10,9},{11,... | collective-permute-start | bytes 36872 | tf_op jit(solution)/shard_map/ppermute | solution.py:628
  107.4 4.2 %shard_map.109 = (f32[96,256]{1,0:T(8,128)S(1)}, f32[96,256]{1,0:T(8,128)S(1)}, f32[96,256]{1,0:T(8,128)S(1)}, f32[192,256]{1,0:T(8,128)S(1)}) custom-call(f32[192,256]{1,0:T(8,128)S(1)} %get-tuple-element.164.values_ref, f32[96,256]{1,0:T(8,128)S(1)} %get-tuple-element.165.residual_ref, f32[96,256]{1,0:T(8,128)S(1)} %get-tuple-element.120.inverse_ref, ...), custom_call_target="tpu_custom_call" | custom-call | tf_op jit(solution)/shard_map/pallas_call | solution.py:732
  111.8 2.3 %shard_map.110 = (f32[24,128]{1,0:T(8,128)S(1)}, f32[24,128]{1,0:T(8,128)S(1)}, f32[24,128]{1,0:T(8,128)S(1)}, f32[192,256]{1,0:T(8,128)S(1)}, f32[24,128]{1,0:T(8,128)S(1)}) custom-call(f32[24,128]{1,0:T(8,128)S(1)} %get-tuple-element.160.message_in, f32[24,128]{1,0:T(8,128)S(1)} %collective-permute-done.14.near_in, ...), custom_call_target="tpu_custom_call" | custom-call | tf_op jit(solution)/shard_map/pallas_call | solution.py:737
  114.2 4.9 %collective-permute-start.17 = (f32[24,128]{1,0:T(8,128)S(1)}, f32[24,128]{1,0:T(8,128)S(1)}, u32[]{:S(2)}, u32[]{:S(2)}) collective-permute-start(f32[24,128]{1,0:T(8,128)S(1)} %get-tuple-element.169.message_in), channel_id=1, source_target_pairs={{1,2},{2,1},{3,4},{4,3},{5,6},{6,5},{7,8},{8,7},{9,10},{10,9},{11,... | collective-permute-start | bytes 36872 | tf_op jit(solution)/shard_map/ppermute | solution.py:628
  119.1 2.1 %shard_map.111.field_ref = f32[96,256]{1,0:T(8,128)S(1)} custom-call(f32[192,256]{1,0:T(8,128)S(1)} %get-tuple-element.173.values_ref, f32[96,256]{1,0:T(8,128)S(1)} %get-tuple-element.174.residual_ref, f32[96,256]{1,0:T(8,128)S(1)} %get-tuple-element.120.inverse_ref, f32[96,256]{1,0:T(8,128)S(1)} %get-tuple-element.175.update_ref, ...), custom_call_target="tpu_custom_call" | custom-call | tf_op jit(solution)/shard_map/pallas_call | solution.py:746
  121.2 2.3 %collective-permute-done.17.other_in = f32[24,128]{1,0:T(8,128)S(1)} collective-permute-done((f32[24,128]{1,0:T(8,128)S(1)}, f32[24,128]{1,0:T(8,128)S(1)}, u32[]{:S(2)}, u32[]{:S(2)}) %collective-permute-start.17) | collective-permute-done | bytes 12320 | tf_op jit(solution)/shard_map/ppermute | solution.py:628
  123.4 1.0 shard_map.112
  (25 shorter events, 1.1 us)
Async XLA Ops:
  2.7 23.2 %all-to-all-start = ((f32[128,1,256]{2,1,0:T(1,128)}), f32[128,1,256]{2,1,0:T(1,128)S(1)}, u32[]{:S(2)}, u32[]{:S(2)}) async-start(f32[128,1,256]{2,1,0:T(1,128)} %get-tuple-element.94), calls=%async_computation | async-start | bytes 262144 | tf_op jit(solution)/shard_map/all_to_all | solution.py:682
  13.2 12.7 %collective-permute-start = (f32[40,256]{1,0:T(8,128)S(1)}, f32[40,256]{1,0:T(8,128)S(1)}, u32[]{:S(2)}, u32[]{:S(2)}) collective-permute-start(f32[40,256]{1,0:T(8,128)S(1)} %get-tuple-element.95.field_message), channel_id=1, source_target_pairs={{0,1},{1,0},{2,3},{3,2},{4,5},{5,4},{6,7},{7,6},{8,9},{9,8},{10,11... | collective-permute-start | bytes 122888 | tf_op jit(solution)/shard_map/ppermute | solution.py:629
  13.4 12.5 %collective-permute-start.1 = (f32[40,256]{1,0:T(8,128)S(1)}, f32[40,256]{1,0:T(8,128)S(1)}, u32[]{:S(2)}, u32[]{:S(2)}) collective-permute-start(f32[40,256]{1,0:T(8,128)S(1)} %get-tuple-element.96), channel_id=1, source_target_pairs={{1,2},{2,1},{3,4},{4,3},{5,6},{6,5},{7,8},{8,7},{9,10},{10,9},{11,... | collective-permute-start | bytes 122888 | tf_op jit(solution)/shard_map/ppermute | solution.py:628
  32.3 9.1 %collective-permute-start.2 = (f32[48,128]{1,0:T(8,128)S(1)}, f32[48,128]{1,0:T(8,128)S(1)}, u32[]{:S(2)}, u32[]{:S(2)}) collective-permute-start(f32[48,128]{1,0:T(8,128)S(1)} %get-tuple-element.105.message_in), channel_id=1, source_target_pairs={{0,1},{1,0},{2,3},{3,2},{4,5},{5,4},{6,7},{7,6},{8,9},{9,8},{10,11... | collective-permute-start | bytes 73736 | tf_op jit(solution)/shard_map/ppermute | solution.py:629
  32.4 9.4 %collective-permute-start.3 = (f32[48,128]{1,0:T(8,128)S(1)}, f32[48,128]{1,0:T(8,128)S(1)}, u32[]{:S(2)}, u32[]{:S(2)}) collective-permute-start(f32[48,128]{1,0:T(8,128)S(1)} %get-tuple-element.105.message_in), channel_id=1, source_target_pairs={{1,2},{2,1},{3,4},{4,3},{5,6},{6,5},{7,8},{8,7},{9,10},{10,9},{11,... | collective-permute-start | bytes 73736 | tf_op jit(solution)/shard_map/ppermute | solution.py:628
  44.1 9.4 %collective-permute-start.4 = (f32[24,128]{1,0:T(8,128)S(1)}, f32[24,128]{1,0:T(8,128)S(1)}, u32[]{:S(2)}, u32[]{:S(2)}) collective-permute-start(f32[24,128]{1,0:T(8,128)S(1)} %get-tuple-element.114.message_in), channel_id=1, source_target_pairs={{0,1},{1,0},{2,3},{3,2},{4,5},{5,4},{6,7},{7,6},{8,9},{9,8},{10,11... | collective-permute-start | bytes 36872 | tf_op jit(solution)/shard_map/ppermute | solution.py:629
  44.2 9.3 %collective-permute-start.5 = (f32[24,128]{1,0:T(8,128)S(1)}, f32[24,128]{1,0:T(8,128)S(1)}, u32[]{:S(2)}, u32[]{:S(2)}) collective-permute-start(f32[24,128]{1,0:T(8,128)S(1)} %get-tuple-element.114.message_in), channel_id=1, source_target_pairs={{1,2},{2,1},{3,4},{4,3},{5,6},{6,5},{7,8},{8,7},{9,10},{10,9},{11,... | collective-permute-start | bytes 36872 | tf_op jit(solution)/shard_map/ppermute | solution.py:628
  55.8 9.2 %collective-permute-start.6 = (f32[24,128]{1,0:T(8,128)S(1)}, f32[24,128]{1,0:T(8,128)S(1)}, u32[]{:S(2)}, u32[]{:S(2)}) collective-permute-start(f32[24,128]{1,0:T(8,128)S(1)} %get-tuple-element.124.message_in), channel_id=1, source_target_pairs={{0,1},{1,0},{2,3},{3,2},{4,5},{5,4},{6,7},{7,6},{8,9},{9,8},{10,11... | collective-permute-start | bytes 36872 | tf_op jit(solution)/shard_map/ppermute | solution.py:629
  55.9 9.2 %collective-permute-start.7 = (f32[24,128]{1,0:T(8,128)S(1)}, f32[24,128]{1,0:T(8,128)S(1)}, u32[]{:S(2)}, u32[]{:S(2)}) collective-permute-start(f32[24,128]{1,0:T(8,128)S(1)} %get-tuple-element.124.message_in), channel_id=1, source_target_pairs={{1,2},{2,1},{3,4},{4,3},{5,6},{6,5},{7,8},{8,7},{9,10},{10,9},{11,... | collective-permute-start | bytes 36872 | tf_op jit(solution)/shard_map/ppermute | solution.py:628
  67.4 9.2 %collective-permute-start.8 = (f32[24,128]{1,0:T(8,128)S(1)}, f32[24,128]{1,0:T(8,128)S(1)}, u32[]{:S(2)}, u32[]{:S(2)}) collective-permute-start(f32[24,128]{1,0:T(8,128)S(1)} %get-tuple-element.133.message_in), channel_id=1, source_target_pairs={{0,1},{1,0},{2,3},{3,2},{4,5},{5,4},{6,7},{7,6},{8,9},{9,8},{10,11... | collective-permute-start | bytes 36872 | tf_op jit(solution)/shard_map/ppermute | solution.py:629
  67.5 9.2 %collective-permute-start.9 = (f32[24,128]{1,0:T(8,128)S(1)}, f32[24,128]{1,0:T(8,128)S(1)}, u32[]{:S(2)}, u32[]{:S(2)}) collective-permute-start(f32[24,128]{1,0:T(8,128)S(1)} %get-tuple-element.133.message_in), channel_id=1, source_target_pairs={{1,2},{2,1},{3,4},{4,3},{5,6},{6,5},{7,8},{8,7},{9,10},{10,9},{11,... | collective-permute-start | bytes 36872 | tf_op jit(solution)/shard_map/ppermute | solution.py:628
  79.1 9.4 %collective-permute-start.10 = (f32[24,128]{1,0:T(8,128)S(1)}, f32[24,128]{1,0:T(8,128)S(1)}, u32[]{:S(2)}, u32[]{:S(2)}) collective-permute-start(f32[24,128]{1,0:T(8,128)S(1)} %get-tuple-element.142.message_in), channel_id=1, source_target_pairs={{0,1},{1,0},{2,3},{3,2},{4,5},{5,4},{6,7},{7,6},{8,9},{9,8},{10,11... | collective-permute-start | bytes 36872 | tf_op jit(solution)/shard_map/ppermute | solution.py:629
  79.1 9.4 %collective-permute-start.11 = (f32[24,128]{1,0:T(8,128)S(1)}, f32[24,128]{1,0:T(8,128)S(1)}, u32[]{:S(2)}, u32[]{:S(2)}) collective-permute-start(f32[24,128]{1,0:T(8,128)S(1)} %get-tuple-element.142.message_in), channel_id=1, source_target_pairs={{1,2},{2,1},{3,4},{4,3},{5,6},{6,5},{7,8},{8,7},{9,10},{10,9},{11,... | collective-permute-start | bytes 36872 | tf_op jit(solution)/shard_map/ppermute | solution.py:628
  90.8 9.2 %collective-permute-start.12 = (f32[24,128]{1,0:T(8,128)S(1)}, f32[24,128]{1,0:T(8,128)S(1)}, u32[]{:S(2)}, u32[]{:S(2)}) collective-permute-start(f32[24,128]{1,0:T(8,128)S(1)} %get-tuple-element.151.message_in), channel_id=1, source_target_pairs={{0,1},{1,0},{2,3},{3,2},{4,5},{5,4},{6,7},{7,6},{8,9},{9,8},{10,11... | collective-permute-start | bytes 36872 | tf_op jit(solution)/shard_map/ppermute | solution.py:629
  90.9 9.2 %collective-permute-start.13 = (f32[24,128]{1,0:T(8,128)S(1)}, f32[24,128]{1,0:T(8,128)S(1)}, u32[]{:S(2)}, u32[]{:S(2)}) collective-permute-start(f32[24,128]{1,0:T(8,128)S(1)} %get-tuple-element.151.message_in), channel_id=1, source_target_pairs={{1,2},{2,1},{3,4},{4,3},{5,6},{6,5},{7,8},{8,7},{9,10},{10,9},{11,... | collective-permute-start | bytes 36872 | tf_op jit(solution)/shard_map/ppermute | solution.py:628
  102.5 9.2 %collective-permute-start.14 = (f32[24,128]{1,0:T(8,128)S(1)}, f32[24,128]{1,0:T(8,128)S(1)}, u32[]{:S(2)}, u32[]{:S(2)}) collective-permute-start(f32[24,128]{1,0:T(8,128)S(1)} %get-tuple-element.160.message_in), channel_id=1, source_target_pairs={{0,1},{1,0},{2,3},{3,2},{4,5},{5,4},{6,7},{7,6},{8,9},{9,8},{10,11... | collective-permute-start | bytes 36872 | tf_op jit(solution)/shard_map/ppermute | solution.py:629
  102.6 9.2 %collective-permute-start.15 = (f32[24,128]{1,0:T(8,128)S(1)}, f32[24,128]{1,0:T(8,128)S(1)}, u32[]{:S(2)}, u32[]{:S(2)}) collective-permute-start(f32[24,128]{1,0:T(8,128)S(1)} %get-tuple-element.160.message_in), channel_id=1, source_target_pairs={{1,2},{2,1},{3,4},{4,3},{5,6},{6,5},{7,8},{8,7},{9,10},{10,9},{11,... | collective-permute-start | bytes 36872 | tf_op jit(solution)/shard_map/ppermute | solution.py:628
  114.1 7.1 %collective-permute-start.16 = (f32[24,128]{1,0:T(8,128)S(1)}, f32[24,128]{1,0:T(8,128)S(1)}, u32[]{:S(2)}, u32[]{:S(2)}) collective-permute-start(f32[24,128]{1,0:T(8,128)S(1)} %get-tuple-element.169.message_in), channel_id=1, source_target_pairs={{0,1},{1,0},{2,3},{3,2},{4,5},{5,4},{6,7},{7,6},{8,9},{9,8},{10,11... | collective-permute-start | bytes 36872 | tf_op jit(solution)/shard_map/ppermute | solution.py:629
  114.2 9.2 %collective-permute-start.17 = (f32[24,128]{1,0:T(8,128)S(1)}, f32[24,128]{1,0:T(8,128)S(1)}, u32[]{:S(2)}, u32[]{:S(2)}) collective-permute-start(f32[24,128]{1,0:T(8,128)S(1)} %get-tuple-element.169.message_in), channel_id=1, source_target_pairs={{1,2},{2,1},{3,4},{4,3},{5,6},{6,5},{7,8},{8,7},{9,10},{10,9},{11,... | collective-permute-start | bytes 36872 | tf_op jit(solution)/shard_map/ppermute | solution.py:628

commit v6 on v5

--- a/solution.py
+++ b/solution.py
@@ -169,33 +169,40 @@
     lax.fori_loop(0, PER // BLOCK, block, 0)
 
 
-def scatter_shared(index_ref, hot_ref, values_ref, high_ref, low_ref, out_ref):
+def scatter_shared(index_ref, hot_ref, values_ref, high_ref, low_ref, sums_ref, out_ref):
     high, low = split(values_ref[...])
     high_ref[...] = high
     low_ref[...] = low
+    sums_ref[...] = jnp.zeros_like(sums_ref)
     lines = iota((8, 256), 0)
-    line = index_ref[...] >> 7
-    left = []
-    for n in range(PER):
-        here = line[n : n + 1, :] == lines
-        left.append(
-            jnp.concatenate(
-                [
-                    jnp.where(
-                        here,
-                        jnp.broadcast_to(ref[c * PER + n : c * PER + n + 1, :], (8, 256)),
-                        0.0,
-                    )
-                    for ref in (high_ref, low_ref)
-                    for c in range(3)
-                ],
-                axis=0,
-            ).astype(BF16)
-        )
-    sums = jnp.dot(
-        jnp.concatenate(left, axis=1), hot_ref[...], preferred_element_type=F32
-    )
-    out_ref[...] = sums[0:24, :] + sums[24:48, :]
+
+    def block(b, carry):
+        row = pl.multiple_of(b * BLOCK, BLOCK)
+        line = index_ref[pl.ds(row, BLOCK), :] >> 7
+        left = []
+        for k in range(BLOCK):
+            here = line[k : k + 1, :] == lines
+            left.append(
+                jnp.concatenate(
+                    [
+                        jnp.where(
+                            here,
+                            jnp.broadcast_to(ref[pl.ds(c * PER + row + k, 1), :], (8, 256)),
+                            0.0,
+                        )
+                        for ref in (high_ref, low_ref)
+                        for c in range(3)
+                    ],
+                    axis=0,
+                ).astype(BF16)
+            )
+        left = jnp.concatenate(left, axis=1)
+        right = hot_ref[pl.ds(pl.multiple_of(row * 256, 256), BLOCK * 256), :]
+        sums_ref[...] += jnp.dot(left, right, preferred_element_type=F32)
+        return carry
+
+    lax.fori_loop(0, PER // BLOCK, block, 0)
+    out_ref[...] = sums_ref[0:24, :] + sums_ref[24:48, :]
 
 
 def add_parts(sums_ref, first, channels):
@@ -396,9 +403,8 @@
     for i in range(2):
         high, low = split(stiff_ref[i])
         high = high.astype(BF16)
-        blocks_ref[DOFS * i : DOFS * i + DOFS, :] = jnp.concatenate(
-            [low.astype(BF16), high, high], axis=1
-        )
+        blocks_ref[DOFS * i : DOFS * i + DOFS, :] = high
+        blocks_ref[DOFS * (2 + i) : DOFS * (3 + i), :] = low.astype(BF16)
 
 
 def build_hot(index_ref, hot_ref, width):
@@ -416,12 +422,16 @@
                 hot_ref[top : top + 16, :] = jnp.where(column == lanes, one, zero)
 
 
-def multiply_blocks(blocks_ref, rows_ref):
-    high, low = split(rows_ref[...])
+def multiply_blocks(blocks_ref, rows):
+    high, low = split(rows)
     high = high.astype(BF16)
     low = low.astype(BF16)
-    return jnp.dot(
-        blocks_ref[...], jnp.concatenate([high, low, high], axis=0), preferred_element_type=F32
+    block_high = blocks_ref[: 2 * DOFS]
+    block_low = blocks_ref[2 * DOFS :]
+    return (
+        jnp.dot(block_low, high, preferred_element_type=F32)
+        + jnp.dot(block_high, low, preferred_element_type=F32)
+        + jnp.dot(block_high, high, preferred_element_type=F32)
     )
 
 
@@ -457,7 +467,7 @@
 ):
     shared_field[...] = field_message[NEAR_CAP:, 0:128] + from_neighbours(near_in, other_in, NEAR_CAP)
     gather_shared(shared_field, shared_index_ref, gathered_in, gathered, 3)
-    products = multiply_blocks(blocks_ref, gathered)
+    products = multiply_blocks(blocks_ref, gathered[...])
     me = lax.axis_index(AXES)
     received = jnp.concatenate(
         [far_ref[:, 0, :], near_in[0:NEAR_CAP, :], other_in[0:NEAR_CAP, :]], axis=0
@@ -500,12 +510,12 @@
 
 def apply_operator(
     shared_update, gathered_in, shared_index_ref, coefs_ref, hot_ref, blocks_ref, values_ref,
-    message, gathered, value_high, value_low,
+    message, gathered, value_high, value_low, sums,
 ):
     gather_shared(shared_update, shared_index_ref, gathered_in, gathered, 0)
-    products = multiply_blocks(blocks_ref, gathered)
+    products = multiply_blocks(blocks_ref, gathered[...])
     values_ref[...] = products[:DOFS] * coefs_ref[0:1, :] + products[DOFS:] * coefs_ref[1:2, :]
-    scatter_shared(shared_index_ref, hot_ref, values_ref, value_high, value_low, message)
+    scatter_shared(shared_index_ref, hot_ref, values_ref, value_high, value_low, sums, message)
 
 
 def inverse_of(diagonal):
@@ -529,7 +539,7 @@
 def begin_shared(
     step, message_in, near_in, other_in, shared_field, gathered_in, shared_index_ref, coefs_ref,
     hot_ref, blocks_ref, residual_out, inverse_out, update_out, field_out, values_ref, message,
-    gathered, value_high, value_low,
+    gathered, value_high, value_low, sums,
 ):
     residual = message_in[0:24, :] + from_neighbours(near_in, other_in, 0)
     inverse = inverse_of(message_in[24:48, :] + from_neighbours(near_in, other_in, 24))
@@ -540,7 +550,7 @@
     field_out[...] = shared_field[...] + update
     apply_operator(
         update_out, gathered_in, shared_index_ref, coefs_ref, hot_ref, blocks_ref, values_ref,
-        message, gathered, value_high, value_low,
+        message, gathered, value_high, value_low, sums,
     )
 
 
@@ -565,7 +575,7 @@
 def step_shared(
     step, message_in, near_in, other_in, residual_ref, inverse_ref, update_ref, field_ref,
     gathered_in, shared_index_ref, coefs_ref, hot_ref, blocks_ref, residual_out, update_out,
-    field_out, values_ref, message, gathered, value_high, value_low,
+    field_out, values_ref, message, gathered, value_high, value_low, sums,
 ):
     residual = residual_ref[...] - (message_in[...] + from_neighbours(near_in, other_in, 0))
     update = next_update(step, residual, inverse_ref[...], update_ref[...])
@@ -574,7 +584,7 @@
     field_out[...] = field_ref[...] + update
     apply_operator(
         update_out, gathered_in, shared_index_ref, coefs_ref, hot_ref, blocks_ref, values_ref,
-        message, gathered, value_high, value_low,
+        message, gathered, value_high, value_low, sums,
     )
 
 
@@ -686,7 +696,7 @@
             integers(PER, ELEM),
             integers(PER, ELEM),
             shaped(32, 256),
-            shaped(2 * DOFS, 3 * DOFS, dtype=BF16),
+            shaped(4 * DOFS, DOFS, dtype=BF16),
             ELEMENT_ROWS,
         ),
         [rows(32), rows(PER)],
@@ -714,7 +724,7 @@
     )
     near, other = exchange(message, message)
     plan = steps()
-    scratch = [rows(DOFS)] * 3
+    scratch = [rows(DOFS)] * 3 + [pltpu.VMEM((48, 128), F32)]
     window_scratch = [rows(DOFS)] * 2 + [rows(192)]
     residual = partial
     inverse, update, field, gathered, hot_shared = call(

time: 125 us -> 123 us (0.984)
  Pallas kernels: 61.6 us -> 59.2 us
    pallas_call x6, Pallas kernels: 13.8 us -> 11.8 us  [local(): call(functools.partial(step_shared, step), (SHARED, SHARED, SHARED, ELEME...]
  transfers between devices with their start and end apart: 19 -> 19, of which waited for: 6 -> 6; matrix products, arithmetic and copies ran while one was open for 0% -> 0% of each run, Pallas kernels for 29% -> 30%
where the time goes in v6:
time: 123 us; the launch traced here: 122 us
  Pallas kernels  59.2 us (48%)
  starting transfers between devices  58.8 us (48%)
  waiting for transfers between devices  3.03 us (2%)
    ppermute x9, starting transfers between devices, exchange(): other = lax.ppermute(other_message, AXES, OTHER_PAIRS)  47.4 us
    pallas_call x6, Pallas kernels, local(): call(functools.partial(step_unshared, step), (STATE, STATE, STATE, ELEMEN...  25.3 us
    pallas_call x6, Pallas kernels, local(): call(functools.partial(step_shared, step), (SHARED, SHARED, SHARED, ELEME...  11.8 us
    all_to_all x1, starting transfers between devices, local(): far = lax.all_to_all(far, AXES, split_axis=0, concat_axis=0, tiled=True)  10.5 us
    pallas_call x1, Pallas kernels, local(): call(place_kernel, (shaped(PER * ELEM, 256, dtype=BF16), ELEMENT_ROWS, sh...  6.37 us
    pallas_call x1, Pallas kernels, local(): call(index_kernel, (integers(PER, ELEM), integers(PER, ELEM), shaped(32,...  4.57 us
    pallas_call x1, Pallas kernels, local(): call(functools.partial(begin_unshared, plan[0]), (STATE, STATE, STATE, EL...  4.07 us
    ppermute x9, waiting for transfers between devices, exchange(): other = lax.ppermute(other_message, AXES, OTHER_PAIRS)  3.01 us
  transfers between devices with their start and end apart: 19, of which 6 were waited for; matrix products, arithmetic and copies ran while one was open for 0% of the time, Pallas kernels for 30%

profile of v6, /device:TPU:6, one launch (start us, length us, event | category | flops | bytes accessed | tf_op | source)
XLA Modules:
  0.0 122.0 jit_solution(17619456921352717516)
XLA Ops:
  0.6 2.0 %shard_map.94 = (f32[128,1,256]{2,1,0:T(1,128)}, f32[40,256]{1,0:T(8,128)S(1)}, f32[40,256]{1,0:T(8,128)S(1)}, s32[8,128]{1,0:T(8,128)S(1)}, f32[96,256]{1,0:T(8...) custom-call(f32[192,256]{1,0:T(8,128)} %loads_hbm.1, ...), custom_call_target="tpu_custom_call" | custom-call | tf_op jit(solution)/shard_map/pallas_call | solution.py:666
  2.7 10.5 %all-to-all-start = ((f32[128,1,256]{2,1,0:T(1,128)}), f32[128,1,256]{2,1,0:T(1,128)S(1)}, u32[]{:S(2)}, u32[]{:S(2)}) async-start(f32[128,1,256]{2,1,0:T(1,128)} %get-tuple-element.94), calls=%async_computation | async-start | bytes 262144 | tf_op jit(solution)/shard_map/all_to_all | solution.py:692
  13.2 0.2 collective-permute-start
  13.4 7.9 %collective-permute-start.1 = (f32[40,256]{1,0:T(8,128)S(1)}, f32[40,256]{1,0:T(8,128)S(1)}, u32[]{:S(2)}, u32[]{:S(2)}) collective-permute-start(f32[40,256]{1,0:T(8,128)S(1)} %get-tuple-element.96), channel_id=1, source_target_pairs={{1,2},{2,1},{3,4},{4,3},{5,6},{6,5},{7,8},{8,7},{9,10},{10,9},{11,... | collective-permute-start | bytes 122888 | tf_op jit(solution)/shard_map/ppermute | solution.py:638
  21.2 4.6 %shard_map.95 = (s32[64,256]{1,0:T(8,128)S(1)}, s32[64,256]{1,0:T(8,128)S(1)}, f32[32,256]{1,0:T(8,128)S(1)}, bf16[768,192]{1,0:T(8,128)(2,1)S(1)}, f32[192,256]{1,0:T(8,128)S(1)}) custom-call(f32[96,256]{1,0:T(8,128)S(1)} %get-tuple-element.98.state_ref.field_ref, s32[8,128]{1,0:T(8,128)S(1)} %get-tuple-element.99.places_ref, ...), custom_call_target="tpu_custom_call" | custom-call | tf_op jit(solution)/shard_map/pallas_call | solution.py:693
  25.8 6.4 %shard_map.96 = (bf16[16384,256]{1,0:T(8,128)(2,1)S(1)}, f32[192,256]{1,0:T(8,128)}, f32[2,256]{1,0:T(2,128)}, f32[2,256]{1,0:T(2,128)S(1)}, f32[96,256]{1,0:T(8...) custom-call(f32[192,256]{1,0:T(8,128)S(1)} %get-tuple-element.91.loads_ref, ...), custom_call_target="tpu_custom_call" | custom-call | tf_op jit(solution)/shard_map/pallas_call | solution.py:704
  32.3 4.9 %collective-permute-start.3 = (f32[48,128]{1,0:T(8,128)S(1)}, f32[48,128]{1,0:T(8,128)S(1)}, u32[]{:S(2)}, u32[]{:S(2)}) collective-permute-start(f32[48,128]{1,0:T(8,128)S(1)} %get-tuple-element.105.message_in), channel_id=1, source_target_pairs={{1,2},{2,1},{3,4},{4,3},{5,6},{6,5},{7,8},{8,7},{9,10},{10,9},{11,... | collective-permute-start | bytes 73736 | tf_op jit(solution)/shard_map/ppermute | solution.py:638
  37.2 4.1 %shard_map.97 = (f32[96,256]{1,0:T(8,128)S(1)}, f32[96,256]{1,0:T(8,128)S(1)}, f32[96,256]{1,0:T(8,128)S(1)}, f32[192,256]{1,0:T(8,128)S(1)}, bf16[16384,128]{1,0:T(8,128)(2,1)S(1)}) custom-call(f32[96,256]{1,0:T(8,128)S(1)} %get-tuple-element.107.partial_ref.residual_ref, f32[96,256]{1,0:T(8,128)S(1)} %get-tuple-element.108.diagonal_ref, ...), custom_call_target="tpu_custom_call" | custom-call | tf_op jit(solution)/shard_map/pallas_call | solution.py:730
  41.3 0.3 collective-permute-done.3.other_in
  41.7 2.0 %shard_map.98 = (f32[24,128]{1,0:T(8,128)S(1)}, f32[24,128]{1,0:T(8,128)S(1)}, f32[24,128]{1,0:T(8,128)S(1)}, f32[24,128]{1,0:T(8,128)S(1)}, f32[192,256]{1,0:T(8,128)S(1)}, /*index=5*/f32[24,128]{1,0:T(8,128)S(1)}) custom-call(f32[48,128]{1,0:T(8,128)S(1)} %get-tuple-element.105.message_in, f32[48,128]{1,0:T(8,128)S(1)} %collective-permute-done.2.near_in, ...), custom_call_target="tpu_custom_call" | custom-call | tf_op jit(solution)/shard_map/pallas_call | solution.py:735
  43.8 5.1 %collective-permute-start.5 = (f32[24,128]{1,0:T(8,128)S(1)}, f32[24,128]{1,0:T(8,128)S(1)}, u32[]{:S(2)}, u32[]{:S(2)}) collective-permute-start(f32[24,128]{1,0:T(8,128)S(1)} %get-tuple-element.114.message_in), channel_id=1, source_target_pairs={{1,2},{2,1},{3,4},{4,3},{5,6},{6,5},{7,8},{8,7},{9,10},{10,9},{11,... | collective-permute-start | bytes 36872 | tf_op jit(solution)/shard_map/ppermute | solution.py:638
  48.9 4.2 %shard_map.99 = (f32[96,256]{1,0:T(8,128)S(1)}, f32[96,256]{1,0:T(8,128)S(1)}, f32[96,256]{1,0:T(8,128)S(1)}, f32[192,256]{1,0:T(8,128)S(1)}) custom-call(f32[192,256]{1,0:T(8,128)S(1)} %get-tuple-element.119.values_ref, f32[96,256]{1,0:T(8,128)S(1)} %get-tuple-element.107.partial_ref.residual_ref, f32[96,256]{1,0:T(8,128)S(1)} %get-tuple-element.120.inverse_ref, ...), custom_call_target="tpu_custom_call" | custom-call | tf_op jit(solution)/shard_map/pallas_call | solution.py:742
  53.1 2.0 %shard_map.100 = (f32[24,128]{1,0:T(8,128)S(1)}, f32[24,128]{1,0:T(8,128)S(1)}, f32[24,128]{1,0:T(8,128)S(1)}, f32[192,256]{1,0:T(8,128)S(1)}, f32[24,128]{1,0:T(8,128)S(1)}) custom-call(f32[24,128]{1,0:T(8,128)S(1)} %get-tuple-element.114.message_in, f32[24,128]{1,0:T(8,128)S(1)} %collective-permute-done.4.near_in, ...), custom_call_target="tpu_custom_call" | custom-call | tf_op jit(solution)/shard_map/pallas_call | solution.py:747
  55.2 4.9 %collective-permute-start.7 = (f32[24,128]{1,0:T(8,128)S(1)}, f32[24,128]{1,0:T(8,128)S(1)}, u32[]{:S(2)}, u32[]{:S(2)}) collective-permute-start(f32[24,128]{1,0:T(8,128)S(1)} %get-tuple-element.124.message_in), channel_id=1, source_target_pairs={{1,2},{2,1},{3,4},{4,3},{5,6},{6,5},{7,8},{8,7},{9,10},{10,9},{11,... | collective-permute-start | bytes 36872 | tf_op jit(solution)/shard_map/ppermute | solution.py:638
  60.1 4.2 %shard_map.101 = (f32[96,256]{1,0:T(8,128)S(1)}, f32[96,256]{1,0:T(8,128)S(1)}, f32[96,256]{1,0:T(8,128)S(1)}, f32[192,256]{1,0:T(8,128)S(1)}) custom-call(f32[192,256]{1,0:T(8,128)S(1)} %get-tuple-element.128.values_ref, f32[96,256]{1,0:T(8,128)S(1)} %get-tuple-element.129.residual_ref, f32[96,256]{1,0:T(8,128)S(1)} %get-tuple-element.120.inverse_ref, ...), custom_call_target="tpu_custom_call" | custom-call | tf_op jit(solution)/shard_map/pallas_call | solution.py:742
  64.4 2.0 %shard_map.102 = (f32[24,128]{1,0:T(8,128)S(1)}, f32[24,128]{1,0:T(8,128)S(1)}, f32[24,128]{1,0:T(8,128)S(1)}, f32[192,256]{1,0:T(8,128)S(1)}, f32[24,128]{1,0:T(8,128)S(1)}) custom-call(f32[24,128]{1,0:T(8,128)S(1)} %get-tuple-element.124.message_in, f32[24,128]{1,0:T(8,128)S(1)} %collective-permute-done.6.near_in, ...), custom_call_target="tpu_custom_call" | custom-call | tf_op jit(solution)/shard_map/pallas_call | solution.py:747
  66.5 4.9 %collective-permute-start.9 = (f32[24,128]{1,0:T(8,128)S(1)}, f32[24,128]{1,0:T(8,128)S(1)}, u32[]{:S(2)}, u32[]{:S(2)}) collective-permute-start(f32[24,128]{1,0:T(8,128)S(1)} %get-tuple-element.133.message_in), channel_id=1, source_target_pairs={{1,2},{2,1},{3,4},{4,3},{5,6},{6,5},{7,8},{8,7},{9,10},{10,9},{11,... | collective-permute-start | bytes 36872 | tf_op jit(solution)/shard_map/ppermute | solution.py:638
  71.4 4.2 %shard_map.103 = (f32[96,256]{1,0:T(8,128)S(1)}, f32[96,256]{1,0:T(8,128)S(1)}, f32[96,256]{1,0:T(8,128)S(1)}, f32[192,256]{1,0:T(8,128)S(1)}) custom-call(f32[192,256]{1,0:T(8,128)S(1)} %get-tuple-element.137.values_ref, f32[96,256]{1,0:T(8,128)S(1)} %get-tuple-element.138.residual_ref, f32[96,256]{1,0:T(8,128)S(1)} %get-tuple-element.120.inverse_ref, ...), custom_call_target="tpu_custom_call" | custom-call | tf_op jit(solution)/shard_map/pallas_call | solution.py:742
  75.7 2.0 %shard_map.104 = (f32[24,128]{1,0:T(8,128)S(1)}, f32[24,128]{1,0:T(8,128)S(1)}, f32[24,128]{1,0:T(8,128)S(1)}, f32[192,256]{1,0:T(8,128)S(1)}, f32[24,128]{1,0:T(8,128)S(1)}) custom-call(f32[24,128]{1,0:T(8,128)S(1)} %get-tuple-element.133.message_in, f32[24,128]{1,0:T(8,128)S(1)} %collective-permute-done.8.near_in, ...), custom_call_target="tpu_custom_call" | custom-call | tf_op jit(solution)/shard_map/pallas_call | solution.py:747
  77.8 4.9 %collective-permute-start.11 = (f32[24,128]{1,0:T(8,128)S(1)}, f32[24,128]{1,0:T(8,128)S(1)}, u32[]{:S(2)}, u32[]{:S(2)}) collective-permute-start(f32[24,128]{1,0:T(8,128)S(1)} %get-tuple-element.142.message_in), channel_id=1, source_target_pairs={{1,2},{2,1},{3,4},{4,3},{5,6},{6,5},{7,8},{8,7},{9,10},{10,9},{11,... | collective-permute-start | bytes 36872 | tf_op jit(solution)/shard_map/ppermute | solution.py:638
  82.7 4.2 %shard_map.105 = (f32[96,256]{1,0:T(8,128)S(1)}, f32[96,256]{1,0:T(8,128)S(1)}, f32[96,256]{1,0:T(8,128)S(1)}, f32[192,256]{1,0:T(8,128)S(1)}) custom-call(f32[192,256]{1,0:T(8,128)S(1)} %get-tuple-element.146.values_ref, f32[96,256]{1,0:T(8,128)S(1)} %get-tuple-element.147.residual_ref, f32[96,256]{1,0:T(8,128)S(1)} %get-tuple-element.120.inverse_ref, ...), custom_call_target="tpu_custom_call" | custom-call | tf_op jit(solution)/shard_map/pallas_call | solution.py:742
  87.0 2.0 %shard_map.106 = (f32[24,128]{1,0:T(8,128)S(1)}, f32[24,128]{1,0:T(8,128)S(1)}, f32[24,128]{1,0:T(8,128)S(1)}, f32[192,256]{1,0:T(8,128)S(1)}, f32[24,128]{1,0:T(8,128)S(1)}) custom-call(f32[24,128]{1,0:T(8,128)S(1)} %get-tuple-element.142.message_in, f32[24,128]{1,0:T(8,128)S(1)} %collective-permute-done.10.near_in, ...), custom_call_target="tpu_custom_call" | custom-call | tf_op jit(solution)/shard_map/pallas_call | solution.py:747
  89.1 5.1 %collective-permute-start.13 = (f32[24,128]{1,0:T(8,128)S(1)}, f32[24,128]{1,0:T(8,128)S(1)}, u32[]{:S(2)}, u32[]{:S(2)}) collective-permute-start(f32[24,128]{1,0:T(8,128)S(1)} %get-tuple-element.151.message_in), channel_id=1, source_target_pairs={{1,2},{2,1},{3,4},{4,3},{5,6},{6,5},{7,8},{8,7},{9,10},{10,9},{11,... | collective-permute-start | bytes 36872 | tf_op jit(solution)/shard_map/ppermute | solution.py:638
  94.2 4.2 %shard_map.107 = (f32[96,256]{1,0:T(8,128)S(1)}, f32[96,256]{1,0:T(8,128)S(1)}, f32[96,256]{1,0:T(8,128)S(1)}, f32[192,256]{1,0:T(8,128)S(1)}) custom-call(f32[192,256]{1,0:T(8,128)S(1)} %get-tuple-element.155.values_ref, f32[96,256]{1,0:T(8,128)S(1)} %get-tuple-element.156.residual_ref, f32[96,256]{1,0:T(8,128)S(1)} %get-tuple-element.120.inverse_ref, ...), custom_call_target="tpu_custom_call" | custom-call | tf_op jit(solution)/shard_map/pallas_call | solution.py:742
  98.4 2.0 %shard_map.108 = (f32[24,128]{1,0:T(8,128)S(1)}, f32[24,128]{1,0:T(8,128)S(1)}, f32[24,128]{1,0:T(8,128)S(1)}, f32[192,256]{1,0:T(8,128)S(1)}, f32[24,128]{1,0:T(8,128)S(1)}) custom-call(f32[24,128]{1,0:T(8,128)S(1)} %get-tuple-element.151.message_in, f32[24,128]{1,0:T(8,128)S(1)} %collective-permute-done.12.near_in, ...), custom_call_target="tpu_custom_call" | custom-call | tf_op jit(solution)/shard_map/pallas_call | solution.py:747
  100.5 4.9 %collective-permute-start.15 = (f32[24,128]{1,0:T(8,128)S(1)}, f32[24,128]{1,0:T(8,128)S(1)}, u32[]{:S(2)}, u32[]{:S(2)}) collective-permute-start(f32[24,128]{1,0:T(8,128)S(1)} %get-tuple-element.160.message_in), channel_id=1, source_target_pairs={{1,2},{2,1},{3,4},{4,3},{5,6},{6,5},{7,8},{8,7},{9,10},{10,9},{11,... | collective-permute-start | bytes 36872 | tf_op jit(solution)/shard_map/ppermute | solution.py:638
  105.4 4.2 %shard_map.109 = (f32[96,256]{1,0:T(8,128)S(1)}, f32[96,256]{1,0:T(8,128)S(1)}, f32[96,256]{1,0:T(8,128)S(1)}, f32[192,256]{1,0:T(8,128)S(1)}) custom-call(f32[192,256]{1,0:T(8,128)S(1)} %get-tuple-element.164.values_ref, f32[96,256]{1,0:T(8,128)S(1)} %get-tuple-element.165.residual_ref, f32[96,256]{1,0:T(8,128)S(1)} %get-tuple-element.120.inverse_ref, ...), custom_call_target="tpu_custom_call" | custom-call | tf_op jit(solution)/shard_map/pallas_call | solution.py:742
  109.8 2.0 %shard_map.110 = (f32[24,128]{1,0:T(8,128)S(1)}, f32[24,128]{1,0:T(8,128)S(1)}, f32[24,128]{1,0:T(8,128)S(1)}, f32[192,256]{1,0:T(8,128)S(1)}, f32[24,128]{1,0:T(8,128)S(1)}) custom-call(f32[24,128]{1,0:T(8,128)S(1)} %get-tuple-element.160.message_in, f32[24,128]{1,0:T(8,128)S(1)} %collective-permute-done.14.near_in, ...), custom_call_target="tpu_custom_call" | custom-call | tf_op jit(solution)/shard_map/pallas_call | solution.py:747
  111.8 4.9 %collective-permute-start.17 = (f32[24,128]{1,0:T(8,128)S(1)}, f32[24,128]{1,0:T(8,128)S(1)}, u32[]{:S(2)}, u32[]{:S(2)}) collective-permute-start(f32[24,128]{1,0:T(8,128)S(1)} %get-tuple-element.169.message_in), channel_id=1, source_target_pairs={{1,2},{2,1},{3,4},{4,3},{5,6},{6,5},{7,8},{8,7},{9,10},{10,9},{11,... | collective-permute-start | bytes 36872 | tf_op jit(solution)/shard_map/ppermute | solution.py:638
  116.7 2.1 %shard_map.111.field_ref = f32[96,256]{1,0:T(8,128)S(1)} custom-call(f32[192,256]{1,0:T(8,128)S(1)} %get-tuple-element.173.values_ref, f32[96,256]{1,0:T(8,128)S(1)} %get-tuple-element.174.residual_ref, f32[96,256]{1,0:T(8,128)S(1)} %get-tuple-element.120.inverse_ref, f32[96,256]{1,0:T(8,128)S(1)} %get-tuple-element.175.update_ref, ...), custom_call_target="tpu_custom_call" | custom-call | tf_op jit(solution)/shard_map/pallas_call | solution.py:756
  118.8 2.2 %collective-permute-done.17.other_in = f32[24,128]{1,0:T(8,128)S(1)} collective-permute-done((f32[24,128]{1,0:T(8,128)S(1)}, f32[24,128]{1,0:T(8,128)S(1)}, u32[]{:S(2)}, u32[]{:S(2)}) %collective-permute-start.17) | collective-permute-done | bytes 12320 | tf_op jit(solution)/shard_map/ppermute | solution.py:638
  121.1 1.0 shard_map.112
  (25 shorter events, 1.1 us)
Async XLA Ops:
  2.7 23.2 %all-to-all-start = ((f32[128,1,256]{2,1,0:T(1,128)}), f32[128,1,256]{2,1,0:T(1,128)S(1)}, u32[]{:S(2)}, u32[]{:S(2)}) async-start(f32[128,1,256]{2,1,0:T(1,128)} %get-tuple-element.94), calls=%async_computation | async-start | bytes 262144 | tf_op jit(solution)/shard_map/all_to_all | solution.py:692
  13.2 12.6 %collective-permute-start = (f32[40,256]{1,0:T(8,128)S(1)}, f32[40,256]{1,0:T(8,128)S(1)}, u32[]{:S(2)}, u32[]{:S(2)}) collective-permute-start(f32[40,256]{1,0:T(8,128)S(1)} %get-tuple-element.95.field_message), channel_id=1, source_target_pairs={{0,1},{1,0},{2,3},{3,2},{4,5},{5,4},{6,7},{7,6},{8,9},{9,8},{10,11... | collective-permute-start | bytes 122888 | tf_op jit(solution)/shard_map/ppermute | solution.py:639
  13.4 12.5 %collective-permute-start.1 = (f32[40,256]{1,0:T(8,128)S(1)}, f32[40,256]{1,0:T(8,128)S(1)}, u32[]{:S(2)}, u32[]{:S(2)}) collective-permute-start(f32[40,256]{1,0:T(8,128)S(1)} %get-tuple-element.96), channel_id=1, source_target_pairs={{1,2},{2,1},{3,4},{4,3},{5,6},{6,5},{7,8},{8,7},{9,10},{10,9},{11,... | collective-permute-start | bytes 122888 | tf_op jit(solution)/shard_map/ppermute | solution.py:638
  32.2 9.1 %collective-permute-start.2 = (f32[48,128]{1,0:T(8,128)S(1)}, f32[48,128]{1,0:T(8,128)S(1)}, u32[]{:S(2)}, u32[]{:S(2)}) collective-permute-start(f32[48,128]{1,0:T(8,128)S(1)} %get-tuple-element.105.message_in), channel_id=1, source_target_pairs={{0,1},{1,0},{2,3},{3,2},{4,5},{5,4},{6,7},{7,6},{8,9},{9,8},{10,11... | collective-permute-start | bytes 73736 | tf_op jit(solution)/shard_map/ppermute | solution.py:639
  32.3 9.4 %collective-permute-start.3 = (f32[48,128]{1,0:T(8,128)S(1)}, f32[48,128]{1,0:T(8,128)S(1)}, u32[]{:S(2)}, u32[]{:S(2)}) collective-permute-start(f32[48,128]{1,0:T(8,128)S(1)} %get-tuple-element.105.message_in), channel_id=1, source_target_pairs={{1,2},{2,1},{3,4},{4,3},{5,6},{6,5},{7,8},{8,7},{9,10},{10,9},{11,... | collective-permute-start | bytes 73736 | tf_op jit(solution)/shard_map/ppermute | solution.py:638
  43.7 9.4 %collective-permute-start.4 = (f32[24,128]{1,0:T(8,128)S(1)}, f32[24,128]{1,0:T(8,128)S(1)}, u32[]{:S(2)}, u32[]{:S(2)}) collective-permute-start(f32[24,128]{1,0:T(8,128)S(1)} %get-tuple-element.114.message_in), channel_id=1, source_target_pairs={{0,1},{1,0},{2,3},{3,2},{4,5},{5,4},{6,7},{7,6},{8,9},{9,8},{10,11... | collective-permute-start | bytes 36872 | tf_op jit(solution)/shard_map/ppermute | solution.py:639
  43.8 9.3 %collective-permute-start.5 = (f32[24,128]{1,0:T(8,128)S(1)}, f32[24,128]{1,0:T(8,128)S(1)}, u32[]{:S(2)}, u32[]{:S(2)}) collective-permute-start(f32[24,128]{1,0:T(8,128)S(1)} %get-tuple-element.114.message_in), channel_id=1, source_target_pairs={{1,2},{2,1},{3,4},{4,3},{5,6},{6,5},{7,8},{8,7},{9,10},{10,9},{11,... | collective-permute-start | bytes 36872 | tf_op jit(solution)/shard_map/ppermute | solution.py:638
  55.1 9.2 %collective-permute-start.6 = (f32[24,128]{1,0:T(8,128)S(1)}, f32[24,128]{1,0:T(8,128)S(1)}, u32[]{:S(2)}, u32[]{:S(2)}) collective-permute-start(f32[24,128]{1,0:T(8,128)S(1)} %get-tuple-element.124.message_in), channel_id=1, source_target_pairs={{0,1},{1,0},{2,3},{3,2},{4,5},{5,4},{6,7},{7,6},{8,9},{9,8},{10,11... | collective-permute-start | bytes 36872 | tf_op jit(solution)/shard_map/ppermute | solution.py:639
  55.2 9.2 %collective-permute-start.7 = (f32[24,128]{1,0:T(8,128)S(1)}, f32[24,128]{1,0:T(8,128)S(1)}, u32[]{:S(2)}, u32[]{:S(2)}) collective-permute-start(f32[24,128]{1,0:T(8,128)S(1)} %get-tuple-element.124.message_in), channel_id=1, source_target_pairs={{1,2},{2,1},{3,4},{4,3},{5,6},{6,5},{7,8},{8,7},{9,10},{10,9},{11,... | collective-permute-start | bytes 36872 | tf_op jit(solution)/shard_map/ppermute | solution.py:638
  66.4 9.2 %collective-permute-start.8 = (f32[24,128]{1,0:T(8,128)S(1)}, f32[24,128]{1,0:T(8,128)S(1)}, u32[]{:S(2)}, u32[]{:S(2)}) collective-permute-start(f32[24,128]{1,0:T(8,128)S(1)} %get-tuple-element.133.message_in), channel_id=1, source_target_pairs={{0,1},{1,0},{2,3},{3,2},{4,5},{5,4},{6,7},{7,6},{8,9},{9,8},{10,11... | collective-permute-start | bytes 36872 | tf_op jit(solution)/shard_map/ppermute | solution.py:639
  66.5 9.2 %collective-permute-start.9 = (f32[24,128]{1,0:T(8,128)S(1)}, f32[24,128]{1,0:T(8,128)S(1)}, u32[]{:S(2)}, u32[]{:S(2)}) collective-permute-start(f32[24,128]{1,0:T(8,128)S(1)} %get-tuple-element.133.message_in), channel_id=1, source_target_pairs={{1,2},{2,1},{3,4},{4,3},{5,6},{6,5},{7,8},{8,7},{9,10},{10,9},{11,... | collective-permute-start | bytes 36872 | tf_op jit(solution)/shard_map/ppermute | solution.py:638
  77.7 9.2 %collective-permute-start.10 = (f32[24,128]{1,0:T(8,128)S(1)}, f32[24,128]{1,0:T(8,128)S(1)}, u32[]{:S(2)}, u32[]{:S(2)}) collective-permute-start(f32[24,128]{1,0:T(8,128)S(1)} %get-tuple-element.142.message_in), channel_id=1, source_target_pairs={{0,1},{1,0},{2,3},{3,2},{4,5},{5,4},{6,7},{7,6},{8,9},{9,8},{10,11... | collective-permute-start | bytes 36872 | tf_op jit(solution)/shard_map/ppermute | solution.py:639
  77.8 9.2 %collective-permute-start.11 = (f32[24,128]{1,0:T(8,128)S(1)}, f32[24,128]{1,0:T(8,128)S(1)}, u32[]{:S(2)}, u32[]{:S(2)}) collective-permute-start(f32[24,128]{1,0:T(8,128)S(1)} %get-tuple-element.142.message_in), channel_id=1, source_target_pairs={{1,2},{2,1},{3,4},{4,3},{5,6},{6,5},{7,8},{8,7},{9,10},{10,9},{11,... | collective-permute-start | bytes 36872 | tf_op jit(solution)/shard_map/ppermute | solution.py:638
  89.0 9.4 %collective-permute-start.12 = (f32[24,128]{1,0:T(8,128)S(1)}, f32[24,128]{1,0:T(8,128)S(1)}, u32[]{:S(2)}, u32[]{:S(2)}) collective-permute-start(f32[24,128]{1,0:T(8,128)S(1)} %get-tuple-element.151.message_in), channel_id=1, source_target_pairs={{0,1},{1,0},{2,3},{3,2},{4,5},{5,4},{6,7},{7,6},{8,9},{9,8},{10,11... | collective-permute-start | bytes 36872 | tf_op jit(solution)/shard_map/ppermute | solution.py:639
  89.1 9.3 %collective-permute-start.13 = (f32[24,128]{1,0:T(8,128)S(1)}, f32[24,128]{1,0:T(8,128)S(1)}, u32[]{:S(2)}, u32[]{:S(2)}) collective-permute-start(f32[24,128]{1,0:T(8,128)S(1)} %get-tuple-element.151.message_in), channel_id=1, source_target_pairs={{1,2},{2,1},{3,4},{4,3},{5,6},{6,5},{7,8},{8,7},{9,10},{10,9},{11,... | collective-permute-start | bytes 36872 | tf_op jit(solution)/shard_map/ppermute | solution.py:638
  100.4 9.2 %collective-permute-start.14 = (f32[24,128]{1,0:T(8,128)S(1)}, f32[24,128]{1,0:T(8,128)S(1)}, u32[]{:S(2)}, u32[]{:S(2)}) collective-permute-start(f32[24,128]{1,0:T(8,128)S(1)} %get-tuple-element.160.message_in), channel_id=1, source_target_pairs={{0,1},{1,0},{2,3},{3,2},{4,5},{5,4},{6,7},{7,6},{8,9},{9,8},{10,11... | collective-permute-start | bytes 36872 | tf_op jit(solution)/shard_map/ppermute | solution.py:639
  100.5 9.2 %collective-permute-start.15 = (f32[24,128]{1,0:T(8,128)S(1)}, f32[24,128]{1,0:T(8,128)S(1)}, u32[]{:S(2)}, u32[]{:S(2)}) collective-permute-start(f32[24,128]{1,0:T(8,128)S(1)} %get-tuple-element.160.message_in), channel_id=1, source_target_pairs={{1,2},{2,1},{3,4},{4,3},{5,6},{6,5},{7,8},{8,7},{9,10},{10,9},{11,... | collective-permute-start | bytes 36872 | tf_op jit(solution)/shard_map/ppermute | solution.py:638
  111.7 7.1 %collective-permute-start.16 = (f32[24,128]{1,0:T(8,128)S(1)}, f32[24,128]{1,0:T(8,128)S(1)}, u32[]{:S(2)}, u32[]{:S(2)}) collective-permute-start(f32[24,128]{1,0:T(8,128)S(1)} %get-tuple-element.169.message_in), channel_id=1, source_target_pairs={{0,1},{1,0},{2,3},{3,2},{4,5},{5,4},{6,7},{7,6},{8,9},{9,8},{10,11... | collective-permute-start | bytes 36872 | tf_op jit(solution)/shard_map/ppermute | solution.py:639
  111.8 9.2 %collective-permute-start.17 = (f32[24,128]{1,0:T(8,128)S(1)}, f32[24,128]{1,0:T(8,128)S(1)}, u32[]{:S(2)}, u32[]{:S(2)}) collective-permute-start(f32[24,128]{1,0:T(8,128)S(1)} %get-tuple-element.169.message_in), channel_id=1, source_target_pairs={{1,2},{2,1},{3,4},{4,3},{5,6},{6,5},{7,8},{8,7},{9,10},{10,9},{11,... | collective-permute-start | bytes 36872 | tf_op jit(solution)/shard_map/ppermute | solution.py:638

commit v7 on v6

--- a/solution.py
+++ b/solution.py
@@ -435,6 +435,22 @@
     )
 
 
+def products_kernel(
+    near_in,
+    other_in,
+    field_message,
+    gathered_in,
+    shared_index_ref,
+    blocks_ref,
+    shared_field,
+    products_ref,
+    gathered,
+):
+    shared_field[...] = field_message[NEAR_CAP:, 0:128] + from_neighbours(near_in, other_in, NEAR_CAP)
+    gather_shared(shared_field, shared_index_ref, gathered_in, gathered, 3)
+    products_ref[...] = multiply_blocks(blocks_ref, gathered[...])
+
+
 def place_kernel(
     loads_ref,
     coefs_ref,
@@ -442,22 +458,17 @@
     far_ref,
     near_in,
     other_in,
-    field_message,
     stiff_ref,
-    gathered_in,
+    products_ref,
     nodes_ref,
-    shared_index_ref,
     places_ref,
-    blocks_ref,
     hot_ref,
     moved_loads,
     moved_coefs,
     coefs_out,
     partial_ref,
     diagonal_ref,
-    shared_field,
     message,
-    gathered,
     values,
     value_high,
     value_low,
@@ -465,9 +476,6 @@
     kept_loads,
     sems,
 ):
-    shared_field[...] = field_message[NEAR_CAP:, 0:128] + from_neighbours(near_in, other_in, NEAR_CAP)
-    gather_shared(shared_field, shared_index_ref, gathered_in, gathered, 3)
-    products = multiply_blocks(blocks_ref, gathered[...])
     me = lax.axis_index(AXES)
     received = jnp.concatenate(
         [far_ref[:, 0, :], near_in[0:NEAR_CAP, :], other_in[0:NEAR_CAP, :]], axis=0
@@ -493,7 +501,9 @@
     )
     for copy in copies:
         copy.start()
-    values[0:DOFS, :] = loads - (products[:DOFS] * coefs[0:1, :] + products[DOFS:] * coefs[1:2, :])
+    values[0:DOFS, :] = loads - (
+        products_ref[0:DOFS, :] * coefs[0:1, :] + products_ref[DOFS:, :] * coefs[1:2, :]
+    )
     eye = iota((DOFS, DOFS), 0) == iota((DOFS, DOFS), 1)
     first_diag = jnp.sum(jnp.where(eye, stiff_ref[0], 0.0), axis=1, keepdims=True)
     second_diag = jnp.sum(jnp.where(eye, stiff_ref[1], 0.0), axis=1, keepdims=True)
@@ -701,7 +711,10 @@
         ),
         [rows(32), rows(PER)],
     )(field, places, nodes, stiff)
-    hot, moved_loads, moved_coefs, coefs, partial, diagonal, shared_field, message = call(
+    shared_field, products = call(
+        products_kernel, (SHARED, shaped(2 * DOFS, ELEM)), [rows(DOFS)]
+    )(near, other, field_message, gathered, shared_index, blocks)
+    hot, moved_loads, moved_coefs, coefs, partial, diagonal, message = call(
         place_kernel,
         (
             shaped(PER * ELEM, 256, dtype=BF16),
@@ -710,18 +723,14 @@
             shaped(2, ELEM),
             STATE,
             STATE,
-            SHARED,
             shaped(48, 128),
         ),
-        [rows(DOFS), rows(2 * DOFS), rows(2 * DOFS), rows(2 * DOFS), rows(384), rows(DOFS)]
+        [rows(2 * DOFS), rows(2 * DOFS), rows(2 * DOFS), rows(384), rows(DOFS)]
         + [pltpu.SemaphoreType.DMA((2,))],
         out_specs=[
-            pl.BlockSpec(memory_space=pltpu.HBM if i in (1, 2) else pltpu.VMEM) for i in range(8)
+            pl.BlockSpec(memory_space=pltpu.HBM if i in (1, 2) else pltpu.VMEM) for i in range(7)
         ],
-    )(
-        loads, coefs, moves, far, near, other, field_message, stiff,
-        gathered, nodes, shared_index, places, blocks,
-    )
+    )(loads, coefs, moves, far, near, other, stiff, products, nodes, places)
     near, other = exchange(message, message)
     plan = steps()
     scratch = [rows(DOFS)] * 3 + [pltpu.VMEM((48, 128), F32)]

time: 123 us -> 123 us (level)
  no operation moved by 1% of the time
where the time goes in v7:
time: 123 us
  Pallas kernels  59.8 us (49%)
  starting transfers between devices  58.7 us (48%)
  waiting for transfers between devices  3.04 us (2%)
    ppermute x9, starting transfers between devices, exchange(): other = lax.ppermute(other_message, AXES, OTHER_PAIRS)  47.4 us
    pallas_call x6, Pallas kernels, local(): call(functools.partial(step_unshared, step), (STATE, STATE, STATE, ELEMEN...  25.3 us
    pallas_call x6, Pallas kernels, local(): call(functools.partial(step_shared, step), (SHARED, SHARED, SHARED, ELEME...  11.8 us
    all_to_all x1, starting transfers between devices, local(): far = lax.all_to_all(far, AXES, split_axis=0, concat_axis=0, tiled=True)  10.5 us
    pallas_call x1, Pallas kernels, local(): call(place_kernel, (shaped(PER * ELEM, 256, dtype=BF16), ELEMENT_ROWS, sh...  6.08 us
    pallas_call x1, Pallas kernels, local(): call(index_kernel, (integers(PER, ELEM), integers(PER, ELEM), shaped(32,...  4.57 us
    pallas_call x1, Pallas kernels, local(): call(functools.partial(begin_unshared, plan[0]), (STATE, STATE, STATE, EL...  4.08 us
    ppermute x9, waiting for transfers between devices, exchange(): other = lax.ppermute(other_message, AXES, OTHER_PAIRS)  3.02 us
  transfers between devices with their start and end apart: 19, of which 6 were waited for; matrix products, arithmetic and copies ran while one was open for 0% of the time, Pallas kernels for 30%

profile of v7, /device:TPU:6, one launch (start us, length us, event | category | flops | bytes accessed | tf_op | source)
XLA Modules:
  0.0 122.6 jit_solution(12446093127455750140)
XLA Ops:
  0.6 2.0 %shard_map.94 = (f32[128,1,256]{2,1,0:T(1,128)}, f32[40,256]{1,0:T(8,128)S(1)}, f32[40,256]{1,0:T(8,128)S(1)}, s32[8,128]{1,0:T(8,128)S(1)}, f32[96,256]{1,0:T(8...) custom-call(f32[192,256]{1,0:T(8,128)} %loads_hbm.1, ...), custom_call_target="tpu_custom_call" | custom-call | tf_op jit(solution)/shard_map/pallas_call | solution.py:676
  2.7 10.5 %all-to-all-start = ((f32[128,1,256]{2,1,0:T(1,128)}), f32[128,1,256]{2,1,0:T(1,128)S(1)}, u32[]{:S(2)}, u32[]{:S(2)}) async-start(f32[128,1,256]{2,1,0:T(1,128)} %get-tuple-element.95), calls=%async_computation | async-start | bytes 262144 | tf_op jit(solution)/shard_map/all_to_all | solution.py:702
  13.4 7.9 %collective-permute-start.1 = (f32[40,256]{1,0:T(8,128)S(1)}, f32[40,256]{1,0:T(8,128)S(1)}, u32[]{:S(2)}, u32[]{:S(2)}) collective-permute-start(f32[40,256]{1,0:T(8,128)S(1)} %get-tuple-element.97), channel_id=1, source_target_pairs={{1,2},{2,1},{3,4},{4,3},{5,6},{6,5},{7,8},{8,7},{9,10},{10,9},{11,... | collective-permute-start | bytes 122888 | tf_op jit(solution)/shard_map/ppermute | solution.py:648
  21.2 4.6 %shard_map.95 = (s32[64,256]{1,0:T(8,128)S(1)}, s32[64,256]{1,0:T(8,128)S(1)}, f32[32,256]{1,0:T(8,128)S(1)}, bf16[768,192]{1,0:T(8,128)(2,1)S(1)}, f32[192,256]{1,0:T(8,128)S(1)}) custom-call(f32[96,256]{1,0:T(8,128)S(1)} %get-tuple-element.99.state_ref.field_ref, s32[8,128]{1,0:T(8,128)S(1)} %get-tuple-element.100.places_ref, ...), custom_call_target="tpu_custom_call" | custom-call | tf_op jit(solution)/shard_map/pallas_call | solution.py:703
  25.8 0.8 shard_map.96
  26.7 6.1 %shard_map.97 = (bf16[16384,256]{1,0:T(8,128)(2,1)S(1)}, f32[192,256]{1,0:T(8,128)}, f32[2,256]{1,0:T(2,128)}, f32[2,256]{1,0:T(2,128)S(1)}, f32[96,256]{1,0:T(8...) custom-call(f32[192,256]{1,0:T(8,128)S(1)} %get-tuple-element.92.loads_ref, ...), custom_call_target="tpu_custom_call" | custom-call | tf_op jit(solution)/shard_map/pallas_call | solution.py:717
  32.9 4.9 %collective-permute-start.3 = (f32[48,128]{1,0:T(8,128)S(1)}, f32[48,128]{1,0:T(8,128)S(1)}, u32[]{:S(2)}, u32[]{:S(2)}) collective-permute-start(f32[48,128]{1,0:T(8,128)S(1)} %get-tuple-element.107.message_in), channel_id=1, source_target_pairs={{1,2},{2,1},{3,4},{4,3},{5,6},{6,5},{7,8},{8,7},{9,10},{10,9},{11,... | collective-permute-start | bytes 73736 | tf_op jit(solution)/shard_map/ppermute | solution.py:648
  37.8 4.1 %shard_map.98 = (f32[96,256]{1,0:T(8,128)S(1)}, f32[96,256]{1,0:T(8,128)S(1)}, f32[96,256]{1,0:T(8,128)S(1)}, f32[192,256]{1,0:T(8,128)S(1)}, bf16[16384,128]{1,0:T(8,128)(2,1)S(1)}) custom-call(f32[96,256]{1,0:T(8,128)S(1)} %get-tuple-element.109.partial_ref.residual_ref, f32[96,256]{1,0:T(8,128)S(1)} %get-tuple-element.110.diagonal_ref, ...), custom_call_target="tpu_custom_call" | custom-call | tf_op jit(solution)/shard_map/pallas_call | solution.py:739
  41.9 0.3 collective-permute-done.3.other_in
  42.2 2.0 %shard_map.99 = (f32[24,128]{1,0:T(8,128)S(1)}, f32[24,128]{1,0:T(8,128)S(1)}, f32[24,128]{1,0:T(8,128)S(1)}, f32[24,128]{1,0:T(8,128)S(1)}, f32[192,256]{1,0:T(8,128)S(1)}, /*index=5*/f32[24,128]{1,0:T(8,128)S(1)}) custom-call(f32[48,128]{1,0:T(8,128)S(1)} %get-tuple-element.107.message_in, f32[48,128]{1,0:T(8,128)S(1)} %collective-permute-done.2.near_in, ...), custom_call_target="tpu_custom_call" | custom-call | tf_op jit(solution)/shard_map/pallas_call | solution.py:744
  44.3 5.1 %collective-permute-start.5 = (f32[24,128]{1,0:T(8,128)S(1)}, f32[24,128]{1,0:T(8,128)S(1)}, u32[]{:S(2)}, u32[]{:S(2)}) collective-permute-start(f32[24,128]{1,0:T(8,128)S(1)} %get-tuple-element.116.message_in), channel_id=1, source_target_pairs={{1,2},{2,1},{3,4},{4,3},{5,6},{6,5},{7,8},{8,7},{9,10},{10,9},{11,... | collective-permute-start | bytes 36872 | tf_op jit(solution)/shard_map/ppermute | solution.py:648
  49.4 4.2 %shard_map.100 = (f32[96,256]{1,0:T(8,128)S(1)}, f32[96,256]{1,0:T(8,128)S(1)}, f32[96,256]{1,0:T(8,128)S(1)}, f32[192,256]{1,0:T(8,128)S(1)}) custom-call(f32[192,256]{1,0:T(8,128)S(1)} %get-tuple-element.121.values_ref, f32[96,256]{1,0:T(8,128)S(1)} %get-tuple-element.109.partial_ref.residual_ref, f32[96,256]{1,0:T(8,128)S(1)} %get-tuple-element.122.inverse_ref, ...), custom_call_target="tpu_custom_call" | custom-call | tf_op jit(solution)/shard_map/pallas_call | solution.py:751
  53.7 2.0 %shard_map.101 = (f32[24,128]{1,0:T(8,128)S(1)}, f32[24,128]{1,0:T(8,128)S(1)}, f32[24,128]{1,0:T(8,128)S(1)}, f32[192,256]{1,0:T(8,128)S(1)}, f32[24,128]{1,0:T(8,128)S(1)}) custom-call(f32[24,128]{1,0:T(8,128)S(1)} %get-tuple-element.116.message_in, f32[24,128]{1,0:T(8,128)S(1)} %collective-permute-done.4.near_in, ...), custom_call_target="tpu_custom_call" | custom-call | tf_op jit(solution)/shard_map/pallas_call | solution.py:756
  55.8 4.8 %collective-permute-start.7 = (f32[24,128]{1,0:T(8,128)S(1)}, f32[24,128]{1,0:T(8,128)S(1)}, u32[]{:S(2)}, u32[]{:S(2)}) collective-permute-start(f32[24,128]{1,0:T(8,128)S(1)} %get-tuple-element.126.message_in), channel_id=1, source_target_pairs={{1,2},{2,1},{3,4},{4,3},{5,6},{6,5},{7,8},{8,7},{9,10},{10,9},{11,... | collective-permute-start | bytes 36872 | tf_op jit(solution)/shard_map/ppermute | solution.py:648
  60.6 4.2 %shard_map.102 = (f32[96,256]{1,0:T(8,128)S(1)}, f32[96,256]{1,0:T(8,128)S(1)}, f32[96,256]{1,0:T(8,128)S(1)}, f32[192,256]{1,0:T(8,128)S(1)}) custom-call(f32[192,256]{1,0:T(8,128)S(1)} %get-tuple-element.130.values_ref, f32[96,256]{1,0:T(8,128)S(1)} %get-tuple-element.131.residual_ref, f32[96,256]{1,0:T(8,128)S(1)} %get-tuple-element.122.inverse_ref, ...), custom_call_target="tpu_custom_call" | custom-call | tf_op jit(solution)/shard_map/pallas_call | solution.py:751
  65.0 2.0 %shard_map.103 = (f32[24,128]{1,0:T(8,128)S(1)}, f32[24,128]{1,0:T(8,128)S(1)}, f32[24,128]{1,0:T(8,128)S(1)}, f32[192,256]{1,0:T(8,128)S(1)}, f32[24,128]{1,0:T(8,128)S(1)}) custom-call(f32[24,128]{1,0:T(8,128)S(1)} %get-tuple-element.126.message_in, f32[24,128]{1,0:T(8,128)S(1)} %collective-permute-done.6.near_in, ...), custom_call_target="tpu_custom_call" | custom-call | tf_op jit(solution)/shard_map/pallas_call | solution.py:756
  67.1 4.8 %collective-permute-start.9 = (f32[24,128]{1,0:T(8,128)S(1)}, f32[24,128]{1,0:T(8,128)S(1)}, u32[]{:S(2)}, u32[]{:S(2)}) collective-permute-start(f32[24,128]{1,0:T(8,128)S(1)} %get-tuple-element.135.message_in), channel_id=1, source_target_pairs={{1,2},{2,1},{3,4},{4,3},{5,6},{6,5},{7,8},{8,7},{9,10},{10,9},{11,... | collective-permute-start | bytes 36872 | tf_op jit(solution)/shard_map/ppermute | solution.py:648
  71.9 4.2 %shard_map.104 = (f32[96,256]{1,0:T(8,128)S(1)}, f32[96,256]{1,0:T(8,128)S(1)}, f32[96,256]{1,0:T(8,128)S(1)}, f32[192,256]{1,0:T(8,128)S(1)}) custom-call(f32[192,256]{1,0:T(8,128)S(1)} %get-tuple-element.139.values_ref, f32[96,256]{1,0:T(8,128)S(1)} %get-tuple-element.140.residual_ref, f32[96,256]{1,0:T(8,128)S(1)} %get-tuple-element.122.inverse_ref, ...), custom_call_target="tpu_custom_call" | custom-call | tf_op jit(solution)/shard_map/pallas_call | solution.py:751
  76.3 2.0 %shard_map.105 = (f32[24,128]{1,0:T(8,128)S(1)}, f32[24,128]{1,0:T(8,128)S(1)}, f32[24,128]{1,0:T(8,128)S(1)}, f32[192,256]{1,0:T(8,128)S(1)}, f32[24,128]{1,0:T(8,128)S(1)}) custom-call(f32[24,128]{1,0:T(8,128)S(1)} %get-tuple-element.135.message_in, f32[24,128]{1,0:T(8,128)S(1)} %collective-permute-done.8.near_in, ...), custom_call_target="tpu_custom_call" | custom-call | tf_op jit(solution)/shard_map/pallas_call | solution.py:756
  78.4 4.8 %collective-permute-start.11 = (f32[24,128]{1,0:T(8,128)S(1)}, f32[24,128]{1,0:T(8,128)S(1)}, u32[]{:S(2)}, u32[]{:S(2)}) collective-permute-start(f32[24,128]{1,0:T(8,128)S(1)} %get-tuple-element.144.message_in), channel_id=1, source_target_pairs={{1,2},{2,1},{3,4},{4,3},{5,6},{6,5},{7,8},{8,7},{9,10},{10,9},{11,... | collective-permute-start | bytes 36872 | tf_op jit(solution)/shard_map/ppermute | solution.py:648
  83.2 4.2 %shard_map.106 = (f32[96,256]{1,0:T(8,128)S(1)}, f32[96,256]{1,0:T(8,128)S(1)}, f32[96,256]{1,0:T(8,128)S(1)}, f32[192,256]{1,0:T(8,128)S(1)}) custom-call(f32[192,256]{1,0:T(8,128)S(1)} %get-tuple-element.148.values_ref, f32[96,256]{1,0:T(8,128)S(1)} %get-tuple-element.149.residual_ref, f32[96,256]{1,0:T(8,128)S(1)} %get-tuple-element.122.inverse_ref, ...), custom_call_target="tpu_custom_call" | custom-call | tf_op jit(solution)/shard_map/pallas_call | solution.py:751
  87.6 2.0 %shard_map.107 = (f32[24,128]{1,0:T(8,128)S(1)}, f32[24,128]{1,0:T(8,128)S(1)}, f32[24,128]{1,0:T(8,128)S(1)}, f32[192,256]{1,0:T(8,128)S(1)}, f32[24,128]{1,0:T(8,128)S(1)}) custom-call(f32[24,128]{1,0:T(8,128)S(1)} %get-tuple-element.144.message_in, f32[24,128]{1,0:T(8,128)S(1)} %collective-permute-done.10.near_in, ...), custom_call_target="tpu_custom_call" | custom-call | tf_op jit(solution)/shard_map/pallas_call | solution.py:756
  89.7 5.1 %collective-permute-start.13 = (f32[24,128]{1,0:T(8,128)S(1)}, f32[24,128]{1,0:T(8,128)S(1)}, u32[]{:S(2)}, u32[]{:S(2)}) collective-permute-start(f32[24,128]{1,0:T(8,128)S(1)} %get-tuple-element.153.message_in), channel_id=1, source_target_pairs={{1,2},{2,1},{3,4},{4,3},{5,6},{6,5},{7,8},{8,7},{9,10},{10,9},{11,... | collective-permute-start | bytes 36872 | tf_op jit(solution)/shard_map/ppermute | solution.py:648
  94.7 4.2 %shard_map.108 = (f32[96,256]{1,0:T(8,128)S(1)}, f32[96,256]{1,0:T(8,128)S(1)}, f32[96,256]{1,0:T(8,128)S(1)}, f32[192,256]{1,0:T(8,128)S(1)}) custom-call(f32[192,256]{1,0:T(8,128)S(1)} %get-tuple-element.157.values_ref, f32[96,256]{1,0:T(8,128)S(1)} %get-tuple-element.158.residual_ref, f32[96,256]{1,0:T(8,128)S(1)} %get-tuple-element.122.inverse_ref, ...), custom_call_target="tpu_custom_call" | custom-call | tf_op jit(solution)/shard_map/pallas_call | solution.py:751
  99.0 2.0 %shard_map.109 = (f32[24,128]{1,0:T(8,128)S(1)}, f32[24,128]{1,0:T(8,128)S(1)}, f32[24,128]{1,0:T(8,128)S(1)}, f32[192,256]{1,0:T(8,128)S(1)}, f32[24,128]{1,0:T(8,128)S(1)}) custom-call(f32[24,128]{1,0:T(8,128)S(1)} %get-tuple-element.153.message_in, f32[24,128]{1,0:T(8,128)S(1)} %collective-permute-done.12.near_in, ...), custom_call_target="tpu_custom_call" | custom-call | tf_op jit(solution)/shard_map/pallas_call | solution.py:756
  101.1 4.9 %collective-permute-start.15 = (f32[24,128]{1,0:T(8,128)S(1)}, f32[24,128]{1,0:T(8,128)S(1)}, u32[]{:S(2)}, u32[]{:S(2)}) collective-permute-start(f32[24,128]{1,0:T(8,128)S(1)} %get-tuple-element.162.message_in), channel_id=1, source_target_pairs={{1,2},{2,1},{3,4},{4,3},{5,6},{6,5},{7,8},{8,7},{9,10},{10,9},{11,... | collective-permute-start | bytes 36872 | tf_op jit(solution)/shard_map/ppermute | solution.py:648
  106.0 4.2 %shard_map.110 = (f32[96,256]{1,0:T(8,128)S(1)}, f32[96,256]{1,0:T(8,128)S(1)}, f32[96,256]{1,0:T(8,128)S(1)}, f32[192,256]{1,0:T(8,128)S(1)}) custom-call(f32[192,256]{1,0:T(8,128)S(1)} %get-tuple-element.166.values_ref, f32[96,256]{1,0:T(8,128)S(1)} %get-tuple-element.167.residual_ref, f32[96,256]{1,0:T(8,128)S(1)} %get-tuple-element.122.inverse_ref, ...), custom_call_target="tpu_custom_call" | custom-call | tf_op jit(solution)/shard_map/pallas_call | solution.py:751
  110.3 2.0 %shard_map.111 = (f32[24,128]{1,0:T(8,128)S(1)}, f32[24,128]{1,0:T(8,128)S(1)}, f32[24,128]{1,0:T(8,128)S(1)}, f32[192,256]{1,0:T(8,128)S(1)}, f32[24,128]{1,0:T(8,128)S(1)}) custom-call(f32[24,128]{1,0:T(8,128)S(1)} %get-tuple-element.162.message_in, f32[24,128]{1,0:T(8,128)S(1)} %collective-permute-done.14.near_in, ...), custom_call_target="tpu_custom_call" | custom-call | tf_op jit(solution)/shard_map/pallas_call | solution.py:756
  112.4 4.9 %collective-permute-start.17 = (f32[24,128]{1,0:T(8,128)S(1)}, f32[24,128]{1,0:T(8,128)S(1)}, u32[]{:S(2)}, u32[]{:S(2)}) collective-permute-start(f32[24,128]{1,0:T(8,128)S(1)} %get-tuple-element.171.message_in), channel_id=1, source_target_pairs={{1,2},{2,1},{3,4},{4,3},{5,6},{6,5},{7,8},{8,7},{9,10},{10,9},{11,... | collective-permute-start | bytes 36872 | tf_op jit(solution)/shard_map/ppermute | solution.py:648
  117.3 2.1 %shard_map.112.field_ref = f32[96,256]{1,0:T(8,128)S(1)} custom-call(f32[192,256]{1,0:T(8,128)S(1)} %get-tuple-element.175.values_ref, f32[96,256]{1,0:T(8,128)S(1)} %get-tuple-element.176.residual_ref, f32[96,256]{1,0:T(8,128)S(1)} %get-tuple-element.122.inverse_ref, f32[96,256]{1,0:T(8,128)S(1)} %get-tuple-element.177.update_ref, ...), custom_call_target="tpu_custom_call" | custom-call | tf_op jit(solution)/shard_map/pallas_call | solution.py:765
  119.4 2.2 %collective-permute-done.17.other_in = f32[24,128]{1,0:T(8,128)S(1)} collective-permute-done((f32[24,128]{1,0:T(8,128)S(1)}, f32[24,128]{1,0:T(8,128)S(1)}, u32[]{:S(2)}, u32[]{:S(2)}) %collective-permute-start.17) | collective-permute-done | bytes 12320 | tf_op jit(solution)/shard_map/ppermute | solution.py:648
  121.6 1.0 shard_map.113
  (26 shorter events, 1.4 us)
Async XLA Ops:
  2.7 24.0 %all-to-all-start = ((f32[128,1,256]{2,1,0:T(1,128)}), f32[128,1,256]{2,1,0:T(1,128)S(1)}, u32[]{:S(2)}, u32[]{:S(2)}) async-start(f32[128,1,256]{2,1,0:T(1,128)} %get-tuple-element.95), calls=%async_computation | async-start | bytes 262144 | tf_op jit(solution)/shard_map/all_to_all | solution.py:702
  13.2 12.6 %collective-permute-start = (f32[40,256]{1,0:T(8,128)S(1)}, f32[40,256]{1,0:T(8,128)S(1)}, u32[]{:S(2)}, u32[]{:S(2)}) collective-permute-start(f32[40,256]{1,0:T(8,128)S(1)} %get-tuple-element.96.field_message), channel_id=1, source_target_pairs={{0,1},{1,0},{2,3},{3,2},{4,5},{5,4},{6,7},{7,6},{8,9},{9,8},{10,11... | collective-permute-start | bytes 122888 | tf_op jit(solution)/shard_map/ppermute | solution.py:649
  13.4 12.5 %collective-permute-start.1 = (f32[40,256]{1,0:T(8,128)S(1)}, f32[40,256]{1,0:T(8,128)S(1)}, u32[]{:S(2)}, u32[]{:S(2)}) collective-permute-start(f32[40,256]{1,0:T(8,128)S(1)} %get-tuple-element.97), channel_id=1, source_target_pairs={{1,2},{2,1},{3,4},{4,3},{5,6},{6,5},{7,8},{8,7},{9,10},{10,9},{11,... | collective-permute-start | bytes 122888 | tf_op jit(solution)/shard_map/ppermute | solution.py:648
  32.8 9.1 %collective-permute-start.2 = (f32[48,128]{1,0:T(8,128)S(1)}, f32[48,128]{1,0:T(8,128)S(1)}, u32[]{:S(2)}, u32[]{:S(2)}) collective-permute-start(f32[48,128]{1,0:T(8,128)S(1)} %get-tuple-element.107.message_in), channel_id=1, source_target_pairs={{0,1},{1,0},{2,3},{3,2},{4,5},{5,4},{6,7},{7,6},{8,9},{9,8},{10,11... | collective-permute-start | bytes 73736 | tf_op jit(solution)/shard_map/ppermute | solution.py:649
  32.9 9.4 %collective-permute-start.3 = (f32[48,128]{1,0:T(8,128)S(1)}, f32[48,128]{1,0:T(8,128)S(1)}, u32[]{:S(2)}, u32[]{:S(2)}) collective-permute-start(f32[48,128]{1,0:T(8,128)S(1)} %get-tuple-element.107.message_in), channel_id=1, source_target_pairs={{1,2},{2,1},{3,4},{4,3},{5,6},{6,5},{7,8},{8,7},{9,10},{10,9},{11,... | collective-permute-start | bytes 73736 | tf_op jit(solution)/shard_map/ppermute | solution.py:648
  44.2 9.4 %collective-permute-start.4 = (f32[24,128]{1,0:T(8,128)S(1)}, f32[24,128]{1,0:T(8,128)S(1)}, u32[]{:S(2)}, u32[]{:S(2)}) collective-permute-start(f32[24,128]{1,0:T(8,128)S(1)} %get-tuple-element.116.message_in), channel_id=1, source_target_pairs={{0,1},{1,0},{2,3},{3,2},{4,5},{5,4},{6,7},{7,6},{8,9},{9,8},{10,11... | collective-permute-start | bytes 36872 | tf_op jit(solution)/shard_map/ppermute | solution.py:649
  44.3 9.4 %collective-permute-start.5 = (f32[24,128]{1,0:T(8,128)S(1)}, f32[24,128]{1,0:T(8,128)S(1)}, u32[]{:S(2)}, u32[]{:S(2)}) collective-permute-start(f32[24,128]{1,0:T(8,128)S(1)} %get-tuple-element.116.message_in), channel_id=1, source_target_pairs={{1,2},{2,1},{3,4},{4,3},{5,6},{6,5},{7,8},{8,7},{9,10},{10,9},{11,... | collective-permute-start | bytes 36872 | tf_op jit(solution)/shard_map/ppermute | solution.py:648
  55.7 9.2 %collective-permute-start.6 = (f32[24,128]{1,0:T(8,128)S(1)}, f32[24,128]{1,0:T(8,128)S(1)}, u32[]{:S(2)}, u32[]{:S(2)}) collective-permute-start(f32[24,128]{1,0:T(8,128)S(1)} %get-tuple-element.126.message_in), channel_id=1, source_target_pairs={{0,1},{1,0},{2,3},{3,2},{4,5},{5,4},{6,7},{7,6},{8,9},{9,8},{10,11... | collective-permute-start | bytes 36872 | tf_op jit(solution)/shard_map/ppermute | solution.py:649
  55.8 9.2 %collective-permute-start.7 = (f32[24,128]{1,0:T(8,128)S(1)}, f32[24,128]{1,0:T(8,128)S(1)}, u32[]{:S(2)}, u32[]{:S(2)}) collective-permute-start(f32[24,128]{1,0:T(8,128)S(1)} %get-tuple-element.126.message_in), channel_id=1, source_target_pairs={{1,2},{2,1},{3,4},{4,3},{5,6},{6,5},{7,8},{8,7},{9,10},{10,9},{11,... | collective-permute-start | bytes 36872 | tf_op jit(solution)/shard_map/ppermute | solution.py:648
  67.0 9.2 %collective-permute-start.8 = (f32[24,128]{1,0:T(8,128)S(1)}, f32[24,128]{1,0:T(8,128)S(1)}, u32[]{:S(2)}, u32[]{:S(2)}) collective-permute-start(f32[24,128]{1,0:T(8,128)S(1)} %get-tuple-element.135.message_in), channel_id=1, source_target_pairs={{0,1},{1,0},{2,3},{3,2},{4,5},{5,4},{6,7},{7,6},{8,9},{9,8},{10,11... | collective-permute-start | bytes 36872 | tf_op jit(solution)/shard_map/ppermute | solution.py:649
  67.1 9.2 %collective-permute-start.9 = (f32[24,128]{1,0:T(8,128)S(1)}, f32[24,128]{1,0:T(8,128)S(1)}, u32[]{:S(2)}, u32[]{:S(2)}) collective-permute-start(f32[24,128]{1,0:T(8,128)S(1)} %get-tuple-element.135.message_in), channel_id=1, source_target_pairs={{1,2},{2,1},{3,4},{4,3},{5,6},{6,5},{7,8},{8,7},{9,10},{10,9},{11,... | collective-permute-start | bytes 36872 | tf_op jit(solution)/shard_map/ppermute | solution.py:648
  78.3 9.2 %collective-permute-start.10 = (f32[24,128]{1,0:T(8,128)S(1)}, f32[24,128]{1,0:T(8,128)S(1)}, u32[]{:S(2)}, u32[]{:S(2)}) collective-permute-start(f32[24,128]{1,0:T(8,128)S(1)} %get-tuple-element.144.message_in), channel_id=1, source_target_pairs={{0,1},{1,0},{2,3},{3,2},{4,5},{5,4},{6,7},{7,6},{8,9},{9,8},{10,11... | collective-permute-start | bytes 36872 | tf_op jit(solution)/shard_map/ppermute | solution.py:649
  78.4 9.2 %collective-permute-start.11 = (f32[24,128]{1,0:T(8,128)S(1)}, f32[24,128]{1,0:T(8,128)S(1)}, u32[]{:S(2)}, u32[]{:S(2)}) collective-permute-start(f32[24,128]{1,0:T(8,128)S(1)} %get-tuple-element.144.message_in), channel_id=1, source_target_pairs={{1,2},{2,1},{3,4},{4,3},{5,6},{6,5},{7,8},{8,7},{9,10},{10,9},{11,... | collective-permute-start | bytes 36872 | tf_op jit(solution)/shard_map/ppermute | solution.py:648
  89.6 9.4 %collective-permute-start.12 = (f32[24,128]{1,0:T(8,128)S(1)}, f32[24,128]{1,0:T(8,128)S(1)}, u32[]{:S(2)}, u32[]{:S(2)}) collective-permute-start(f32[24,128]{1,0:T(8,128)S(1)} %get-tuple-element.153.message_in), channel_id=1, source_target_pairs={{0,1},{1,0},{2,3},{3,2},{4,5},{5,4},{6,7},{7,6},{8,9},{9,8},{10,11... | collective-permute-start | bytes 36872 | tf_op jit(solution)/shard_map/ppermute | solution.py:649
  89.7 9.3 %collective-permute-start.13 = (f32[24,128]{1,0:T(8,128)S(1)}, f32[24,128]{1,0:T(8,128)S(1)}, u32[]{:S(2)}, u32[]{:S(2)}) collective-permute-start(f32[24,128]{1,0:T(8,128)S(1)} %get-tuple-element.153.message_in), channel_id=1, source_target_pairs={{1,2},{2,1},{3,4},{4,3},{5,6},{6,5},{7,8},{8,7},{9,10},{10,9},{11,... | collective-permute-start | bytes 36872 | tf_op jit(solution)/shard_map/ppermute | solution.py:648
  101.0 9.3 %collective-permute-start.14 = (f32[24,128]{1,0:T(8,128)S(1)}, f32[24,128]{1,0:T(8,128)S(1)}, u32[]{:S(2)}, u32[]{:S(2)}) collective-permute-start(f32[24,128]{1,0:T(8,128)S(1)} %get-tuple-element.162.message_in), channel_id=1, source_target_pairs={{0,1},{1,0},{2,3},{3,2},{4,5},{5,4},{6,7},{7,6},{8,9},{9,8},{10,11... | collective-permute-start | bytes 36872 | tf_op jit(solution)/shard_map/ppermute | solution.py:649
  101.1 9.2 %collective-permute-start.15 = (f32[24,128]{1,0:T(8,128)S(1)}, f32[24,128]{1,0:T(8,128)S(1)}, u32[]{:S(2)}, u32[]{:S(2)}) collective-permute-start(f32[24,128]{1,0:T(8,128)S(1)} %get-tuple-element.162.message_in), channel_id=1, source_target_pairs={{1,2},{2,1},{3,4},{4,3},{5,6},{6,5},{7,8},{8,7},{9,10},{10,9},{11,... | collective-permute-start | bytes 36872 | tf_op jit(solution)/shard_map/ppermute | solution.py:648
  112.3 7.1 %collective-permute-start.16 = (f32[24,128]{1,0:T(8,128)S(1)}, f32[24,128]{1,0:T(8,128)S(1)}, u32[]{:S(2)}, u32[]{:S(2)}) collective-permute-start(f32[24,128]{1,0:T(8,128)S(1)} %get-tuple-element.171.message_in), channel_id=1, source_target_pairs={{0,1},{1,0},{2,3},{3,2},{4,5},{5,4},{6,7},{7,6},{8,9},{9,8},{10,11... | collective-permute-start | bytes 36872 | tf_op jit(solution)/shard_map/ppermute | solution.py:649
  112.4 9.2 %collective-permute-start.17 = (f32[24,128]{1,0:T(8,128)S(1)}, f32[24,128]{1,0:T(8,128)S(1)}, u32[]{:S(2)}, u32[]{:S(2)}) collective-permute-start(f32[24,128]{1,0:T(8,128)S(1)} %get-tuple-element.171.message_in), channel_id=1, source_target_pairs={{1,2},{2,1},{3,4},{4,3},{5,6},{6,5},{7,8},{8,7},{9,10},{10,9},{11,... | collective-permute-start | bytes 36872 | tf_op jit(solution)/shard_map/ppermute | solution.py:648
